TPU v7x, 32 devices: a whole 2x2x4 slice. The times are simulated.
32 devices in a mesh: fsdp: 8 (over z, x), tp: 4 (over y, core).
Axes of the slice: x: 2, y: 2, z: 4, core: 2. Of those that a mesh axis runs over, the one named last changes fastest.
Arguments:
- inputs: float32 [16384, 768], P(('fsdp', 'tp')), may hold values from -6 to 6
- cotangent: float32 [16384, 768], P(('fsdp', 'tp')), may hold values from -6 to 6
- lengths: int32 [8, 4], P('fsdp'), may hold values from 1 to 768, as said below
- routes: int32 [16384, 2], P('fsdp'), may hold values from 0 to 11, all different within a row
- drop_order: int32 [16384, 2], P('fsdp'), may hold values from 0 to 4095, as said below
- prior_logits: float32 [16384, 12], P('fsdp'), may hold values from -6 to 6
- attn_gain: float32 [768], replicated, may hold values from 0.5 to 1.5
- w_query: bfloat16 [768, 768], P('fsdp', 'tp'), may hold values from -0.21875 to 0.21875
- w_key: bfloat16 [768, 768], P('fsdp', 'tp'), may hold values from -0.21875 to 0.21875
- w_value: bfloat16 [768, 768], P('fsdp', 'tp'), may hold values from -0.21875 to 0.21875
- w_out: bfloat16 [768, 768], P('tp', 'fsdp'), may hold values from -3.5 to 3.5
- moe_gain: float32 [768], replicated, may hold values from 0.5 to 1.5
- w_router: float32 [768, 12], replicated, may hold values from -0.21875 to 0.21875
- w_prior: float32 [12, 12], replicated, may hold values from -1.75 to 1.75
- w_const: float32 [2, 768, 2], replicated, may hold values from -0.21875 to 0.21875
- const_vector: float32 [2, 768], replicated, may hold values from -6 to 6
- w_gate: bfloat16 [8, 768, 2048], P(None, 'fsdp', 'tp'), may hold values from -0.21875 to 0.21875
- w_up: bfloat16 [8, 768, 2048], P(None, 'fsdp', 'tp'), may hold values from -0.21875 to 0.21875
- w_down: bfloat16 [8, 2048, 768], P(None, 'tp', 'fsdp'), may hold values from -2 to 2
Outputs:
- output: float32 [16384, 768], P(('fsdp', 'tp'))
- grad_inputs: float32 [16384, 768], P(('fsdp', 'tp'))
- grad_prior: float32 [16384, 12], P(('fsdp', 'tp'))
- grad_attn_gain: float32 [768], replicated
- grad_w_query: float32 [768, 768], P('fsdp', 'tp')
- grad_w_key: float32 [768, 768], P('fsdp', 'tp')
- grad_w_value: float32 [768, 768], P('fsdp', 'tp')
- grad_w_out: float32 [768, 768], P('tp', 'fsdp')
- grad_moe_gain: float32 [768], replicated
- grad_w_router: float32 [768, 12], replicated
- grad_w_prior: float32 [12, 12], replicated
- grad_w_const: float32 [2, 768, 2], replicated
- grad_const_vector: float32 [2, 768], replicated
- grad_w_gate: float32 [8, 768, 2048], P(None, 'fsdp', 'tp')
- grad_w_up: float32 [8, 768, 2048], P(None, 'fsdp', 'tp')
- grad_w_down: float32 [8, 2048, 768], P(None, 'tp', 'fsdp')
Inputs may be any that keep to these rules, and one draw needn't show every extreme that they name: In each row the first 3 entries are the group's sequence lengths in order and the last counts padding tokens at the group's end; each row sums to 2048. Every sequence has 512 tokens or more, one sequence of each row has exactly 768, and the padding is 1 or more. `routes`: each token names two different experts: 0 to 7 feed-forward, 8 zero, 9 copy, 10 and 11 constant. `drop_order`: within each group the 4096 pairs carry each rank once.
All inputs are finite; a program needn't handle non-finite values.
Results may differ from a plain program's by a relative error of at most 0.015.
Values may be sent and summed in bfloat16 or wider, within the bound.
No kernel may reach another device: no remote copies, remote signals or barrier semaphores. Data moves between devices by JAX's collectives and lax.ppermute only.
A program may use at most 256 MiB of HBM per device.

v0:
```python
import jax
import jax.numpy as jnp
from jax import lax
from jax.sharding import PartitionSpec as P

HEAD = 64


EPSILON = 1e-06
PRECISE = lax.Precision.HIGHEST


def rms_norm(values, gain):
    return values * lax.rsqrt(jnp.mean(values * values, axis=-1, keepdims=True) + EPSILON) * gain


def segments_of(lengths_row, group):
    boundary = jnp.cumsum(lengths_row)
    places = jnp.arange(group, dtype=jnp.int32)
    return jnp.sum((places[:, None] >= boundary[None, :]).astype(jnp.int32), axis=1)


def routing(routes, drop_order, valid, capacity, experts):
    group = routes.shape[0]
    live = (routes < experts) & valid[:, None]
    target = jnp.where(live, routes, experts)
    flat_order = drop_order.reshape(-1)
    by_rank = jnp.zeros((2 * group,), jnp.int32).at[flat_order].set(target.reshape(-1))
    onehot = (by_rank[:, None] == jnp.arange(experts, dtype=jnp.int32)[None, :]).astype(jnp.int32)
    before = jnp.sum((jnp.cumsum(onehot, axis=0) - onehot) * onehot, axis=1)
    placed = before[flat_order].reshape(group, 2)
    kept = live & (placed < capacity)
    slot_ids = jnp.where(kept, routes * capacity + placed, experts * capacity)
    token_ids = jnp.broadcast_to(jnp.arange(group, dtype=jnp.int32)[:, None], (group, 2))
    slot_token = (
        jnp.zeros((experts * capacity + 1,), jnp.int32)
        .at[slot_ids.reshape(-1)]
        .set(token_ids.reshape(-1))[:-1]
    )
    used = jnp.zeros((experts * capacity + 1,), jnp.int32).at[slot_ids.reshape(-1)].set(1)[:-1]
    return (kept, slot_ids, slot_token, used)


def block_mask(segment, first_row, block):
    segment_rows = lax.dynamic_slice_in_dim(segment, first_row, block)
    places = first_row + jnp.arange(block, dtype=jnp.int32)
    columns = jnp.arange(segment.shape[0], dtype=jnp.int32)
    return (segment_rows[:, None] == segment[None, :]) & (columns[None, :] <= places[:, None])


def router_weights(rounded, prior_rows, w_router, w_prior, route_rows):
    logits = jnp.dot(rounded, w_router, precision=PRECISE) + jnp.dot(
        prior_rows, w_prior, precision=PRECISE
    )
    router = jax.nn.softmax(logits, axis=-1)
    picked = (
        route_rows[:, :, None] == jnp.arange(w_router.shape[1], dtype=jnp.int32)[None, None, :]
    ).astype(jnp.float32)
    return jnp.sum(router[:, None, :] * picked, axis=-1)


def other_terms(normed, chosen, w_const, const_vector, route_rows, experts):
    mix_one = jax.nn.softmax(jnp.dot(normed, w_const[0], precision=PRECISE), axis=-1)
    mix_two = jax.nn.softmax(jnp.dot(normed, w_const[1], precision=PRECISE), axis=-1)
    constant_one = mix_one[:, :1] * normed + mix_one[:, 1:] * const_vector[0]
    constant_two = mix_two[:, :1] * normed + mix_two[:, 1:] * const_vector[1]
    weight_copy = jnp.sum(
        chosen * (route_rows == experts + 1).astype(jnp.float32), axis=1, keepdims=True
    )
    weight_first = jnp.sum(
        chosen * (route_rows == experts + 2).astype(jnp.float32), axis=1, keepdims=True
    )
    weight_second = jnp.sum(
        chosen * (route_rows == experts + 3).astype(jnp.float32), axis=1, keepdims=True
    )
    return weight_copy * normed + weight_first * constant_one + weight_second * constant_two


def per_device(
    inputs,
    cotangent,
    lengths,
    routes,
    drop_order,
    prior_logits,
    attn_gain,
    w_query,
    w_key,
    w_value,
    w_out,
    moe_gain,
    w_router,
    w_prior,
    w_const,
    const_vector,
    w_gate,
    w_up,
    w_down,
):
    tok_rows, width = inputs.shape
    group = tok_rows * lax.axis_size("tp")
    first_mine = lax.axis_index("tp") * tok_rows
    experts = w_gate.shape[0]
    capacity = 3 * group // 16
    slot_count = experts * capacity
    local_width = w_query.shape[1]
    local_heads = local_width // HEAD
    block = min(1024, group)
    block_count = group // block
    segment = segments_of(lengths[0], group)
    valid = segment < lengths.shape[1] - 1
    valid_mine = lax.dynamic_slice_in_dim(valid, first_mine, tok_rows).astype(jnp.float32)[:, None]
    routes_mine = lax.dynamic_slice_in_dim(routes, first_mine, tok_rows)
    prior_mine = lax.dynamic_slice_in_dim(prior_logits, first_mine, tok_rows)
    normed_one = rms_norm(inputs, attn_gain)
    gathered_one = lax.all_gather(normed_one.astype(jnp.bfloat16), "tp", axis=0, tiled=True)
    query_full, key_full, value_full, out_full = (
        lax.all_gather(w_query, "fsdp", axis=0, tiled=True),
        lax.all_gather(w_key, "fsdp", axis=0, tiled=True),
        lax.all_gather(w_value, "fsdp", axis=0, tiled=True),
        lax.all_gather(w_out, "fsdp", axis=1, tiled=True),
    )

    def project_heads(weight):
        return (
            jnp.dot(gathered_one, weight, preferred_element_type=jnp.float32)
            .astype(jnp.bfloat16)
            .reshape(group, local_heads, HEAD)
        )

    queries = project_heads(query_full)
    keys = project_heads(key_full)
    values_all = project_heads(value_full)

    def scores_of(block_id):
        first_row = block_id * block
        query_rows = lax.dynamic_slice_in_dim(queries, first_row, block)
        raw = (
            jnp.einsum("qhd,khd->hqk", query_rows, keys, preferred_element_type=jnp.float32) * 0.125
        )
        return (query_rows, jnp.where(block_mask(segment, first_row, block)[None], raw, -1e30))

    def forward_block(block_id):
        _, scores = scores_of(block_id)
        highest = jnp.max(scores, axis=-1, keepdims=True)
        weights = jnp.exp(scores - highest)
        denominator = jnp.sum(weights, axis=-1, keepdims=True)
        soft = (weights / denominator).astype(jnp.bfloat16)
        mixed_rows = jnp.einsum(
            "hqk,khd->qhd", soft, values_all, preferred_element_type=jnp.float32
        )
        return (mixed_rows.astype(jnp.bfloat16), (highest + jnp.log(denominator))[..., 0])

    mixed_blocks, log_totals = lax.map(forward_block, jnp.arange(block_count, dtype=jnp.int32))
    mixed = mixed_blocks.reshape(group, local_width)
    hidden = inputs + lax.psum_scatter(
        jnp.dot(mixed, out_full, preferred_element_type=jnp.float32),
        "tp",
        scatter_dimension=0,
        tiled=True,
    )
    normed_two = rms_norm(hidden, moe_gain)
    rounded_two = normed_two.astype(jnp.bfloat16)
    gathered_two = lax.all_gather(rounded_two, "tp", axis=0, tiled=True)
    gate_full, up_full, down_full = (
        lax.all_gather(w_gate, "fsdp", axis=1, tiled=True),
        lax.all_gather(w_up, "fsdp", axis=1, tiled=True),
        lax.all_gather(w_down, "fsdp", axis=2, tiled=True),
    )
    chosen_all = router_weights(
        gathered_two.astype(jnp.float32), prior_logits, w_router, w_prior, routes
    )
    kept, slot_ids, slot_token, used = routing(routes, drop_order, valid, capacity, experts)
    dispatched = (
        jnp.take(gathered_two, slot_token, axis=0) * used.astype(jnp.bfloat16)[:, None]
    ).reshape(experts, capacity, width)
    gate_pre = jnp.einsum("ecd,edf->ecf", dispatched, gate_full, preferred_element_type=jnp.float32)
    up_pre = jnp.einsum("ecd,edf->ecf", dispatched, up_full, preferred_element_type=jnp.float32)
    activated = (jax.nn.silu(gate_pre) * up_pre).astype(jnp.bfloat16)
    expert_out = jnp.einsum(
        "ecf,efd->ecd", activated, down_full, preferred_element_type=jnp.float32
    ).reshape(slot_count, width)
    safe_slots = jnp.where(kept, slot_ids, 0)
    kept_float = kept.astype(jnp.float32)
    pair_first = jnp.take(expert_out, safe_slots[:, 0], axis=0)
    pair_second = jnp.take(expert_out, safe_slots[:, 1], axis=0)
    combine_weights = chosen_all * kept_float
    feed_part = pair_first * combine_weights[:, :1] + pair_second * combine_weights[:, 1:]
    feed_mine = lax.psum_scatter(feed_part, "tp", scatter_dimension=0, tiled=True)

    def local_gate(normed, rounded, prior_rows, router, prior_weight, const_weight, const_vec):
        chosen = router_weights(rounded, prior_rows, router, prior_weight, routes_mine)
        return (chosen, other_terms(normed, chosen, const_weight, const_vec, routes_mine, experts))

    (_, other_mine), gate_pull = jax.vjp(
        local_gate,
        normed_two,
        rounded_two.astype(jnp.float32),
        prior_mine,
        w_router,
        w_prior,
        w_const,
        const_vector,
    )
    output = valid_mine * (hidden + feed_mine + other_mine)
    grad_out = cotangent * valid_mine
    grad_out_all = lax.all_gather(grad_out, "tp", axis=0, tiled=True)
    slot_weight = (
        jnp.zeros((slot_count + 1,), jnp.float32)
        .at[slot_ids.reshape(-1)]
        .set(combine_weights.reshape(-1))[:-1]
    )
    grad_expert = (
        (jnp.take(grad_out_all, slot_token, axis=0) * slot_weight[:, None])
        .astype(jnp.bfloat16)
        .reshape(experts, capacity, width)
    )
    pair_grads = (
        jnp.stack(
            [
                jnp.sum(pair_first * grad_out_all, axis=1),
                jnp.sum(pair_second * grad_out_all, axis=1),
            ],
            axis=1,
        )
        * kept_float
    )
    gate_back, up_back, down_back = (
        lax.all_gather(w_gate, "fsdp", axis=1, tiled=True),
        lax.all_gather(w_up, "fsdp", axis=1, tiled=True),
        lax.all_gather(w_down, "fsdp", axis=2, tiled=True),
    )
    grad_act = jnp.einsum(
        "ecd,efd->ecf", grad_expert, down_back, preferred_element_type=jnp.float32
    )
    sigmoid_gate = jax.nn.sigmoid(gate_pre)
    grad_gate = (grad_act * up_pre * sigmoid_gate * (1.0 + gate_pre * (1.0 - sigmoid_gate))).astype(
        jnp.bfloat16
    )
    grad_up = (grad_act * gate_pre * sigmoid_gate).astype(jnp.bfloat16)
    grad_down_w = jnp.einsum(
        "ecf,ecd->efd", activated, grad_expert, preferred_element_type=jnp.float32
    )
    grad_gate_w = jnp.einsum(
        "ecd,ecf->edf", dispatched, grad_gate, preferred_element_type=jnp.float32
    )
    grad_up_w = jnp.einsum("ecd,ecf->edf", dispatched, grad_up, preferred_element_type=jnp.float32)
    grad_slots = jnp.einsum(
        "ecf,edf->ecd", grad_gate, gate_back, preferred_element_type=jnp.float32
    )
    grad_slots = (
        grad_slots
        + jnp.einsum("ecf,edf->ecd", grad_up, up_back, preferred_element_type=jnp.float32)
    ).reshape(slot_count, width)
    grad_tokens = (
        jnp.take(grad_slots, safe_slots[:, 0], axis=0) * kept_float[:, :1]
        + jnp.take(grad_slots, safe_slots[:, 1], axis=0) * kept_float[:, 1:]
    )
    grad_tokens_mine, pair_grads_mine = (
        lax.psum_scatter(grad_tokens, "tp", scatter_dimension=0, tiled=True),
        lax.psum_scatter(pair_grads, "tp", scatter_dimension=0, tiled=True),
    )
    grad_gate_own, grad_up_own, grad_down_own = (
        lax.psum_scatter(grad_gate_w, "fsdp", scatter_dimension=1, tiled=True),
        lax.psum_scatter(grad_up_w, "fsdp", scatter_dimension=1, tiled=True),
        lax.psum_scatter(grad_down_w, "fsdp", scatter_dimension=2, tiled=True),
    )
    grad_normed, grad_rounded, grad_prior, grad_router, grad_prior_w, grad_const, grad_vector = (
        gate_pull((pair_grads_mine, grad_out))
    )
    _, norm_pull_two = jax.vjp(rms_norm, hidden, moe_gain)
    grad_hidden_part, grad_moe_gain = norm_pull_two(grad_normed + grad_rounded + grad_tokens_mine)
    grad_hidden = grad_out + grad_hidden_part
    grad_attn_all = lax.all_gather(grad_hidden.astype(jnp.bfloat16), "tp", axis=0, tiled=True)
    grad_out_w = jnp.einsum("gi,gd->id", mixed, grad_attn_all, preferred_element_type=jnp.float32)
    grad_mixed = (
        jnp.einsum("gd,id->gi", grad_attn_all, out_full, preferred_element_type=jnp.float32)
        .astype(jnp.bfloat16)
        .reshape(group, local_heads, HEAD)
    )

    def backward_block(carry, block_id):
        grad_keys_sum, grad_values_sum = carry
        query_rows, scores = scores_of(block_id)
        grad_rows = lax.dynamic_slice_in_dim(grad_mixed, block_id * block, block)
        soft = jnp.exp(scores - log_totals[block_id][..., None])
        grad_soft = jnp.einsum(
            "qhd,khd->hqk", grad_rows, values_all, preferred_element_type=jnp.float32
        )
        grad_values_sum = grad_values_sum + jnp.einsum(
            "hqk,qhd->khd", soft.astype(jnp.bfloat16), grad_rows, preferred_element_type=jnp.float32
        )
        grad_scores = soft * (grad_soft - jnp.sum(soft * grad_soft, axis=-1, keepdims=True))
        grad_raw = (0.125 * grad_scores).astype(jnp.bfloat16)
        grad_query_rows = jnp.einsum(
            "hqk,khd->qhd", grad_raw, keys, preferred_element_type=jnp.float32
        )
        grad_keys_sum = grad_keys_sum + jnp.einsum(
            "hqk,qhd->khd", grad_raw, query_rows, preferred_element_type=jnp.float32
        )
        return ((grad_keys_sum, grad_values_sum), grad_query_rows.astype(jnp.bfloat16))

    zero_heads = jnp.zeros((group, local_heads, HEAD), jnp.float32)
    (grad_keys_sum, grad_values_sum), grad_query_blocks = lax.scan(
        backward_block, (zero_heads, zero_heads), jnp.arange(block_count, dtype=jnp.int32)
    )
    grad_queries = grad_query_blocks.reshape(group, local_width)
    grad_keys = grad_keys_sum.astype(jnp.bfloat16).reshape(group, local_width)
    grad_values = grad_values_sum.astype(jnp.bfloat16).reshape(group, local_width)
    grad_query_w = jnp.einsum(
        "gd,gi->di", gathered_one, grad_queries, preferred_element_type=jnp.float32
    )
    grad_key_w = jnp.einsum(
        "gd,gi->di", gathered_one, grad_keys, preferred_element_type=jnp.float32
    )
    grad_value_w = jnp.einsum(
        "gd,gi->di", gathered_one, grad_values, preferred_element_type=jnp.float32
    )

    def partial_term(grads, weight):
        return jnp.einsum("gi,di->gd", grads, weight, preferred_element_type=jnp.float32)

    grad_normed_one = lax.psum_scatter(
        partial_term(grad_queries, query_full)
        + partial_term(grad_keys, key_full)
        + partial_term(grad_values, value_full),
        "tp",
        scatter_dimension=0,
        tiled=True,
    )
    owned_query, owned_key, owned_value, owned_out = (
        lax.psum_scatter(grad_query_w, "fsdp", scatter_dimension=0, tiled=True),
        lax.psum_scatter(grad_key_w, "fsdp", scatter_dimension=0, tiled=True),
        lax.psum_scatter(grad_value_w, "fsdp", scatter_dimension=0, tiled=True),
        lax.psum_scatter(grad_out_w, "fsdp", scatter_dimension=1, tiled=True),
    )
    _, norm_pull_one = jax.vjp(rms_norm, inputs, attn_gain)
    grad_input_part, grad_attn_gain = norm_pull_one(grad_normed_one)
    grad_inputs = grad_hidden + grad_input_part
    summed = lax.psum(
        (grad_attn_gain, grad_moe_gain, grad_router, grad_prior_w, grad_const, grad_vector),
        ("fsdp", "tp"),
    )
    return (
        output,
        grad_inputs,
        grad_prior,
        summed[0],
        owned_query,
        owned_key,
        owned_value,
        owned_out,
        summed[1],
        summed[2],
        summed[3],
        summed[4],
        summed[5],
        grad_gate_own,
        grad_up_own,
        grad_down_own,
    )


def solution(mesh):
    return jax.shard_map(
        per_device,
        mesh=mesh,
        in_specs=(
            P(("fsdp", "tp"), None),
            P(("fsdp", "tp"), None),
            P("fsdp", None),
            P("fsdp", None),
            P("fsdp", None),
            P("fsdp", None),
            P(),
            P("fsdp", "tp"),
            P("fsdp", "tp"),
            P("fsdp", "tp"),
            P("tp", "fsdp"),
            P(),
            P(),
            P(),
            P(),
            P(),
            P(None, "fsdp", "tp"),
            P(None, "fsdp", "tp"),
            P(None, "tp", "fsdp"),
        ),
        out_specs=(
            P(("fsdp", "tp"), None),
            P(("fsdp", "tp"), None),
            P(("fsdp", "tp"), None),
            P(),
            P("fsdp", "tp"),
            P("fsdp", "tp"),
            P("fsdp", "tp"),
            P("tp", "fsdp"),
            P(),
            P(),
            P(),
            P(),
            P(),
            P(None, "fsdp", "tp"),
            P(None, "fsdp", "tp"),
            P(None, "tp", "fsdp"),
        ),
        check_vma=False,
    )
```

profile of v0, /device:TPU:1, one launch (start us, length us, event | category | flops | bytes accessed | tf_op | source)
XLA Modules:
  0.0 2166.1 jit_solution(17893501875384959554)
XLA Ops:
  13.1 27.8 %all_gather.40 = bf16[192,768]{0,1:T(8,128)(2,1)} all-gather(bf16[192,96]{0,1:T(8,128)(2,1)S(1)} %copy.115), channel_id=1, replica_groups=mesh['fsdp'=8,'tp'=4] {'fsdp'}, dimensions={1}, use_global_device_ids=true | all-gather | bytes 331776 | tf_op jit(solution)/shard_map/all_gather | solution.py:121
  40.9 25.0 %all_gather.37 = bf16[768,192]{1,0:T(8,128)(2,1)S(1)} all-gather(bf16[96,192]{1,0:T(8,128)(2,1)S(1)} %copy-done.82), channel_id=1, replica_groups=mesh['fsdp'=8,'tp'=4] {'fsdp'}, dimensions={0}, use_global_device_ids=true | all-gather | bytes 331776 | tf_op jit(solution)/shard_map/all_gather | solution.py:118
  65.9 25.2 %all_gather.38 = bf16[768,192]{1,0:T(8,128)(2,1)S(1)} all-gather(bf16[96,192]{1,0:T(8,128)(2,1)S(1)} %copy-done.83), channel_id=1, replica_groups=mesh['fsdp'=8,'tp'=4] {'fsdp'}, dimensions={0}, use_global_device_ids=true | all-gather | bytes 331776 | tf_op jit(solution)/shard_map/all_gather | solution.py:119
  91.2 24.9 %all_gather.39 = bf16[768,192]{1,0:T(8,128)(2,1)S(1)} all-gather(bf16[96,192]{1,0:T(8,128)(2,1)S(1)} %copy-done.84), channel_id=1, replica_groups=mesh['fsdp'=8,'tp'=4] {'fsdp'}, dimensions={0}, use_global_device_ids=true | all-gather | bytes 331776 | tf_op jit(solution)/shard_map/all_gather | solution.py:120
  121.9 79.1 %while.27 = (s32[]{:T(128)}, bf16[2,1024,3,64]{1,3,2,0:T(8,128)(2,1)S(1)}, f32[2,3,1024]{2,1,0:T(4,128)S(1)}, s32[2]{0:T(128)S(1)}, s32[2048]{0:T(1024)S(1)}, /*...) while((s32[]{:T(128)}, ...), condition=%wide.region_6.7_spmd, body=%wide.region_3.6_spmd.sunk | while | flops 1692596224 | bytes 86393032 | solution.py:154
  137.4 11.8 fusion.250
  149.2 12.3 fusion.251
  176.8 11.8 fusion.250
  188.6 12.3 fusion.251
  206.8 83.9 %reduce-scatter.17.cloned.1.call-done = f32[512,768]{1,0:T(8,128)} async-done(((f32[2048,768]{1,0:T(8,128)}), f32[512,768]{1,0:T(8,128)}) %reduce-scatter.17.cloned.1.call-update) | async-done | bytes 1572880 | tf_op jit(solution)/shard_map/reduce_scatter | solution.py:156
  308.4 15.5 scatter_custom_fusion
  327.0 23.0 %gather_fusion = s32[4096]{0:T(1024)S(1)} fusion(s32[4096]{0:T(1024)S(1)} %fusion.98, s32[4096]{0:T(1024)S(1)} %broadcast_clamp_fusion), kind=kCustom, calls=%fused_computation.4 | custom fusion | bytes 49152 | tf_op jit(solution)/shard_map/gather | solution.py:31
  352.5 15.7 scatter_custom_fusion.2
  368.8 15.5 scatter_custom_fusion.1
  393.9 15.5 scatter_custom_fusion.3
  409.4 13.6 gather_fusion.1
  439.9 83.3 %all-gather.12.cloned.1.call-done = bf16[8,768,512]{2,1,0:T(8,128)(2,1)} async-done(((bf16[8,96,512]{2,1,0:T(8,128)(2,1)}), bf16[8,768,512]{2,1,0:T(8,128)(2,1)}) %all-gather.12.cloned.1.call-update) | async-done | bytes 6291472 | tf_op jit(solution)/shard_map/all_gather | solution.py:166
  533.0 37.7 %all-gather.18.cloned.1.call-done = f32[2048,768]{1,0:T(8,128)} async-done(((f32[512,768]{1,0:T(8,128)}), f32[2048,768]{1,0:T(8,128)}) %all-gather.18.cloned.1.call-update) | async-done | bytes 6291472 | tf_op jit(solution)/shard_map/all_gather | solution.py:207
  570.8 18.3 gather_fusion.2
  598.6 72.7 %all-gather.16.cloned.1.call-done = bf16[8,512,768]{1,2,0:T(8,128)(2,1)} async-done(((bf16[8,512,96]{1,2,0:T(8,128)(2,1)}), bf16[8,512,768]{1,2,0:T(8,128)(2,1)}) %all-gather.16.cloned.1.call-update) | async-done | bytes 6291472 | tf_op jit(solution)/shard_map/all_gather | solution.py:168
  671.3 15.0 multiply_convert_fusion.2
  702.9 14.4 gather_fusion.6
  717.3 14.5 gather_fusion.5
  741.2 14.4 gather_fusion.3
  755.5 14.4 gather_fusion.4
  770.0 15.3 multiply_reduce_fusion.2
  793.7 16.7 reduce-scatter.37.cloned.1.call-done
  812.4 58.9 %reduce-scatter.21.cloned.1.call-done = f32[512,768]{1,0:T(8,128)} async-done(((f32[2048,768]{1,0:T(8,128)}), f32[512,768]{1,0:T(8,128)}) %reduce-scatter.21.cloned.1.call-update) | async-done | bytes 1572880 | tf_op jit(solution)/shard_map/reduce_scatter | solution.py:260
  877.0 55.3 %reduce-scatter.19.cloned.1.call-done = f32[512,768]{1,0:T(8,128)} async-done(((f32[2048,768]{1,0:T(8,128)}), f32[512,768]{1,0:T(8,128)}) %reduce-scatter.19.cloned.1.call-update) | async-done | bytes 1572880 | tf_op jit(solution)/shard_map/reduce_scatter | solution.py:189
  936.5 29.0 %all-gather.20.cloned.1.call-done = bf16[2048,768]{1,0:T(8,128)(2,1)} async-done(((bf16[512,768]{1,0:T(8,128)(2,1)}), bf16[2048,768]{1,0:T(8,128)(2,1)}) %all-gather.20.cloned.1.call-update) | async-done | bytes 3145744 | tf_op jit(solution)/shard_map/all_gather | solution.py:274
  970.7 231.9 %while.28 = (s32[]{:T(128)}, f32[2048,3,64]{0,2,1:T(8,128)}, f32[2048,3,64]{0,2,1:T(8,128)}, bf16[2,1024,3,64]{1,3,2,0:T(8,128)(2,1)}, s32[2]{0:T(128)S(1)}, /*i...) while((s32[]{:T(128)}, f32[2048,3,64]{0,2,1:T(8,128)}, ...), condition=%wide.region_48.50_spmd.clone, body=%wide.region_46.49_spmd.clone.sunk | while | flops 4198181888 | bytes 303305024 | solution.py:304
  977.1 13.1 fusion.263
  990.2 12.9 fusion.266
  1013.2 35.8 %fusion.267 = bf16[2,1024,3,64]{1,3,2,0:T(8,128)(2,1)} fusion(bf16[2,1024,3,64]{1,3,2,0:T(8,128)(2,1)} %get-tuple-element.441, s32[]{:T(128)S(6)} %copy.155, bf16[2048,3,64]{0,2,1:T(8,128)(2,1)} %get-tuple-element.461, f32[3,1024,2048]{2,1,0:T(8,128)} %fusion.262, f32[3,1024,2048]{2,1,0:T(8,128)} %fusion.263, ...), kind=kOutput, calls=%fused_computation.55.clone.1 | convolution fusion | flops 874714112 | bytes 106070016 | tf_op jit(solution)/shard_map/while/body/eval_jaxpr/hqk,khd->qhd/dot_general | solution.py:295
  1049.1 37.0 %fusion.265 = f32[2048,3,64]{0,2,1:T(8,128)} fusion(f32[3,1024,2048]{2,1,0:T(8,128)} %fusion.262, f32[3,1024,2048]{2,1,0:T(8,128)} %fusion.263, f32[3,1024]{1,0:T(4,128)S(1)} %dynamic-slice_bitcast_fusion.2, pred[1024,2048]{1,0:T(8,128)(4,1)S(1)} %fusion.264, f32[2048,3,64]{0,2,1:T(8,128)} %get-tuple-element.439, pred[]{:T(512)S(6)} %compare.11, ...), kind=kOutput, calls=%fused_computation.51.clone.1 | convolution fusion | flops 875303936 | bytes 108429320 | tf_op jit(solution)/shard_map/while/body/eval_jaxpr/hqk,qhd->khd/dot_general | solution.py:298
  1092.3 13.1 fusion.263
  1105.4 13.4 fusion.266
  1128.9 35.8 %fusion.267 = bf16[2,1024,3,64]{1,3,2,0:T(8,128)(2,1)} fusion(bf16[2,1024,3,64]{1,3,2,0:T(8,128)(2,1)} %get-tuple-element.441, s32[]{:T(128)S(6)} %copy.155, bf16[2048,3,64]{0,2,1:T(8,128)(2,1)} %get-tuple-element.461, f32[3,1024,2048]{2,1,0:T(8,128)} %fusion.262, f32[3,1024,2048]{2,1,0:T(8,128)} %fusion.263, ...), kind=kOutput, calls=%fused_computation.55.clone.1 | convolution fusion | flops 874714112 | bytes 106070016 | tf_op jit(solution)/shard_map/while/body/eval_jaxpr/hqk,khd->qhd/dot_general | solution.py:295
  1164.7 37.5 %fusion.265 = f32[2048,3,64]{0,2,1:T(8,128)} fusion(f32[3,1024,2048]{2,1,0:T(8,128)} %fusion.262, f32[3,1024,2048]{2,1,0:T(8,128)} %fusion.263, f32[3,1024]{1,0:T(4,128)S(1)} %dynamic-slice_bitcast_fusion.2, pred[1024,2048]{1,0:T(8,128)(4,1)S(1)} %fusion.264, f32[2048,3,64]{0,2,1:T(8,128)} %get-tuple-element.439, pred[]{:T(512)S(6)} %compare.11, ...), kind=kOutput, calls=%fused_computation.51.clone.1 | convolution fusion | flops 875303936 | bytes 108429320 | tf_op jit(solution)/shard_map/while/body/eval_jaxpr/hqk,qhd->khd/dot_general | solution.py:298
  1228.0 12.6 fusion.93
  1269.3 60.3 %reduce-scatter.23.cloned.1.call-done = f32[512,768]{1,0:T(8,128)} async-done(((f32[2048,768]{1,0:T(8,128)}), f32[512,768]{1,0:T(8,128)}) %reduce-scatter.23.cloned.1.call-update) | async-done | bytes 1572880 | tf_op jit(solution)/shard_map/reduce_scatter | solution.py:323
  1331.4 41.2 %all-reduce.8 = (f32[768]{0:T(1024)}, f32[768]{0:T(1024)}, f32[768,12]{0,1:T(8,128)}, f32[12,12]{1,0:T(8,128)}, f32[2,768,2]{1,2,0:T(2,128)}, /*index=5*/f32[2,768]{1,0:T(2,128)}) all-reduce(f32[768]{0:T(1024)S(1)} %get-tuple-element.169, f32[768]{0:T(1024)S(1)} %copy-done.132, ...), channel_id=1, replica_groups=mesh['fsdp'=8,'tp'=4] {'fsdp','tp'}, use_global_device_ids=true, to_apply=%region_52.54 | all-reduce | flops 15504 | bytes 124032 | tf_op jit(solution)/shard_map/psum | solution.py:340
  1375.6 18.6 reduce-scatter.25.cloned.1.call-done
  1394.1 65.7 %reduce-scatter.27.cloned.1.call-done = f32[96,192]{1,0:T(8,128)} async-done(((f32[768,192]{1,0:T(8,128)}), f32[96,192]{1,0:T(8,128)}) %reduce-scatter.27.cloned.1.call-update) | async-done | bytes 73744 | tf_op jit(solution)/shard_map/reduce_scatter | solution.py:333
  1459.8 65.2 %reduce-scatter.29.cloned.1.call-done = f32[96,192]{1,0:T(8,128)} async-done(((f32[768,192]{1,0:T(8,128)}), f32[96,192]{1,0:T(8,128)}) %reduce-scatter.29.cloned.1.call-update) | async-done | bytes 73744 | tf_op jit(solution)/shard_map/reduce_scatter | solution.py:334
  1525.0 212.4 %reduce-scatter.35.cloned.1.call-done = f32[8,512,96]{1,2,0:T(8,128)} async-done(((f32[8,512,768]{1,2,0:T(8,128)}), f32[8,512,96]{1,2,0:T(8,128)}) %reduce-scatter.35.cloned.1.call-update) | async-done | bytes 1572880 | tf_op jit(solution)/shard_map/reduce_scatter | solution.py:266
  1737.5 210.9 %reduce-scatter.33.cloned.1.call-done = f32[8,96,512]{2,1,0:T(8,128)} async-done(((f32[8,768,512]{2,1,0:T(8,128)}), f32[8,96,512]{2,1,0:T(8,128)}) %reduce-scatter.33.cloned.1.call-update) | async-done | bytes 1572880 | tf_op jit(solution)/shard_map/reduce_scatter | solution.py:265
  1948.3 211.0 %reduce-scatter.31.cloned.1.call-done = f32[8,96,512]{2,1,0:T(8,128)} async-done(((f32[8,768,512]{2,1,0:T(8,128)}), f32[8,96,512]{2,1,0:T(8,128)}) %reduce-scatter.31.cloned.1.call-update) | async-done | bytes 1572880 | tf_op jit(solution)/shard_map/reduce_scatter | solution.py:264
  (492 shorter events, 251.6 us)
Async XLA Ops:
  7.2 293.0 %copy-start = (f32[2048,12]{0,1:T(8,128)S(1)}, f32[2048,12]{0,1:T(8,128)}, u32[]{:S(2)}) copy-start(f32[2048,12]{0,1:T(8,128)} %param.30) | copy-start | bytes 294916
  7.2 83.9 %copy-start.84 = (bf16[96,192]{1,0:T(8,128)(2,1)S(1)}, bf16[96,192]{1,0:T(8,128)(2,1)}, u32[]{:S(2)}) copy-start(bf16[96,192]{1,0:T(8,128)(2,1)} %param.34) | copy-start | bytes 110596
  7.2 108.9 %all-gather.8.cloned.1.call-start = ((), (), s32[]{:S(2)}) async-start(), calls=%async_computation.12 | async-start | bytes 3932160 | tf_op jit(solution)/shard_map/all_gather | solution.py:116
  12.6 278.1 %reduce-scatter.17.cloned.1.call-start = ((), (), s32[]{:S(2)}) async-start(), calls=%async_computation.13 | async-start | bytes 7864320 | tf_op jit(solution)/shard_map/reduce_scatter | solution.py:156
  201.0 94.9 %copy-start.33 = (s32[2048]{0:T(1024)}, s32[2048]{0:T(1024)S(1)}, u32[]{:S(2)}) copy-start(s32[2048]{0:T(1024)S(1)} %get-tuple-element.524) | copy-start | bytes 24580
  206.7 84.0 %copy-start.5 = (f32[512,768]{1,0:T(8,128)S(1)}, f32[512,768]{1,0:T(8,128)}, u32[]{:S(2)}) copy-start(f32[512,768]{1,0:T(8,128)} %param.25) | copy-start | bytes 4718596
  206.7 86.2 %copy-start.48 = (f32[768]{0:T(1024)S(1)}, f32[768]{0:T(1024)}, u32[]{:S(2)}) copy-start(f32[768]{0:T(1024)} %param.36) | copy-start | bytes 9220
  206.8 178.9 %all-gather.10.cloned.1.call-start = ((), (), s32[]{:S(2)}) async-start(), calls=%async_computation.14 | async-start | bytes 3932160 | tf_op jit(solution)/shard_map/all_gather | solution.py:164
  294.1 135.6 %all-gather.14.cloned.1.call-start = ((), (), s32[]{:S(2)}) async-start(), calls=%async_computation.16 | async-start | bytes 7077888 | tf_op jit(solution)/shard_map/all_gather | solution.py:167
  294.7 228.5 %all-gather.12.cloned.1.call-start = ((), (), s32[]{:S(2)}) async-start(), calls=%async_computation.15 | async-start | bytes 7077888 | tf_op jit(solution)/shard_map/all_gather | solution.py:166
  295.3 275.5 %all-gather.18.cloned.1.call-start = ((), (), s32[]{:S(2)}) async-start(), calls=%async_computation.19 | async-start | bytes 7864320 | tf_op jit(solution)/shard_map/all_gather | solution.py:207
  305.7 365.6 %all-gather.16.cloned.1.call-start = ((), (), s32[]{:S(2)}) async-start(), calls=%async_computation.17 | async-start | bytes 7077888 | tf_op jit(solution)/shard_map/all_gather | solution.py:168
  306.4 504.0 %reduce-scatter.37.cloned.1.call-start = ((), (), s32[]{:S(2)}) async-start(), calls=%async_computation.29 | async-start | bytes 1310720
  368.3 154.9 %copy-start.41 = (bf16[8,384]{1,0:T(8,128)(2,1)}, bf16[8,384]{1,0:T(8,128)(2,1)S(1)}, u32[]{:S(2)}) copy-start(bf16[8,384]{1,0:T(8,128)(2,1)S(1)} %convert_element_type.98) | copy-start | bytes 18436
  384.4 286.9 %copy-start.46 = (pred[8,384]{1,0:T(8,128)(4,1)}, pred[8,384]{1,0:T(8,128)(4,1)S(1)}, u32[]{:S(2)}) copy-start(pred[8,384]{1,0:T(8,128)(4,1)S(1)} %compare_and_fusion.2) | copy-start | bytes 9220
  409.4 261.9 %copy-start.86 = (f32[8,384]{1,0:T(8,128)}, f32[8,384]{1,0:T(8,128)S(1)}, u32[]{:S(2)}) copy-start(f32[8,384]{1,0:T(8,128)S(1)} %mul.601) | copy-start | bytes 36868
  786.7 84.6 %reduce-scatter.21.cloned.1.call-start = ((), (), s32[]{:S(2)}) async-start(), calls=%async_computation.20 | async-start | bytes 7864320 | tf_op jit(solution)/shard_map/reduce_scatter | solution.py:260
  787.5 144.9 %reduce-scatter.19.cloned.1.call-start = ((), (), s32[]{:S(2)}) async-start(), calls=%async_computation.18 | async-start | bytes 7864320 | tf_op jit(solution)/shard_map/reduce_scatter | solution.py:189
  788.1 83.3 %copy-start.3 = (f32[512,768]{1,0:T(8,128)S(1)}, f32[512,768]{1,0:T(8,128)}, u32[]{:S(2)}) copy-start(f32[512,768]{1,0:T(8,128)} %copy-done.2) | copy-start | bytes 4718596
  788.1 83.3 %copy-start.12 = (f32[512,768]{1,0:T(8,128)S(1)}, f32[512,768]{1,0:T(8,128)}, u32[]{:S(2)}) copy-start(f32[512,768]{1,0:T(8,128)} %get-tuple-element.226) | copy-start | bytes 4718596
  788.1 83.2 %copy-start.44 = (f32[768,12]{0,1:T(8,128)S(1)}, f32[768,12]{0,1:T(8,128)}, u32[]{:S(2)}) copy-start(f32[768,12]{0,1:T(8,128)} %param.37) | copy-start | bytes 110596
  788.2 83.2 %copy-start.49 = (f32[768]{0:T(1024)S(1)}, f32[768]{0:T(1024)}, u32[]{:S(2)}) copy-start(f32[768]{0:T(1024)} %param.36) | copy-start | bytes 9220
  788.2 83.2 %copy-start.54 = (f32[512]{0:T(512)S(1)}, f32[512]{0:T(512)}, u32[]{:S(2)}) copy-start(f32[512]{0:T(512)} %copy-done.53) | copy-start | bytes 6148
  788.2 83.2 %copy-start.104 = (f32[512,1]{0,1:T(1,128)S(1)}, f32[512,1]{0,1:T(1,128)}, u32[]{:S(2)}) copy-start(f32[512,1]{0,1:T(1,128)} %copy-done.103) | copy-start | bytes 6148
  788.2 83.2 %copy-start.106 = (f32[512,1]{0,1:T(1,128)S(1)}, f32[512,1]{0,1:T(1,128)}, u32[]{:S(2)}) copy-start(f32[512,1]{0,1:T(1,128)} %copy-done.105) | copy-start | bytes 6148
  788.2 83.2 %copy-start.108 = (f32[512]{0:T(512)S(1)}, f32[512]{0:T(512)}, u32[]{:S(2)}) copy-start(f32[512]{0:T(512)} %copy-done.107) | copy-start | bytes 6148
  788.2 83.2 %copy-start.110 = (f32[512]{0:T(512)S(1)}, f32[512]{0:T(512)}, u32[]{:S(2)}) copy-start(f32[512]{0:T(512)} %copy-done.109) | copy-start | bytes 6148
  788.2 83.2 %copy-start.127 = (f32[512]{0:T(512)S(1)}, f32[512]{0:T(512)}, u32[]{:S(2)}) copy-start(f32[512]{0:T(512)} %get-tuple-element.175) | copy-start | bytes 6148
  788.2 177.3 %all-gather.20.cloned.1.call-start = ((), (), s32[]{:S(2)}) async-start(), calls=%async_computation.21 | async-start | bytes 3932160 | tf_op jit(solution)/shard_map/all_gather | solution.py:274
  812.4 64.6 %copy-start.37 = (f32[512,12]{0,1:T(8,128)}, f32[512,12]{0,1:T(8,128)S(1)}, u32[]{:S(2)}) copy-start(f32[512,12]{0,1:T(8,128)S(1)} %add_multiply_fusion.1) | copy-start | bytes 73732
  871.5 60.9 %copy-start.89 = (f32[768]{0:T(1024)S(1)}, f32[768]{0:T(1024)}, u32[]{:S(2)}) copy-start(f32[768]{0:T(1024)} %copy-done.88) | copy-start | bytes 9220
  871.5 60.9 %copy-start.91 = (f32[768]{0:T(1024)S(1)}, f32[768]{0:T(1024)}, u32[]{:S(2)}) copy-start(f32[768]{0:T(1024)} %copy-done.90) | copy-start | bytes 9220
  871.5 60.9 %copy-start.118 = (f32[512]{0:T(512)S(1)}, f32[512]{0:T(512)}, u32[]{:S(2)}) copy-start(f32[512]{0:T(512)} %copy-done.117) | copy-start | bytes 6148
  871.5 60.8 %copy-start.124 = (f32[512,1]{0,1:T(1,128)S(1)}, f32[512,1]{0,1:T(1,128)}, u32[]{:S(2)}) copy-start(f32[512,1]{0,1:T(1,128)} %copy-done.123) | copy-start | bytes 6148
  936.5 331.2 %reduce-scatter.39.cloned.1.call-start = ((), (), s32[]{:S(2)}) async-start(), calls=%async_computation.30 | async-start | bytes 884736
  1207.1 122.4 %reduce-scatter.23.cloned.1.call-start = ((), (), s32[]{:S(2)}) async-start(), calls=%async_computation.22 | async-start | bytes 7864320 | tf_op jit(solution)/shard_map/reduce_scatter | solution.py:323
  1216.6 177.5 %reduce-scatter.25.cloned.1.call-start = ((), (), s32[]{:S(2)}) async-start(), calls=%async_computation.23 | async-start | bytes 884736 | tf_op jit(solution)/shard_map/reduce_scatter | solution.py:332
  1221.6 238.2 %reduce-scatter.27.cloned.1.call-start = ((), (), s32[]{:S(2)}) async-start(), calls=%async_computation.24 | async-start | bytes 884736 | tf_op jit(solution)/shard_map/reduce_scatter | solution.py:333
  1224.8 300.2 %reduce-scatter.29.cloned.1.call-start = ((), (), s32[]{:S(2)}) async-start(), calls=%async_computation.25 | async-start | bytes 884736 | tf_op jit(solution)/shard_map/reduce_scatter | solution.py:334
  1228.0 509.5 %reduce-scatter.35.cloned.1.call-start = ((), (), s32[]{:S(2)}) async-start(), calls=%async_computation.28 | async-start | bytes 14155776 | tf_op jit(solution)/shard_map/reduce_scatter | solution.py:266
  1240.7 707.7 %reduce-scatter.33.cloned.1.call-start = ((), (), s32[]{:S(2)}) async-start(), calls=%async_computation.27 | async-start | bytes 14155776 | tf_op jit(solution)/shard_map/reduce_scatter | solution.py:265
  1251.5 907.8 %reduce-scatter.31.cloned.1.call-start = ((), (), s32[]{:S(2)}) async-start(), calls=%async_computation.26 | async-start | bytes 14155776 | tf_op jit(solution)/shard_map/reduce_scatter | solution.py:264
  1262.5 67.1 %copy-start.6 = (f32[512,768]{1,0:T(8,128)S(1)}, f32[512,768]{1,0:T(8,128)}, u32[]{:S(2)}) copy-start(f32[512,768]{1,0:T(8,128)} %param.25) | copy-start | bytes 4718596
  1262.5 67.0 %copy-start.92 = (f32[768]{0:T(1024)S(1)}, f32[768]{0:T(1024)}, u32[]{:S(2)}) copy-start(f32[768]{0:T(1024)} %param.31) | copy-start | bytes 9220
  1262.5 67.0 %copy-start.116 = (f32[512]{0:T(512)S(1)}, f32[512]{0:T(512)}, u32[]{:S(2)}) copy-start(f32[512]{0:T(512)} %copy-done.115) | copy-start | bytes 6148
  1264.9 66.5 %copy-start.132 = (f32[768]{0:T(1024)S(1)}, f32[768]{0:T(1024)}, u32[]{:S(2)}) copy-start(f32[768]{0:T(1024)} %get-tuple-element.167) | copy-start | bytes 9220
  1264.9 107.7 %copy-start.129 = (f32[512]{0:T(512)S(1)}, f32[512]{0:T(512)}, u32[]{:S(2)}) copy-start(f32[512]{0:T(512)} %copy-done.128) | copy-start | bytes 6148
  1266.0 106.6 %copy-start.20 = (f32[512,768]{1,0:T(8,128)S(1)}, f32[512,768]{1,0:T(8,128)}, u32[]{:S(2)}) copy-start(f32[512,768]{1,0:T(8,128)} %get-tuple-element.225) | copy-start | bytes 4718596
  (115 other events, 965.8 us)
Sparse Core Ops, SparseCore 0:
  12.7 31.0 all-gather.7
  206.9 83.8 reduce-scatter.16
  294.2 28.9 all-gather.9
  325.5 98.0 all-gather.13
  425.9 97.2 all-gather.11
  525.2 45.4 all-gather.17
  573.2 98.0 all-gather.15
  786.9 23.5 reduce-scatter.36
  813.0 58.3 reduce-scatter.20
  873.9 58.3 reduce-scatter.18
  936.6 28.9 all-gather.19
  1207.2 60.3 reduce-scatter.38
  1270.3 59.1 reduce-scatter.22
  1333.2 60.8 reduce-scatter.24
  1398.2 61.5 reduce-scatter.26
  1463.5 61.4 reduce-scatter.28
  1529.5 207.9 reduce-scatter.34
  1741.9 206.3 reduce-scatter.32
  1952.9 206.3 reduce-scatter.30
where the time goes:
time: 2170 us
  waiting for transfers between devices  1280 us (59%)
  matrix products  413 us (19%)
  local copies, waits for them, and re-layouts  220 us (10%)
  blocking collectives  144 us (7%)
  other arithmetic  78 us (4%)
    reduce_scatter x1, waiting for transfers between devices, per_device(): lax.psum_scatter(grad_down_w, 'fsdp', scatter_dimension=2, tiled=True)  212 us
    reduce_scatter x1, waiting for transfers between devices, per_device(): lax.psum_scatter(grad_gate_w, 'fsdp', scatter_dimension=1, tiled=True)  211 us
    reduce_scatter x1, waiting for transfers between devices, per_device(): lax.psum_scatter(grad_up_w, 'fsdp', scatter_dimension=1, tiled=True)  211 us
    reduce_scatter x1, waiting for transfers between devices, per_device(): lax.psum_scatter(jnp.dot(mixed, out_full, preferred_element_type=jnp.floa...  83.9 us
    all_gather x1, waiting for transfers between devices, per_device(): lax.all_gather(w_gate, 'fsdp', axis=1, tiled=True)  83.3 us
    dot_general x2, matrix products, backward_block(): jnp.einsum('hqk,qhd->khd', grad_raw, query_rows, preferred_element_type=j...  74.5 us
    all_gather x1, waiting for transfers between devices, per_device(): lax.all_gather(w_down, 'fsdp', axis=2, tiled=True)  72.7 us
    dot_general x2, matrix products, backward_block(): jnp.einsum('hqk,khd->qhd', grad_raw, keys, preferred_element_type=jnp.flo...  71.6 us
  transfers between devices with their start and end apart: 19, of which 16 were waited for; matrix products, arithmetic and copies ran while one was open for 12% of the time, Pallas kernels for 0%

commit v1 on v0

v1 whole, which is shorter than its diff:
```python
import functools

import jax
import jax.numpy as jnp
from jax import lax
from jax.experimental import pallas as pl
from jax.experimental.pallas import tpu as pltpu
from jax.sharding import Mesh
from jax.sharding import PartitionSpec as P

HEAD = 64
MAXLEN = 768
LOW = 4
EPSILON = 1e-06
PRECISE = lax.Precision.HIGHEST
NEGATIVE = -1e30
F32 = jnp.float32
BF16 = jnp.bfloat16


def rms_norm(values, gain):
    return values * lax.rsqrt(jnp.mean(values * values, axis=-1, keepdims=True) + EPSILON) * gain


def swap(value, axis):
    return lax.ppermute(value, axis, [(0, 1), (1, 0)])


def gather_pieces(value):
    other = swap(value, "y")
    return [value, swap(value, "c"), other, swap(other, "c")]


def natural(pieces, index):
    ordered = []
    for j in range(4):
        item = pieces[j]
        for t in range(1, 4):
            item = jnp.where(index == t, pieces[j ^ t], item)
        ordered.append(item)
    return jnp.stack(ordered)


def scatter_sum(blocks):
    sent = swap(jnp.stack([blocks[1], blocks[3]]).astype(BF16), "c")
    own = blocks[0] + sent[0].astype(F32)
    other = blocks[2] + sent[1].astype(F32)
    return own + swap(other.astype(BF16), "y").astype(F32)


def scores_mask(first_key, first_query, window, block, start_row):
    key_places = first_key + lax.broadcasted_iota(jnp.int32, (window, block), 0)
    query_places = first_query + lax.broadcasted_iota(jnp.int32, (window, block), 1)
    return (key_places >= start_row) & (key_places <= query_places)


def attend_kernel(block, pad, q_ref, k_ref, v_ref, start_ref, out_ref, lse_ref, key_rows, value_pad):
    group = q_ref.shape[1]
    window = pad + block
    quarter = group // 4
    key_rows[pl.ds(0, pad), :] = jnp.zeros((pad, HEAD), BF16)
    value_pad[:, pl.ds(0, pad)] = jnp.zeros((HEAD, pad), BF16)
    key_rows[pl.ds(pad, group), :] = k_ref[...].T
    value_pad[:, pl.ds(pad, group)] = v_ref[...]

    def one(i, carry):
        first = pl.multiple_of(i * block, block)
        scores = jnp.dot(
            key_rows[pl.ds(first, window), :],
            q_ref[:, pl.ds(first, block)],
            preferred_element_type=F32,
        )
        allowed = scores_mask(first - pad, first, window, block, start_ref[:, pl.ds(first, block)])
        scores = jnp.where(allowed, scores * 0.125, NEGATIVE)
        highest = jnp.max(scores, axis=0, keepdims=True)
        weights = jnp.exp(scores - highest)
        total = jnp.sum(weights, axis=0, keepdims=True)
        mixed = jnp.dot(
            value_pad[:, pl.ds(first, window)], weights.astype(BF16), preferred_element_type=F32
        )
        mixed = (mixed / total).astype(BF16)
        out_ref[first // quarter, :, pl.ds(pl.multiple_of(first % quarter, block), block)] = mixed
        lse_ref[0, :, pl.ds(first, block)] = highest + jnp.log(total)
        return carry

    lax.fori_loop(0, group // block, one, 0)


def attend(qkv, starts, heads):
    group = qkv.shape[1]
    block = 256
    return pl.pallas_call(
        functools.partial(attend_kernel, block, MAXLEN),
        grid=(heads,),
        in_specs=[
            pl.BlockSpec((HEAD, group), lambda h: (h, 0)),
            pl.BlockSpec((HEAD, group), lambda h: (h + heads, 0)),
            pl.BlockSpec((HEAD, group), lambda h: (h + 2 * heads, 0)),
            pl.BlockSpec((1, group), lambda h: (0, 0)),
        ],
        out_specs=[
            pl.BlockSpec((4, HEAD, group // 4), lambda h: (0, h, 0)),
            pl.BlockSpec((1, 1, group), lambda h: (h, 0, 0)),
        ],
        out_shape=[
            jax.ShapeDtypeStruct((4, heads * HEAD, group // 4), BF16),
            jax.ShapeDtypeStruct((heads, 1, group), F32),
        ],
        scratch_shapes=[
            pltpu.VMEM((MAXLEN + group, HEAD), BF16),
            pltpu.VMEM((HEAD, MAXLEN + group), BF16),
        ],
        compiler_params=pltpu.CompilerParams(vmem_limit_bytes=48 * 2**20),
        name="attend",
    )(qkv, qkv, qkv, starts)


def attend_back_kernel(
    block, pad, q_ref, k_ref, v_ref, g_ref, start_ref, lse_ref, out_ref,
    key_rows, value_rows, key_pad, grad_key, grad_value,
):
    group = q_ref.shape[1]
    window = pad + block
    quarter = group // 4
    contract_last = (((1,), (1,)), ((), ()))
    key_rows[pl.ds(0, pad), :] = jnp.zeros((pad, HEAD), BF16)
    value_rows[pl.ds(0, pad), :] = jnp.zeros((pad, HEAD), BF16)
    key_pad[:, pl.ds(0, pad)] = jnp.zeros((HEAD, pad), BF16)
    key_rows[pl.ds(pad, group), :] = k_ref[...].T
    value_rows[pl.ds(pad, group), :] = v_ref[...].T
    key_pad[:, pl.ds(pad, group)] = k_ref[...]
    grad_key[...] = jnp.zeros_like(grad_key)
    grad_value[...] = jnp.zeros_like(grad_value)

    def one(i, carry):
        first = pl.multiple_of(i * block, block)
        query = q_ref[:, pl.ds(first, block)]
        grad = g_ref[:, pl.ds(first, block)]
        scores = jnp.dot(key_rows[pl.ds(first, window), :], query, preferred_element_type=F32)
        allowed = scores_mask(first - pad, first, window, block, start_ref[:, pl.ds(first, block)])
        exponent = jnp.where(allowed, scores * 0.125 - lse_ref[0, :, pl.ds(first, block)], NEGATIVE)
        probs = jnp.exp(exponent)
        grad_probs = jnp.dot(
            value_rows[pl.ds(first, window), :], grad, preferred_element_type=F32
        )
        inner = jnp.sum(probs * grad_probs, axis=0, keepdims=True)
        raw = (0.125 * (probs * (grad_probs - inner))).astype(BF16)
        grad_query = jnp.dot(key_pad[:, pl.ds(first, window)], raw, preferred_element_type=F32)
        out_ref[
            first // quarter, 0, :, pl.ds(pl.multiple_of(first % quarter, block), block)
        ] = grad_query.astype(BF16)
        grad_value[:, pl.ds(first, window)] += lax.dot_general(
            grad, probs.astype(BF16), contract_last, preferred_element_type=F32
        )
        grad_key[:, pl.ds(first, window)] += lax.dot_general(
            query, raw, contract_last, preferred_element_type=F32
        )
        return carry

    lax.fori_loop(0, group // block, one, 0)
    for j in range(4):
        out_ref[j, 1] = grad_key[:, pl.ds(pad + j * quarter, quarter)].astype(BF16)
        out_ref[j, 2] = grad_value[:, pl.ds(pad + j * quarter, quarter)].astype(BF16)


def attend_back(qkv, grad_mixed, starts, lse, heads):
    group = qkv.shape[1]
    block = 256
    return pl.pallas_call(
        functools.partial(attend_back_kernel, block, MAXLEN),
        grid=(heads,),
        in_specs=[
            pl.BlockSpec((HEAD, group), lambda h: (h, 0)),
            pl.BlockSpec((HEAD, group), lambda h: (h + heads, 0)),
            pl.BlockSpec((HEAD, group), lambda h: (h + 2 * heads, 0)),
            pl.BlockSpec((HEAD, group), lambda h: (h, 0)),
            pl.BlockSpec((1, group), lambda h: (0, 0)),
            pl.BlockSpec((1, 1, group), lambda h: (h, 0, 0)),
        ],
        out_specs=pl.BlockSpec((4, 3, HEAD, group // 4), lambda h: (0, 0, h, 0)),
        out_shape=jax.ShapeDtypeStruct((4, 3, heads * HEAD, group // 4), BF16),
        scratch_shapes=[
            pltpu.VMEM((MAXLEN + group, HEAD), BF16),
            pltpu.VMEM((MAXLEN + group, HEAD), BF16),
            pltpu.VMEM((HEAD, MAXLEN + group), BF16),
            pltpu.VMEM((HEAD, MAXLEN + group), F32),
            pltpu.VMEM((HEAD, MAXLEN + group), F32),
        ],
        compiler_params=pltpu.CompilerParams(vmem_limit_bytes=48 * 2**20),
        name="attend_back",
    )(qkv, qkv, qkv, grad_mixed, starts, lse)


def slots_of(routes, drop_order, valid, capacity, experts, parity, half):
    group = routes.shape[0]
    live = (routes < experts) & valid[:, None]
    target = jnp.where(live, routes, experts).reshape(-1)
    span = 2 * group
    code = target * span + drop_order.reshape(-1)
    smaller = jnp.sum((code[:, None] < code[None, :]).astype(jnp.int32), axis=0)
    ids = jnp.arange(experts + 1, dtype=jnp.int32)
    earlier = jnp.sum((target[:, None] < ids[None, :]).astype(jnp.int32), axis=0)
    base = jnp.sum(jnp.where(target[:, None] == ids[None, :], earlier[None, :], 0), axis=1)
    place = smaller - base
    share = capacity // 2
    mine = (
        (target < experts)
        & (place < capacity)
        & (target % 2 == parity)
        & (place // share == half)
    )
    slot = (target // 2) * share + place - half * share
    return jnp.where(mine, slot, -1).reshape(group, 2)


def router_of(rounded, prior_rows, w_router, w_prior):
    logits = jnp.dot(rounded, w_router, precision=PRECISE) + jnp.dot(
        prior_rows, w_prior, precision=PRECISE
    )
    return jax.nn.softmax(logits, axis=-1)


def picked_of(route_rows, kinds):
    return (
        route_rows[:, :, None] == jnp.arange(kinds, dtype=jnp.int32)[None, None, :]
    ).astype(F32)


def other_terms(normed, router, w_const, const_vector, route_rows, experts):
    mix_one = jax.nn.softmax(jnp.dot(normed, w_const[0], precision=PRECISE), axis=-1)
    mix_two = jax.nn.softmax(jnp.dot(normed, w_const[1], precision=PRECISE), axis=-1)
    constant_one = mix_one[:, :1] * normed + mix_one[:, 1:] * const_vector[0]
    constant_two = mix_two[:, :1] * normed + mix_two[:, 1:] * const_vector[1]

    def weight(kind):
        named = jnp.any(route_rows == kind, axis=1, keepdims=True).astype(F32)
        return router[:, kind : kind + 1] * named

    return (
        weight(experts + 1) * normed
        + weight(experts + 2) * constant_one
        + weight(experts + 3) * constant_two
    )


def two_parts(value):
    high = lax.reduce_precision(value, 8, 7)
    return jnp.concatenate([high, value - high], axis=-1).astype(BF16)


def per_device(
    many,
    inputs,
    cotangent,
    lengths,
    routes,
    drop_order,
    prior_logits,
    attn_gain,
    w_query,
    w_key,
    w_value,
    w_out,
    moe_gain,
    w_router,
    w_prior,
    w_const,
    const_vector,
    w_gate,
    w_up,
    w_down,
):
    tok_rows, width = inputs.shape
    group = tok_rows * 4
    kinds = w_router.shape[1]
    experts, shard_rows, shard_units = w_gate.shape
    capacity = 3 * group // 16
    share = capacity // 2
    local_width = w_query.shape[1]
    heads = local_width // HEAD
    high = lax.axis_index("hi")
    parity = lax.axis_index("y")
    core = lax.axis_index("c")
    place_in_group = parity * 2 + core
    first_mine = place_in_group * tok_rows

    attn_weights = jnp.concatenate([w_query, w_key, w_value, w_out.T], axis=1)
    attn_full = lax.all_gather(attn_weights, ("hi", "lo"), axis=0, tiled=True)
    normed_one = rms_norm(inputs, attn_gain).astype(BF16)
    normed_pieces = gather_pieces(normed_one)
    expert_shards = jnp.stack([w_gate, w_up, w_down.transpose(0, 2, 1)], axis=1)
    expert_part = lax.all_to_all(expert_shards, ("lo", "y"), 0, 0, tiled=True)
    if many == 2:
        expert_rows = jnp.stack([expert_part, swap(expert_part, "hi")])
    else:
        expert_rows = lax.all_gather(expert_part, "hi", axis=0)
    expert_all = jnp.stack([expert_rows, swap(expert_rows, "c")]).reshape(
        2, many, LOW, 2, 3, shard_rows, shard_units
    )
    expert_all = expert_all.transpose(4, 1, 2, 5, 0, 3, 6).reshape(3, width, 4 * shard_units)
    attn_all = lax.all_gather(attn_full, ("y", "c"), axis=0)

    boundary = jnp.cumsum(lengths[0])
    places = jnp.arange(group, dtype=jnp.int32)
    reached = places[:, None] >= boundary[None, :]
    segment = jnp.sum(reached.astype(jnp.int32), axis=1)
    starts = jnp.max(jnp.where(reached, boundary[None, :], 0), axis=1).reshape(1, group)
    valid = segment < lengths.shape[1] - 1
    pair_slots = slots_of(routes, drop_order, valid, capacity, experts, parity, core)
    relative = jnp.arange(4, dtype=jnp.int32) ^ place_in_group
    slots_by_piece = jnp.take(pair_slots.reshape(4, tok_rows, 2), relative, axis=0).reshape(
        group, 2
    )
    slot_ids = jnp.arange(LOW * share, dtype=jnp.int32)[:, None]
    dispatch = (
        (slot_ids == slots_by_piece[None, :, 0]) | (slot_ids == slots_by_piece[None, :, 1])
    ).astype(BF16)
    slot_expert = (slot_ids // share) * 2 + parity
    slot_kind = (slot_expert == jnp.arange(kinds, dtype=jnp.int32)[None, :]).astype(F32)
    valid_mine = lax.dynamic_slice_in_dim(valid, first_mine, tok_rows).astype(F32)[:, None]
    routes_mine = lax.dynamic_slice_in_dim(routes, first_mine, tok_rows)
    prior_mine = lax.dynamic_slice_in_dim(prior_logits, first_mine, tok_rows)
    grad_out = cotangent * valid_mine
    grad_out_pieces = jnp.concatenate(gather_pieces(grad_out.astype(BF16)), axis=0)
    grad_out_slots = jnp.dot(dispatch, grad_out_pieces, preferred_element_type=F32)

    normed_all = natural(normed_pieces, place_in_group).reshape(group, width)
    qkv = lax.dot_general(
        attn_full[:, : 3 * local_width],
        normed_all,
        (((0,), (1,)), ((), ())),
        preferred_element_type=F32,
    ).astype(BF16)
    mixed, lse = attend(qkv, starts, heads)
    mixed_mine = lax.all_to_all(mixed, ("y", "c"), 0, 0, tiled=True)
    out_all = attn_all[:, :, 3 * local_width :]
    hidden = inputs + jnp.einsum(
        "jit,jdi->td", mixed_mine, out_all, preferred_element_type=F32
    )

    normed_two = rms_norm(hidden, moe_gain)
    rounded_two = normed_two.astype(BF16)

    def local_gate(normed, rounded, prior_rows, router_weight, prior_weight, const_weight, const_vec):
        router = router_of(rounded, prior_rows, router_weight, prior_weight)
        return (
            router,
            other_terms(normed, router, const_weight, const_vec, routes_mine, experts),
        )

    (router, other_mine), gate_pull = jax.vjp(
        local_gate,
        normed_two,
        rounded_two.astype(F32),
        prior_mine,
        w_router,
        w_prior,
        w_const,
        const_vector,
    )
    extra = jnp.pad(two_parts(router), ((0, 0), (0, 128 - 2 * kinds)))
    sent_two = jnp.concatenate([rounded_two, extra], axis=1)
    pieces_two = jnp.concatenate(gather_pieces(sent_two), axis=0)
    picked_slots = jnp.dot(dispatch, pieces_two, preferred_element_type=F32)
    slot_router = (
        picked_slots[:, width : width + kinds]
        + picked_slots[:, width + kinds : width + 2 * kinds]
    )
    slot_weight = jnp.sum(slot_router * slot_kind, axis=1, keepdims=True)
    sent_slots = jnp.concatenate(
        [picked_slots[:, :width].astype(BF16), (grad_out_slots * slot_weight).astype(BF16)], axis=1
    ).reshape(LOW, share, 2 * width)
    taken = lax.all_to_all(sent_slots, "lo", 0, 0, tiled=True).reshape(LOW * share, 2, width)
    if many == 2:
        taken = jnp.where(high == 0, taken, jnp.roll(taken, width // 2, axis=2))
    dispatched, grad_expert = taken[:, 0], taken[:, 1]

    gate_w, up_w, down_w = expert_all[0], expert_all[1], expert_all[2]
    contract_last = (((1,), (1,)), ((), ()))
    contract_first = (((0,), (0,)), ((), ()))
    gate_pre = jnp.dot(dispatched, gate_w, preferred_element_type=F32)
    up_pre = jnp.dot(dispatched, up_w, preferred_element_type=F32)
    sigmoid_gate = jax.nn.sigmoid(gate_pre)
    activated = (gate_pre * sigmoid_gate * up_pre).astype(BF16)
    expert_out = lax.dot_general(activated, down_w, contract_last, preferred_element_type=F32)
    grad_act = jnp.dot(grad_expert, down_w, preferred_element_type=F32)
    grad_gate = (
        grad_act * up_pre * sigmoid_gate * (1.0 + gate_pre * (1.0 - sigmoid_gate))
    ).astype(BF16)
    grad_up = (grad_act * gate_pre * sigmoid_gate).astype(BF16)
    grad_slots = lax.dot_general(
        grad_gate, gate_w, contract_last, preferred_element_type=F32
    ) + lax.dot_general(grad_up, up_w, contract_last, preferred_element_type=F32)
    weight_grads = jnp.stack(
        [
            lax.dot_general(dispatched, grad_gate, contract_first, preferred_element_type=F32),
            lax.dot_general(dispatched, grad_up, contract_first, preferred_element_type=F32),
            lax.dot_general(grad_expert, activated, contract_first, preferred_element_type=F32),
        ]
    ).reshape(3, many, LOW, shard_rows, 2, 2, shard_units)
    weight_sum = weight_grads[:, :, :, :, 0] + swap(
        weight_grads[:, :, :, :, 1].astype(BF16), "c"
    ).astype(F32)
    if many == 2:
        weight_part = weight_sum[:, 0] + swap(weight_sum[:, 1].astype(BF16), "hi").astype(F32)
    else:
        weight_part = lax.psum_scatter(weight_sum, "hi", scatter_dimension=1)
    weight_part = weight_part.astype(BF16).transpose(1, 3, 0, 2, 4)
    weight_own = lax.all_to_all(
        weight_part.reshape(2 * LOW, 3, shard_rows, shard_units), ("lo", "y"), 0, 0, tiled=True
    ).astype(F32)
    grad_gate_own = weight_own[:, 0]
    grad_up_own = weight_own[:, 1]
    grad_down_own = weight_own[:, 2].transpose(0, 2, 1)

    returned = jnp.concatenate([expert_out, grad_slots], axis=1).astype(BF16)
    returned = returned.reshape(LOW * share, 2, width)
    if many == 2:
        returned = jnp.where(high == 0, returned, jnp.roll(returned, width // 2, axis=2))
    returned = lax.all_to_all(
        returned.reshape(LOW, share, 2 * width), "lo", 0, 0, tiled=True
    ).reshape(LOW * share, 2 * width)
    out_slots = returned[:, :width].astype(F32)
    pair_slots_grad = jnp.sum(out_slots * grad_out_slots, axis=1, keepdims=True) * slot_kind
    extra_back = jnp.pad(two_parts(pair_slots_grad), ((0, 0), (0, 128 - 2 * kinds)))
    back_slots = jnp.concatenate([returned[:, width:], extra_back], axis=1)
    back_blocks = lax.dot_general(
        dispatch, back_slots, contract_first, preferred_element_type=F32
    ).reshape(4, tok_rows, width + 128)
    back_mine = scatter_sum(back_blocks)
    feed_blocks = lax.dot_general(
        dispatch,
        (out_slots * slot_weight).astype(BF16),
        contract_first,
        preferred_element_type=F32,
    ).reshape(4, tok_rows, width)
    feed_mine = scatter_sum(feed_blocks)
    output = valid_mine * (hidden + feed_mine + other_mine)

    grad_router_rows = (
        back_mine[:, width : width + kinds] + back_mine[:, width + kinds : width + 2 * kinds]
    )
    grad_normed, grad_rounded, grad_prior, grad_router, grad_prior_w, grad_const, grad_vector = (
        gate_pull((grad_router_rows, grad_out))
    )
    _, norm_pull_two = jax.vjp(rms_norm, hidden, moe_gain)
    grad_hidden_part, grad_moe_gain = norm_pull_two(
        grad_normed + grad_rounded + back_mine[:, :width]
    )
    grad_hidden = grad_out + grad_hidden_part

    grad_attn_all = natural(gather_pieces(grad_hidden.astype(BF16)), place_in_group)
    grad_mixed = lax.dot_general(
        attn_full[:, 3 * local_width :],
        grad_attn_all.reshape(group, width),
        (((0,), (1,)), ((), ())),
        preferred_element_type=F32,
    ).astype(BF16)
    grad_out_w = jnp.einsum("jit,jtd->di", mixed, grad_attn_all, preferred_element_type=F32)
    grad_qkv = attend_back(qkv, grad_mixed, starts, lse, heads).reshape(
        4, 3 * local_width, tok_rows
    )
    grad_qkv_w = jnp.einsum(
        "jit,jtd->di",
        grad_qkv,
        normed_all.reshape(4, tok_rows, width),
        preferred_element_type=F32,
    )
    grad_attn_w = jnp.concatenate([grad_qkv_w, grad_out_w], axis=1).astype(BF16)
    fsdp = many * LOW
    grad_attn_own = jnp.sum(
        lax.all_to_all(
            grad_attn_w.reshape(fsdp, width // fsdp, 4 * local_width),
            ("hi", "lo"),
            0,
            0,
            tiled=True,
        ).astype(F32),
        axis=0,
    )
    grad_qkv_mine = lax.all_to_all(grad_qkv, ("y", "c"), 0, 0, tiled=True)
    grad_normed_one = jnp.einsum(
        "jit,jdi->td",
        grad_qkv_mine,
        attn_all[:, :, : 3 * local_width],
        preferred_element_type=F32,
    )
    _, norm_pull_one = jax.vjp(rms_norm, inputs, attn_gain)
    grad_input_part, grad_attn_gain = norm_pull_one(grad_normed_one)
    grad_inputs = grad_hidden + grad_input_part
    summed = lax.psum(
        (grad_attn_gain, grad_moe_gain, grad_router, grad_prior_w, grad_const, grad_vector),
        ("hi", "lo", "y", "c"),
    )
    return (
        output,
        grad_inputs,
        grad_prior,
        summed[0],
        grad_attn_own[:, :local_width],
        grad_attn_own[:, local_width : 2 * local_width],
        grad_attn_own[:, 2 * local_width : 3 * local_width],
        grad_attn_own[:, 3 * local_width :].T,
        summed[1],
        summed[2],
        summed[3],
        summed[4],
        summed[5],
        grad_gate_own,
        grad_up_own,
        grad_down_own,
    )


def solution(mesh):
    many = mesh.shape["fsdp"] // LOW
    fine = Mesh(mesh.devices.reshape(many, LOW, 2, 2), ("hi", "lo", "y", "c"))
    fsdp, tp = ("hi", "lo"), ("y", "c")
    every = fsdp + tp
    return jax.shard_map(
        functools.partial(per_device, many),
        mesh=fine,
        in_specs=(
            P(every, None),
            P(every, None),
            P(fsdp, None),
            P(fsdp, None),
            P(fsdp, None),
            P(fsdp, None),
            P(),
            P(fsdp, tp),
            P(fsdp, tp),
            P(fsdp, tp),
            P(tp, fsdp),
            P(),
            P(),
            P(),
            P(),
            P(),
            P(None, fsdp, tp),
            P(None, fsdp, tp),
            P(None, tp, fsdp),
        ),
        out_specs=(
            P(every, None),
            P(every, None),
            P(every, None),
            P(),
            P(fsdp, tp),
            P(fsdp, tp),
            P(fsdp, tp),
            P(tp, fsdp),
            P(),
            P(),
            P(),
            P(),
            P(),
            P(None, fsdp, tp),
            P(None, fsdp, tp),
            P(None, tp, fsdp),
        ),
        check_vma=False,
    )
```

time: 2170 us -> 829 us (0.38)
  waiting for transfers between devices: 1280 us -> 288 us
  matrix products: 413 us -> 110 us
  blocking collectives: 144 us -> 53.1 us
  local copies, waits for them, and re-layouts: 220 us -> 143 us
  starting transfers between devices: 1.36 us -> 56.2 us
  Pallas kernels: 0 us -> 50.5 us
  other arithmetic: 78 us -> 102 us
    reduce_scatter x10 -> x0, waiting for transfers between devices: 1040 us -> none  [the longest x1 212 us: per_device(): lax.psum_scatter(grad_down_w, 'fsdp', scatter_dimension=2, tiled=True)]
    dot_general x42 -> x25, matrix products: 398 us -> 99.6 us  [the longest x1 11 us: per_device(): gate_pre = jnp.dot(dispatched, gate_w, preferred_element_type=F32)]
    ppermute x0 -> x20, waiting for transfers between devices: none -> 232 us  [swap(): return lax.ppermute(value, axis, [(0, 1), (1, 0)])]
    all_gather x7 -> x2, waiting for transfers between devices: 223 us -> 45.4 us  [the longest x1 45.3 us: per_device(): attn_full = lax.all_gather(attn_weights, ('hi', 'lo'), axis=0, tiled=True)]
    gather x9 -> x1, local copies, waits for them, and re-layouts: 129 us -> 0.58 us  [per_device(): jnp.take(pair_slots.reshape(4, tok_rows, 2), relative, axis=0)]
    all_gather x4 -> x0, blocking collectives: 103 us -> none  [the longest x1 27.8 us: per_device(): lax.all_gather(w_out, 'fsdp', axis=1, tiled=True)]
    scatter x4 -> x0, local copies, waits for them, and re-layouts: 62.3 us -> none  [the longest x1 15.7 us: routing(): jnp.zeros((experts * capacity + 1,), jnp.int32).at[slot_ids.reshape(-1)]]
    pallas_call x0 -> x2, Pallas kernels: none -> 50.5 us  [the longest x1 31.3 us: attend_back(): pl.pallas_call(functools.partial(attend_back_kernel, block, MAXLEN), grid...]
  transfers between devices with their start and end apart: 19 -> 29, of which waited for: 16 -> 10; matrix products, arithmetic and copies ran while one was open for 12% -> 31% of each run, Pallas kernels for 0% -> 6%
where the time goes in v1:
time: 829 us; the launch traced here: 819 us
  waiting for transfers between devices  288 us (35%)
  local copies, waits for them, and re-layouts  143 us (17%)
  matrix products  110 us (13%)
  other arithmetic  102 us (12%)
  starting transfers between devices  56.2 us (7%)
  blocking collectives  53.1 us (6%)
  Pallas kernels  50.5 us (6%)
  between operations  16 us (2%)
    ppermute x20, waiting for transfers between devices, swap(): return lax.ppermute(value, axis, [(0, 1), (1, 0)])  232 us
    psum x1, blocking collectives, per_device(): lax.psum((grad_attn_gain, grad_moe_gain, grad_router, grad_prior_w, grad_...  53.1 us
    all_gather x1, waiting for transfers between devices, per_device(): attn_full = lax.all_gather(attn_weights, ('hi', 'lo'), axis=0, tiled=True)  45.3 us
    pallas_call x1, Pallas kernels, attend_back(): pl.pallas_call(functools.partial(attend_back_kernel, block, MAXLEN), grid...  31.3 us
    ppermute x20, starting transfers between devices, swap(): return lax.ppermute(value, axis, [(0, 1), (1, 0)])  24.5 us
    pallas_call x1, Pallas kernels, attend(): pl.pallas_call(functools.partial(attend_kernel, block, MAXLEN), grid=(hea...  19.2 us
    squeeze x3, local copies, waits for them, and re-layouts, per_device(): gate_w, up_w, down_w = (expert_all[0], expert_all[1], expert_all[2])  18.5 us
  transfers between devices with their start and end apart: 29, of which 10 were waited for; matrix products, arithmetic and copies ran while one was open for 31% of the time, Pallas kernels for 6%

profile of v1, /device:TPU:1, one launch (start us, length us, event | category | flops | bytes accessed | tf_op | source)
XLA Modules:
  0.0 818.8 jit_solution(5113778524712698277)
XLA Ops:
  13.1 5.4 all-to-all-start.2
  18.6 45.3 %all-gather.4.cloned.1.call-done = bf16[768,768]{1,0:T(8,128)(2,1)} async-done(((bf16[96,768]{1,0:T(8,128)(2,1)}), bf16[768,768]{1,0:T(8,128)(2,1)}) %all-gather.4.cloned.1.call-update) | async-done | bytes 1179664 | tf_op jit(solution)/shard_map/all_gather | solution.py:288
  72.2 17.7 %collective-permute-done = bf16[512,768]{1,0:T(8,128)(2,1)} collective-permute-done((bf16[512,768]{1,0:T(8,128)(2,1)}, bf16[512,768]{1,0:T(8,128)(2,1)}, u32[]{:S(2)}, u32[]{:S(2)}) %collective-permute-start) | collective-permute-done | bytes 786464 | tf_op jit(solution)/shard_map/ppermute | solution.py:26
  89.8 9.3 %collective-permute-start.1 = (bf16[512,768]{1,0:T(8,128)(2,1)}, bf16[512,768]{1,0:T(8,128)(2,1)}, u32[]{:S(2)}, u32[]{:S(2)}) collective-permute-start(bf16[512,768]{1,0:T(8,128)(2,1)} %collective-permute-done), channel_id=1, source_target_pairs={{0,1},{1,0},{2,3},{3,2},{4,5},{5,4},{6,7},{7,6},{8,9},{9,8},{10,11... | collective-permute-start | bytes 2359304 | tf_op jit(solution)/shard_map/ppermute | solution.py:26
  99.2 8.3 %convert_reduce_fusion = s32[4096]{0:T(1024)S(1)} fusion(s32[4096]{0:T(1024)S(1)} %multiply_add_fusion.2), kind=kLoop, calls=%fused_computation.1 | loop fusion | flops 50327552 | bytes 32768 | tf_op jit(solution)/shard_map/reduce_sum | solution.py:200
  114.1 19.2 %attend.1 = (bf16[4,192,512]{2,1,0:T(8,128)(2,1)}, f32[3,1,2048]{2,1,0:T(1,128)S(1)}) custom-call(bf16[576,2048]{1,0:T(8,128)(2,1)S(1)} %convolution_convert_fusion.q_ref.k_ref.v_ref, bf16[576,2048]{1,0:T(8,128)(2,1)S(1)} %convolution_convert_fusion.q_ref.k_ref.v_ref, bf16[576,2048]{1,0:T(8,128)(2,1)S(1)} %convolution_convert_fusion.q_ref.k_ref.v_ref, ...), custom_call_target="tpu_custom_call" | custom-call | tf_op jit(solution)/shard_map/attend/pallas_call | solution.py:92
  138.7 65.2 %collective-permute-done.9 = bf16[8,3,96,512]{3,2,1,0:T(8,128)(2,1)} collective-permute-done((bf16[8,3,96,512]{3,2,1,0:T(8,128)(2,1)}, bf16[8,3,96,512]{3,2,1,0:T(8,128)(2,1)}, u32[]{:S(2)}, u32[]{:S(2)}) %collective-permute-start.9) | collective-permute-done | bytes 2359328 | tf_op jit(solution)/shard_map/ppermute | solution.py:26
  203.9 5.0 pad_maximum_fusion.1
  223.7 16.3 %collective-permute-done.4 = bf16[512,896]{1,0:T(8,128)(2,1)} collective-permute-done((bf16[512,896]{1,0:T(8,128)(2,1)}, bf16[512,896]{1,0:T(8,128)(2,1)}, u32[]{:S(2)}, u32[]{:S(2)}) %collective-permute-start.4) | collective-permute-done | bytes 917536 | tf_op jit(solution)/shard_map/ppermute | solution.py:26
  241.5 5.5 copy.251
  247.1 5.5 copy.252
  260.9 6.6 multiply_convert_fusion.6
  269.1 4.7 all-to-all-start.1
  273.8 9.4 %copy.253 = bf16[1,2,4,2,3,96,512]{6,3,0,5,2,1,4:T(2,128)(2,1)} copy(bf16[1,2,4,2,3,96,512]{6,5,4,3,2,1,0:T(8,128)(2,1)} %bitcast.26) | data formatting | bytes 9437184 | tf_op jit(solution)/shard_map/stack | solution.py:297
  283.2 15.7 %maximum_bitcast_fusion = bf16[3,2,4,96,2,2,512]{6,5,4,3,2,1,0:T(2,128)(2,1)S(1)} fusion(bf16[1,2,4,2,3,96,512]{6,3,0,5,2,1,4:T(2,128)(2,1)} %copy.253, bf16[1,1,4,2,3,96,512]{6,3,0,5,2,1,4:T(2,128)(2,1)} %copy.252, bf16[1,1,4,2,3,96,512]{6,3,0,5,2,1,4:T(2,128)(2,1)} %copy.251), kind=kLoop, calls=%fused_computation.6 | loop fusion | flops 9437184 | bytes 18874368 | tf_op jit(solution)/shard_map/transpose | solution.py:300
  298.8 9.4 %fusion.140 = (bf16[1,2,4,96,2,2,512]{6,5,4,3,2,1,0:T(2,128)(2,1)}, bf16[1,2,4,96,2,2,512]{6,5,4,3,2,1,0:T(2,128)(2,1)}, bf16[1,2,4,96,2,2,512]{6,5,4,3,2,1,0:T(2,128)(2,1)}) fusion(bf16[3,2,4,96,2,2,512]{6,5,4,3,2,1,0:T(2,128)(2,1)S(1)} %maximum_bitcast_fusion), kind=kLoop, calls=%fused_computation.297 | loop fusion | bytes 18874368 | tf_op jit(solution)/shard_map/slice | solution.py:378
  308.2 6.1 squeeze.49
  314.4 6.2 squeeze.50
  320.6 6.1 squeeze.48
  326.7 6.0 reshape.402
  332.7 7.0 copy.250
  351.3 11.0 %fusion.6 = (bf16[2048,768]{0,1:T(8,128)(2,1)}, bf16[2048,768]{0,1:T(8,128)(2,1)}, bf16[2048,768]{0,1:T(8,128)(2,1)}, f32[768,2048]{1,0:T(8,128)}) fusion(f32[768,2048]{1,0:T(8,128)} %fusion.73, f32[768,2048]{1,0:T(8,128)S(1)} %fusion.71, bf16[768,2048]{1,0:T(8,128)(2,1)S(1)} %copy-done.25, bf16[768,2,768]{0,2,1:T(8,128)(2,1)S(1)} %maximum_select_fusion), kind=kOutput, calls=%fused_computation.16 | convolution fusion | flops 2441084928 | bytes 32636928 | tf_op jit(solution)/shard_map/dot_general | solution.py:381
  362.3 5.8 fusion.37
  368.1 5.8 fusion.51
  373.9 8.0 add_bitcast_fusion
  384.4 6.9 copy.254
  391.3 6.3 select_n.221
  397.6 5.0 all-to-all-start.3
  408.6 4.7 copy.291
  413.2 4.6 copy.290
  417.9 4.7 copy.289
  434.6 6.7 fusion.151
  449.2 4.9 fusion.152
  462.9 8.1 pad_maximum_fusion
  474.2 6.6 fusion.13
  483.3 8.5 %collective-permute-done.12 = bf16[512,768]{1,0:T(8,128)(2,1)S(1)} collective-permute-done((bf16[512,768]{1,0:T(8,128)(2,1)S(1)}, bf16[512,768]{1,0:T(8,128)(2,1)S(1)}, u32[]{:S(2)}, u32[]{:S(2)}) %collective-permute-start.12) | collective-permute-done | bytes 786464 | tf_op jit(solution)/shard_map/ppermute | solution.py:26
  491.9 5.2 multiply_reduce_fusion.8
  503.8 7.7 collective-permute-done.14
  524.0 15.2 %collective-permute-done.15 = bf16[512,768]{1,0:T(8,128)(2,1)S(1)} collective-permute-done((bf16[512,768]{1,0:T(8,128)(2,1)}, bf16[512,768]{1,0:T(8,128)(2,1)S(1)}, u32[]{:S(2)}, u32[]{:S(2)}) %collective-permute-start.15) | collective-permute-done | bytes 786464 | tf_op jit(solution)/shard_map/ppermute | solution.py:26
  541.5 4.7 copy.270
  552.7 31.3 %attend_back.1 = bf16[4,3,192,512]{3,2,1,0:T(8,128)(2,1)} custom-call(bf16[576,2048]{1,0:T(8,128)(2,1)S(1)} %copy-done.2, bf16[576,2048]{1,0:T(8,128)(2,1)S(1)} %copy-done.2, bf16[576,2048]{1,0:T(8,128)(2,1)S(1)} %copy-done.2, bf16[192,2048]{1,0:T(8,128)(2,1)S(1)} %convolution_convert_fusion.1.g_ref, s32[1,2048]{1,0:T(1,128)S(1)} %bitcast.285, ...), custom_call_target="tpu_custom_call" | custom-call | tf_op jit(solution)/shard_map/attend_back/pallas_call | solution.py:169
  584.0 4.8 all-to-all-start.4
  588.7 11.1 %fusion = f32[3,2,4,96,2,512]{5,3,4,2,1,0:T(8,128)} fusion(f32[3,2,4,96,2,2,512]{6,3,5,4,2,1,0:T(8,128)} %pad_maximum_fusion, bf16[3,2,4,96,2,512]{5,3,4,2,1,0:T(8,128)(2,1)} %collective-permute-done.18), kind=kLoop, calls=%fused_computation.5 | loop fusion | flops 4718592 | bytes 23592960 | tf_op jit(solution)/shard_map/add | solution.py:401
  606.2 5.2 bitcast_convert_fusion
  620.0 101.4 %collective-permute-done.19 = bf16[3,4,96,2,512]{4,2,3,1,0:T(8,128)(2,1)} collective-permute-done((bf16[3,4,96,2,512]{4,2,3,1,0:T(8,128)(2,1)}, bf16[3,4,96,2,512]{4,2,3,1,0:T(8,128)(2,1)}, u32[]{:S(2)}, u32[]{:S(2)}) %collective-permute-start.19) | collective-permute-done | bytes 2359328 | tf_op jit(solution)/shard_map/ppermute | solution.py:26
  727.1 6.8 all-to-all-done.5
  742.4 6.5 fusion.61
  749.0 53.1 %all-reduce.13 = (f32[768]{0:T(1024)}, f32[768]{0:T(1024)}, f32[768,12]{0,1:T(8,128)}, f32[12,12]{1,0:T(8,128)}, f32[2,768,2]{1,2,0:T(2,128)}, /*index=5*/f32[2,768]{1,0:T(2,128)}) all-reduce(f32[768]{0:T(1024)S(1)} %get-tuple-element.123, ...), channel_id=1, replica_groups=mesh['hi'=2,'lo'=4,'y'=2,'c'=2] {'hi','lo','y','c'}, use_global_device_ids=true, to_apply=%region_32.33 | all-reduce | flops 15504 | bytes 124032 | tf_op jit(solution)/shard_map/psum | solution.py:491
  (349 shorter events, 172.3 us)
Async XLA Ops:
  7.2 130.2 %copy-start = (f32[2048,12]{0,1:T(8,128)S(1)}, f32[2048,12]{0,1:T(8,128)}, u32[]{:S(2)}) copy-start(f32[2048,12]{0,1:T(8,128)} %param.24) | copy-start | bytes 294916
  7.2 56.7 %all-gather.4.cloned.1.call-start = ((), (), s32[]{:S(2)}) async-start(), calls=%async_computation.7 | async-start | bytes 1327104 | tf_op jit(solution)/shard_map/all_gather | solution.py:288
  13.1 50.9 %copy-start.5 = (f32[512,768]{1,0:T(8,128)S(1)}, f32[512,768]{1,0:T(8,128)}, u32[]{:S(2)}) copy-start(f32[512,768]{1,0:T(8,128)} %param.19) | copy-start | bytes 4718596
  13.1 86.1 %all-to-all-start.2 = ((bf16[8,3,96,512]{3,2,1,0:T(8,128)(2,1)}), bf16[8,3,96,512]{3,2,1,0:T(8,128)(2,1)}, u32[]{:S(2)}, u32[]{:S(2)}) async-start(bf16[8,3,96,512]{3,2,1,0:T(8,128)(2,1)} %pad_maximum_fusion.5), calls=%async_computation.2 | async-start | bytes 4718592 | tf_op jit(solution)/shard_map/all_to_all | solution.py:292
  18.5 45.6 %copy-start.47 = (f32[768]{0:T(1024)S(1)}, f32[768]{0:T(1024)}, u32[]{:S(2)}) copy-start(f32[768]{0:T(1024)} %param.25) | copy-start | bytes 9220
  18.5 191.1 %all-gather.6.cloned.1.call-start = ((), (), s32[]{:S(2)}) async-start(), calls=%async_computation.8 | async-start | bytes 5898240 | tf_op jit(solution)/shard_map/all_gather | solution.py:301
  64.2 43.4 %copy-start.51 = (f32[512]{0:T(512)}, f32[512]{0:T(512)S(1)}, u32[]{:S(2)}) copy-start(f32[512]{0:T(512)S(1)} %fusion.115) | copy-start | bytes 6148
  65.3 24.6 %collective-permute-start = (bf16[512,768]{1,0:T(8,128)(2,1)}, bf16[512,768]{1,0:T(8,128)(2,1)}, u32[]{:S(2)}, u32[]{:S(2)}) collective-permute-start(bf16[512,768]{1,0:T(8,128)(2,1)} %multiply_convert_fusion.11), channel_id=1, source_target_pairs={{0,2},{2,0},{1,3},{3,1},{4,6},{6,4},{5,7},{7,5},{8,10},{10,8},{9,1... | collective-permute-start | bytes 2359304 | tf_op jit(solution)/shard_map/ppermute | solution.py:26
  65.8 41.7 %collective-permute-start.2 = (bf16[512,768]{1,0:T(8,128)(2,1)}, bf16[512,768]{1,0:T(8,128)(2,1)}, u32[]{:S(2)}, u32[]{:S(2)}) collective-permute-start(bf16[512,768]{1,0:T(8,128)(2,1)} %multiply_convert_fusion.11), channel_id=1, source_target_pairs={{0,1},{1,0},{2,3},{3,2},{4,5},{5,4},{6,7},{7,6},{8,9},{9,8},{10,11... | collective-permute-start | bytes 2359304 | tf_op jit(solution)/shard_map/ppermute | solution.py:26
  69.5 172.0 %collective-permute-start.7 = (bf16[512,768]{1,0:T(8,128)(2,1)}, bf16[512,768]{1,0:T(8,128)(2,1)}, u32[]{:S(2)}, u32[]{:S(2)}) collective-permute-start(bf16[512,768]{1,0:T(8,128)(2,1)} %fusion.135), channel_id=1, source_target_pairs={{0,2},{2,0},{1,3},{3,1},{4,6},{6,4},{5,7},{7,5},{8,10},{10,8},{9,1... | collective-permute-start | bytes 2359304 | tf_op jit(solution)/shard_map/ppermute | solution.py:26
  70.2 190.7 %collective-permute-start.6 = (bf16[512,768]{1,0:T(8,128)(2,1)}, bf16[512,768]{1,0:T(8,128)(2,1)}, u32[]{:S(2)}, u32[]{:S(2)}) collective-permute-start(bf16[512,768]{1,0:T(8,128)(2,1)} %fusion.135), channel_id=1, source_target_pairs={{0,1},{1,0},{2,3},{3,2},{4,5},{5,4},{6,7},{7,6},{8,9},{9,8},{10,11... | collective-permute-start | bytes 2359304 | tf_op jit(solution)/shard_map/ppermute | solution.py:26
  89.8 17.7 %collective-permute-start.1 = (bf16[512,768]{1,0:T(8,128)(2,1)}, bf16[512,768]{1,0:T(8,128)(2,1)}, u32[]{:S(2)}, u32[]{:S(2)}) collective-permute-start(bf16[512,768]{1,0:T(8,128)(2,1)} %collective-permute-done), channel_id=1, source_target_pairs={{0,1},{1,0},{2,3},{3,2},{4,5},{5,4},{6,7},{7,6},{8,9},{9,8},{10,11... | collective-permute-start | bytes 2359304 | tf_op jit(solution)/shard_map/ppermute | solution.py:26
  99.2 104.7 %collective-permute-start.9 = (bf16[8,3,96,512]{3,2,1,0:T(8,128)(2,1)}, bf16[8,3,96,512]{3,2,1,0:T(8,128)(2,1)}, u32[]{:S(2)}, u32[]{:S(2)}) collective-permute-start(bf16[8,3,96,512]{3,2,1,0:T(8,128)(2,1)} %all-to-all-done.2), channel_id=1, source_target_pairs={{0,16},{16,0},{1,17},{17,1},{2,18},{18,2},{3,19},{19,3},{4,20},{20... | collective-permute-start | bytes 7077896 | tf_op jit(solution)/shard_map/ppermute | solution.py:26
  114.1 19.2 %copy-start.1 = (bf16[576,2048]{1,0:T(8,128)(2,1)}, bf16[576,2048]{1,0:T(8,128)(2,1)S(1)}, u32[]{:S(2)}) copy-start(bf16[576,2048]{1,0:T(8,128)(2,1)S(1)} %convolution_convert_fusion.q_ref.k_ref.v_ref) | copy-start | bytes 7077892
  114.1 23.3 %copy-start.49 = (f32[12,12]{1,0:T(8,128)S(1)}, f32[12,12]{1,0:T(8,128)}, u32[]{:S(2)}) copy-start(f32[12,12]{1,0:T(8,128)} %param.32) | copy-start | bytes 1732
  133.3 76.3 %all-to-all-start = ((bf16[4,192,512]{2,1,0:T(8,128)(2,1)}), bf16[4,192,512]{2,1,0:T(8,128)(2,1)S(1)}, u32[]{:S(2)}, u32[]{:S(2)}) async-start(bf16[4,192,512]{2,1,0:T(8,128)(2,1)} %get-tuple-element.18), calls=%async_computation | async-start | bytes 1572864 | tf_op jit(solution)/shard_map/all_to_all | solution.py:335
  208.9 64.9 %collective-permute-start.10 = (bf16[2,8,3,96,512]{4,3,2,1,0:T(8,128)(2,1)}, bf16[2,8,3,96,512]{4,3,2,1,0:T(8,128)(2,1)}, u32[]{:S(2)}, u32[]{:S(2)}) collective-permute-start(bf16[2,8,3,96,512]{4,3,2,1,0:T(8,128)(2,1)} %pad_maximum_fusion.1), channel_id=1, source_target_pairs={{0,1},{1,0},{2,3},{3,2},{4,5},{5,4},{6,7},{7,6},{8,9},{9,8},{10,11... | collective-permute-start | bytes 14155784 | tf_op jit(solution)/shard_map/ppermute | solution.py:26
  214.8 39.8 %copy-start.11 = (bf16[512,768]{1,0:T(8,128)(2,1)}, bf16[512,768]{1,0:T(8,128)(2,1)S(1)}, u32[]{:S(2)}) copy-start(bf16[512,768]{1,0:T(8,128)(2,1)S(1)} %fusion.134) | copy-start | bytes 2359300
  217.7 23.1 %copy-start.73 = (f32[2,768]{1,0:T(2,128)S(1)}, f32[2,768]{1,0:T(2,128)}, u32[]{:S(2)}) copy-start(f32[2,768]{1,0:T(2,128)} %param.34) | copy-start | bytes 18436
  217.7 22.3 %collective-permute-start.4 = (bf16[512,896]{1,0:T(8,128)(2,1)}, bf16[512,896]{1,0:T(8,128)(2,1)}, u32[]{:S(2)}, u32[]{:S(2)}) collective-permute-start(bf16[512,896]{1,0:T(8,128)(2,1)} %pad_maximum_fusion.9), channel_id=1, source_target_pairs={{0,2},{2,0},{1,3},{3,1},{4,6},{6,4},{5,7},{7,5},{8,10},{10,8},{9,1... | collective-permute-start | bytes 2752520 | tf_op jit(solution)/shard_map/ppermute | solution.py:26
  223.3 181.0 %copy-start.74 = (pred[512]{0:T(512)(128)(4,1)}, pred[512]{0:T(512)(128)(4,1)S(1)}, u32[]{:S(2)}) copy-start(pred[512]{0:T(512)(128)(4,1)S(1)} %get-tuple-element.133) | copy-start | bytes 1540
  223.3 181.0 %copy-start.76 = (pred[512]{0:T(512)(128)(4,1)}, pred[512]{0:T(512)(128)(4,1)S(1)}, u32[]{:S(2)}) copy-start(pred[512]{0:T(512)(128)(4,1)S(1)} %get-tuple-element.134) | copy-start | bytes 1540
  223.3 181.0 %copy-start.78 = (pred[512]{0:T(512)(128)(4,1)}, pred[512]{0:T(512)(128)(4,1)S(1)}, u32[]{:S(2)}) copy-start(pred[512]{0:T(512)(128)(4,1)S(1)} %get-tuple-element.132) | copy-start | bytes 1540
  223.3 31.3 %collective-permute-start.3 = (bf16[512,896]{1,0:T(8,128)(2,1)}, bf16[512,896]{1,0:T(8,128)(2,1)S(1)}, u32[]{:S(2)}, u32[]{:S(2)}) collective-permute-start(bf16[512,896]{1,0:T(8,128)(2,1)} %pad_maximum_fusion.9), channel_id=1, source_target_pairs={{0,1},{1,0},{2,3},{3,2},{4,5},{5,4},{6,7},{7,6},{8,9},{9,8},{10,11... | collective-permute-start | bytes 2752520 | tf_op jit(solution)/shard_map/ppermute | solution.py:26
  240.0 14.6 %collective-permute-start.5 = (bf16[512,896]{1,0:T(8,128)(2,1)}, bf16[512,896]{1,0:T(8,128)(2,1)S(1)}, u32[]{:S(2)}, u32[]{:S(2)}) collective-permute-start(bf16[512,896]{1,0:T(8,128)(2,1)} %collective-permute-done.4), channel_id=1, source_target_pairs={{0,1},{1,0},{2,3},{3,2},{4,5},{5,4},{6,7},{7,6},{8,9},{9,8},{10,11... | collective-permute-start | bytes 2752520 | tf_op jit(solution)/shard_map/ppermute | solution.py:26
  241.4 193.2 %copy-start.70 = (s32[2048,1]{0,1:T(1,128)}, s32[2048,1]{0,1:T(1,128)S(1)}, u32[]{:S(2)}) copy-start(s32[2048,1]{0,1:T(1,128)S(1)} %get-tuple-element.187) | copy-start | bytes 24580
  241.4 193.2 %copy-start.71 = (s32[2048,1]{0,1:T(1,128)}, s32[2048,1]{0,1:T(1,128)S(1)}, u32[]{:S(2)}) copy-start(s32[2048,1]{0,1:T(1,128)S(1)} %get-tuple-element.188) | copy-start | bytes 24580
  241.5 19.4 %collective-permute-start.8 = (bf16[512,768]{1,0:T(8,128)(2,1)}, bf16[512,768]{1,0:T(8,128)(2,1)}, u32[]{:S(2)}, u32[]{:S(2)}) collective-permute-start(bf16[512,768]{1,0:T(8,128)(2,1)} %collective-permute-done.7), channel_id=1, source_target_pairs={{0,1},{1,0},{2,3},{3,2},{4,5},{5,4},{6,7},{7,6},{8,9},{9,8},{10,11... | collective-permute-start | bytes 2359304 | tf_op jit(solution)/shard_map/ppermute | solution.py:26
  269.1 57.6 %all-to-all-start.1 = ((bf16[4,192,1536]{2,1,0:T(8,128)(2,1)}), bf16[4,192,1536]{2,1,0:T(8,128)(2,1)}, u32[]{:S(2)}, u32[]{:S(2)}) async-start(bf16[4,192,1536]{2,1,0:T(8,128)(2,1)} %bitcast.288), calls=%async_computation.1 | async-start | bytes 4718592 | tf_op jit(solution)/shard_map/all_to_all | solution.py:373
  397.6 37.0 %all-to-all-start.3 = ((bf16[4,192,1536]{2,1,0:T(8,128)(2,1)}), bf16[4,192,1536]{2,1,0:T(8,128)(2,1)}, u32[]{:S(2)}, u32[]{:S(2)}) async-start(bf16[4,192,1536]{2,1,0:T(8,128)(2,1)} %select_n.221), calls=%async_computation.3 | async-start | bytes 4718592 | tf_op jit(solution)/shard_map/all_to_all | solution.py:420
  445.1 25.9 %collective-permute-start.11 = (bf16[2,512,768]{2,1,0:T(8,128)(2,1)}, bf16[2,512,768]{2,1,0:T(8,128)(2,1)S(1)}, u32[]{:S(2)}, u32[]{:S(2)}) collective-permute-start(bf16[2,512,768]{2,1,0:T(8,128)(2,1)} %pad_maximum_fusion.7), channel_id=1, source_target_pairs={{0,1},{1,0},{2,3},{3,2},{4,5},{5,4},{6,7},{7,6},{8,9},{9,8},{10,11... | collective-permute-start | bytes 4718600 | tf_op jit(solution)/shard_map/ppermute | solution.py:26
  454.1 27.7 %copy-start.31 = (f32[2048,896]{1,0:T(8,128)}, f32[2048,896]{1,0:T(8,128)S(1)}, u32[]{:S(2)}) copy-start(f32[2048,896]{1,0:T(8,128)S(1)} %get-tuple-element.208) | copy-start | bytes 22020100
  454.5 27.3 %collective-permute-start.13 = (bf16[2,512,896]{2,1,0:T(8,128)(2,1)S(1)}, bf16[2,512,896]{2,1,0:T(8,128)(2,1)S(1)}, u32[]{:S(2)}, u32[]{:S(2)}) collective-permute-start(bf16[2,512,896]{2,1,0:T(8,128)(2,1)S(1)} %pad_maximum_fusion.6), channel_id=1, source_target_pairs={{0,1},{1,0},{2,3},{3,2},{4,5},{5,4},{6,7},{7,6},{8,9},{9,8},{10,11... | collective-permute-start | bytes 5505032 | tf_op jit(solution)/shard_map/ppermute | solution.py:26
  473.1 18.7 %collective-permute-start.12 = (bf16[512,768]{1,0:T(8,128)(2,1)S(1)}, bf16[512,768]{1,0:T(8,128)(2,1)S(1)}, u32[]{:S(2)}, u32[]{:S(2)}) collective-permute-start(bf16[512,768]{1,0:T(8,128)(2,1)S(1)} %fusion.54), channel_id=1, source_target_pairs={{0,2},{2,0},{1,3},{3,1},{4,6},{6,4},{5,7},{7,5},{8,10},{10,8},{9,1... | collective-permute-start | bytes 2359304 | tf_op jit(solution)/shard_map/ppermute | solution.py:26
  480.9 10.9 %copy-start.55 = (f32[512]{0:T(512)S(1)}, f32[512]{0:T(512)}, u32[]{:S(2)}) copy-start(f32[512]{0:T(512)} %get-tuple-element.130) | copy-start | bytes 6148
  480.9 107.8 %collective-permute-start.18 = (bf16[3,2,4,96,2,512]{5,3,4,2,1,0:T(8,128)(2,1)}, bf16[3,2,4,96,2,512]{5,3,4,2,1,0:T(8,128)(2,1)}, u32[]{:S(2)}, u32[]{:S(2)}) collective-permute-start(bf16[3,2,4,96,2,512]{5,3,4,2,1,0:T(8,128)(2,1)} %fusion.13), channel_id=1, source_target_pairs={{0,1},{1,0},{2,3},{3,2},{4,5},{5,4},{6,7},{7,6},{8,9},{9,8},{10,11... | collective-permute-start | bytes 14155784 | tf_op jit(solution)/shard_map/ppermute | solution.py:26
  481.8 15.3 %copy-start.32 = (bf16[2,512,896]{2,1,0:T(8,128)(2,1)}, bf16[2,512,896]{2,1,0:T(8,128)(2,1)S(1)}, u32[]{:S(2)}) copy-start(bf16[2,512,896]{2,1,0:T(8,128)(2,1)S(1)} %collective-permute-done.13) | copy-start | bytes 5505028
  482.9 28.7 %collective-permute-start.14 = (bf16[512,896]{1,0:T(8,128)(2,1)}, bf16[512,896]{1,0:T(8,128)(2,1)}, u32[]{:S(2)}, u32[]{:S(2)}) collective-permute-start(bf16[512,896]{1,0:T(8,128)(2,1)} %fusion.49), channel_id=1, source_target_pairs={{0,2},{2,0},{1,3},{3,1},{4,6},{6,4},{5,7},{7,5},{8,10},{10,8},{9,1... | collective-permute-start | bytes 2752520 | tf_op jit(solution)/shard_map/ppermute | solution.py:26
  499.8 11.8 %copy-start.33 = (bf16[2,512,896]{2,1,0:T(8,128)(2,1)S(1)}, bf16[2,512,896]{2,1,0:T(8,128)(2,1)}, u32[]{:S(2)}) copy-start(bf16[2,512,896]{2,1,0:T(8,128)(2,1)} %copy-done.32) | copy-start | bytes 5505028
  521.3 17.9 %collective-permute-start.15 = (bf16[512,768]{1,0:T(8,128)(2,1)}, bf16[512,768]{1,0:T(8,128)(2,1)S(1)}, u32[]{:S(2)}, u32[]{:S(2)}) collective-permute-start(bf16[512,768]{1,0:T(8,128)(2,1)} %get-tuple-element.145), channel_id=1, source_target_pairs={{0,2},{2,0},{1,3},{3,1},{4,6},{6,4},{5,7},{7,5},{8,10},{10,8},{9,1... | collective-permute-start | bytes 2359304 | tf_op jit(solution)/shard_map/ppermute | solution.py:26
  522.4 23.8 %collective-permute-start.17 = (bf16[512,768]{1,0:T(8,128)(2,1)}, bf16[512,768]{1,0:T(8,128)(2,1)S(1)}, u32[]{:S(2)}, u32[]{:S(2)}) collective-permute-start(bf16[512,768]{1,0:T(8,128)(2,1)} %get-tuple-element.145), channel_id=1, source_target_pairs={{0,1},{1,0},{2,3},{3,2},{4,5},{5,4},{6,7},{7,6},{8,9},{9,8},{10,11... | collective-permute-start | bytes 2359304 | tf_op jit(solution)/shard_map/ppermute | solution.py:26
  539.2 7.0 collective-permute-start.16
  584.0 32.5 %all-to-all-start.4 = ((bf16[4,576,512]{2,1,0:T(8,128)(2,1)}), bf16[4,576,512]{2,1,0:T(8,128)(2,1)}, u32[]{:S(2)}, u32[]{:S(2)}) async-start(bf16[4,576,512]{2,1,0:T(8,128)(2,1)} %bitcast.58), calls=%async_computation.4 | async-start | bytes 4718592 | tf_op jit(solution)/shard_map/all_to_all | solution.py:481
  604.1 117.3 %collective-permute-start.19 = (bf16[3,4,96,2,512]{4,2,3,1,0:T(8,128)(2,1)}, bf16[3,4,96,2,512]{4,2,3,1,0:T(8,128)(2,1)}, u32[]{:S(2)}, u32[]{:S(2)}) collective-permute-start(bf16[3,4,96,2,512]{4,2,3,1,0:T(8,128)(2,1)} %fusion.42), channel_id=1, source_target_pairs={{0,16},{16,0},{1,17},{17,1},{2,18},{18,2},{3,19},{19,3},{4,20},{20... | collective-permute-start | bytes 7077896 | tf_op jit(solution)/shard_map/ppermute | solution.py:26
  616.4 117.5 %all-to-all-start.5 = ((bf16[8,96,768]{2,1,0:T(8,128)(2,1)}), bf16[8,96,768]{2,1,0:T(8,128)(2,1)S(1)}, u32[]{:S(2)}, u32[]{:S(2)}) async-start(bf16[8,96,768]{2,1,0:T(8,128)(2,1)} %pad_maximum_fusion.8), calls=%async_computation.5 | async-start | bytes 2359296 | tf_op jit(solution)/shard_map/all_to_all | solution.py:472
  733.9 72.9 %all-to-all-start.6 = ((bf16[8,3,96,512]{3,2,1,0:T(8,128)(2,1)}), bf16[8,3,96,512]{3,2,1,0:T(8,128)(2,1)}, u32[]{:S(2)}, u32[]{:S(2)}) async-start(bf16[8,3,96,512]{3,2,1,0:T(8,128)(2,1)} %copy.277), calls=%async_computation.6 | async-start | bytes 4718592 | tf_op jit(solution)/shard_map/all_to_all | solution.py:409
  742.4 59.6 %copy-start.60 = (f32[512]{0:T(512)S(1)}, f32[512]{0:T(512)}, u32[]{:S(2)}) copy-start(f32[512]{0:T(512)} %copy-done.59) | copy-start | bytes 6148
  742.4 59.7 %copy-start.20 = (f32[512,768]{1,0:T(8,128)S(1)}, f32[512,768]{1,0:T(8,128)}, u32[]{:S(2)}) copy-start(f32[512,768]{1,0:T(8,128)} %get-tuple-element.146) | copy-start | bytes 4718596
  (66 other events, 357.1 us)
Sparse Core Ops, SparseCore 0:
  10.8 53.0 all-gather.3
  65.5 61.9 all-gather.5

commit v2 on v1

v2 whole, which is shorter than its diff:
```python
import functools

import jax
import jax.numpy as jnp
from jax import lax
from jax.experimental import pallas as pl
from jax.experimental.pallas import tpu as pltpu
from jax.sharding import Mesh
from jax.sharding import PartitionSpec as P

HEAD = 64
MAXLEN = 768
LOW = 4
SHARDS = 8
BOUNDS = 4
EPSILON = 1e-06
PRECISE = lax.Precision.HIGHEST
NEGATIVE = -1e30
F32 = jnp.float32
BF16 = jnp.bfloat16


def rms_norm(values, gain):
    return values * lax.rsqrt(jnp.mean(values * values, axis=-1, keepdims=True) + EPSILON) * gain


def swap(value, axis):
    return lax.ppermute(value, axis, [(0, 1), (1, 0)])


def gather_pieces(value):
    other = swap(value, "y")
    return [value, swap(value, "c"), other, swap(other, "c")]


def natural(pieces, index):
    ordered = []
    for j in range(4):
        item = pieces[j]
        for t in range(1, 4):
            item = jnp.where(index == t, pieces[j ^ t], item)
        ordered.append(item)
    return jnp.stack(ordered)


def add_core(near, sent):
    got = swap(sent, "c").astype(F32)
    return near[0] + got[0], (near[1] + got[1]).astype(BF16)


def cost_of(microseconds):
    return pl.CostEstimate(
        flops=int(microseconds * 1.15e9), transcendentals=0, bytes_accessed=2**20
    )


def scores_mask(first_key, first_query, window, block, scalars):
    row = first_query + lax.broadcasted_iota(jnp.int32, (1, block), 1)
    start_row = jnp.zeros_like(row)
    for k in range(BOUNDS, scalars.shape[0]):
        start_row = jnp.where(row >= scalars[k], scalars[k], start_row)
    key_places = first_key + lax.broadcasted_iota(jnp.int32, (window, block), 0)
    query_places = first_query + lax.broadcasted_iota(jnp.int32, (window, block), 1)
    return (key_places >= start_row) & (key_places <= query_places)


def attend_kernel(block, pad, scalars, *refs):
    pieces, refs = refs[:4], refs[4:]
    shards, refs = refs[:SHARDS], refs[SHARDS:]
    out_ref, lse_ref, qkv_ref, weight_ref, last_ref, key_rows, value_pad, full = refs
    group = qkv_ref.shape[1]
    window = pad + block
    quarter = group // 4
    inner = qkv_ref.shape[0] // 3
    head = pl.program_id(0)

    @pl.when(head == 0)
    def _():
        rows = shards[0].shape[0]
        for r in range(SHARDS):
            place = pl.multiple_of((scalars[0] ^ r) * rows, rows)
            full[pl.ds(place, rows), :] = shards[r][...]
        weight_ref[...] = full[:, : 3 * inner]
        last_ref[...] = full[:, 3 * inner :]
        turned = full[:, : 3 * inner].T
        for r in range(4):
            place = pl.multiple_of((scalars[1] ^ r) * quarter, quarter)
            qkv_ref[:, pl.ds(place, quarter)] = lax.dot_general(
                turned, pieces[r][...], (((1,), (1,)), ((), ())), preferred_element_type=F32
            ).astype(BF16)

    first_row = pl.multiple_of(head * HEAD, HEAD)
    key_rows[pl.ds(0, pad), :] = jnp.zeros((pad, HEAD), BF16)
    value_pad[:, pl.ds(0, pad)] = jnp.zeros((HEAD, pad), BF16)
    key_rows[pl.ds(pad, group), :] = qkv_ref[pl.ds(inner + first_row, HEAD), :].T
    value_pad[:, pl.ds(pad, group)] = qkv_ref[pl.ds(2 * inner + first_row, HEAD), :]

    def one(i, carry):
        first = pl.multiple_of(i * block, block)
        scores = jnp.dot(
            key_rows[pl.ds(first, window), :],
            qkv_ref[pl.ds(first_row, HEAD), pl.ds(first, block)],
            preferred_element_type=F32,
        )
        allowed = scores_mask(first - pad, first, window, block, scalars)
        scores = jnp.where(allowed, scores * 0.125, NEGATIVE)
        highest = jnp.max(scores, axis=0, keepdims=True)
        weights = jnp.exp(scores - highest)
        total = jnp.sum(weights, axis=0, keepdims=True)
        mixed = jnp.dot(
            value_pad[:, pl.ds(first, window)], weights.astype(BF16), preferred_element_type=F32
        )
        mixed = (mixed / total).astype(BF16)
        out_ref[first // quarter, :, pl.ds(pl.multiple_of(first % quarter, block), block)] = mixed
        lse_ref[0, :, pl.ds(first, block)] = highest + jnp.log(total)
        return carry

    lax.fori_loop(0, group // block, one, 0)


def attend(pieces, shards, scalars, heads):
    rows, width = pieces[0].shape
    group = 4 * rows
    inner = heads * HEAD
    block = 256

    def whole(shape):
        return pl.BlockSpec(
            shape, lambda i, _: (0,) * len(shape), pipeline_mode=pl.Buffered(1)
        )

    return pl.pallas_call(
        functools.partial(attend_kernel, block, MAXLEN),
        grid_spec=pltpu.PrefetchScalarGridSpec(
            num_scalar_prefetch=1,
            grid=(heads,),
            in_specs=[
                *[whole((rows, width)) for _ in range(4)],
                *[whole(shards[0].shape) for _ in range(SHARDS)],
            ],
            out_specs=[
                pl.BlockSpec((4, HEAD, rows), lambda h, _: (0, h, 0)),
                pl.BlockSpec((1, 1, group), lambda h, _: (h, 0, 0)),
                whole((3 * inner, group)),
                whole((width, 3 * inner)),
                whole((width, inner)),
            ],
            scratch_shapes=[
                pltpu.VMEM((MAXLEN + group, HEAD), BF16),
                pltpu.VMEM((HEAD, MAXLEN + group), BF16),
                pltpu.VMEM((width, 4 * inner), BF16),
            ],
        ),
        out_shape=[
            jax.ShapeDtypeStruct((4, inner, rows), BF16),
            jax.ShapeDtypeStruct((heads, 1, group), F32),
            jax.ShapeDtypeStruct((3 * inner, group), BF16),
            jax.ShapeDtypeStruct((width, 3 * inner), BF16),
            jax.ShapeDtypeStruct((width, inner), BF16),
        ],
        compiler_params=pltpu.CompilerParams(vmem_limit_bytes=48 * 2**20),
        cost_estimate=cost_of(24),
        name="attend",
    )(scalars, *pieces, *shards)


def attn_grads_kernel(scalars, *refs):
    grad_qkv, mixed, refs = refs[0], refs[1], refs[2:]
    tokens, grads, refs = refs[:4], refs[4:8], refs[8:]
    outs, (total,) = refs[:SHARDS], refs[SHARDS:]
    inner3 = grad_qkv.shape[1]
    first, second = 0.0, 0.0
    for r in range(4):
        j = scalars[1] ^ r
        first += jnp.dot(grad_qkv[j], tokens[r][...], preferred_element_type=F32)
        second += jnp.dot(mixed[j], grads[r][...], preferred_element_type=F32)
    total[:, :inner3] = first.T.astype(BF16)
    total[:, inner3:] = second.T.astype(BF16)
    rows = outs[0].shape[0]
    for r in range(SHARDS):
        place = pl.multiple_of((scalars[0] ^ r) * rows, rows)
        outs[r][...] = total[pl.ds(place, rows), :]


def attn_grads(grad_qkv, mixed, tokens, grads, scalars):
    width = tokens[0].shape[1]
    columns = grad_qkv.shape[1] + mixed.shape[1]
    rows = width // SHARDS
    whole = pl.BlockSpec(memory_space=pltpu.VMEM)
    return pl.pallas_call(
        attn_grads_kernel,
        in_specs=[pl.BlockSpec(memory_space=pltpu.SMEM)] + [whole] * 10,
        out_specs=[whole] * SHARDS,
        out_shape=[jax.ShapeDtypeStruct((rows, columns), BF16)] * SHARDS,
        scratch_shapes=[pltpu.VMEM((width, columns), BF16)],
        compiler_params=pltpu.CompilerParams(vmem_limit_bytes=48 * 2**20),
        cost_estimate=cost_of(8),
        name="attn_grads",
    )(scalars, grad_qkv, mixed, *tokens, *grads)


def attend_back_kernel(
    block, pad, scalars, q_ref, k_ref, v_ref, g_ref, lse_ref, out_ref,
    key_rows, value_rows, key_pad, grad_key, grad_value,
):
    group = q_ref.shape[1]
    window = pad + block
    quarter = group // 4
    contract_last = (((1,), (1,)), ((), ()))
    key_rows[pl.ds(0, pad), :] = jnp.zeros((pad, HEAD), BF16)
    value_rows[pl.ds(0, pad), :] = jnp.zeros((pad, HEAD), BF16)
    key_pad[:, pl.ds(0, pad)] = jnp.zeros((HEAD, pad), BF16)
    key_rows[pl.ds(pad, group), :] = k_ref[...].T
    value_rows[pl.ds(pad, group), :] = v_ref[...].T
    key_pad[:, pl.ds(pad, group)] = k_ref[...]
    grad_key[...] = jnp.zeros_like(grad_key)
    grad_value[...] = jnp.zeros_like(grad_value)

    def one(i, carry):
        first = pl.multiple_of(i * block, block)
        query = q_ref[:, pl.ds(first, block)]
        grad = g_ref[:, pl.ds(first, block)]
        scores = jnp.dot(key_rows[pl.ds(first, window), :], query, preferred_element_type=F32)
        allowed = scores_mask(first - pad, first, window, block, scalars)
        exponent = jnp.where(allowed, scores * 0.125 - lse_ref[0, :, pl.ds(first, block)], NEGATIVE)
        probs = jnp.exp(exponent)
        grad_probs = jnp.dot(
            value_rows[pl.ds(first, window), :], grad, preferred_element_type=F32
        )
        inner = jnp.sum(probs * grad_probs, axis=0, keepdims=True)
        raw = (0.125 * (probs * (grad_probs - inner))).astype(BF16)
        grad_query = jnp.dot(key_pad[:, pl.ds(first, window)], raw, preferred_element_type=F32)
        out_ref[
            first // quarter, 0, :, pl.ds(pl.multiple_of(first % quarter, block), block)
        ] = grad_query.astype(BF16)
        grad_value[:, pl.ds(first, window)] += lax.dot_general(
            grad, probs.astype(BF16), contract_last, preferred_element_type=F32
        )
        grad_key[:, pl.ds(first, window)] += lax.dot_general(
            query, raw, contract_last, preferred_element_type=F32
        )
        return carry

    lax.fori_loop(0, group // block, one, 0)
    for j in range(4):
        out_ref[j, 1] = grad_key[:, pl.ds(pad + j * quarter, quarter)].astype(BF16)
        out_ref[j, 2] = grad_value[:, pl.ds(pad + j * quarter, quarter)].astype(BF16)


def attend_back(qkv, grad_mixed, scalars, lse, heads):
    group = qkv.shape[1]
    block = 256
    return pl.pallas_call(
        functools.partial(attend_back_kernel, block, MAXLEN),
        grid_spec=pltpu.PrefetchScalarGridSpec(
            num_scalar_prefetch=1,
            grid=(heads,),
            in_specs=[
                pl.BlockSpec((HEAD, group), lambda h, _: (h, 0)),
                pl.BlockSpec((HEAD, group), lambda h, _: (h + heads, 0)),
                pl.BlockSpec((HEAD, group), lambda h, _: (h + 2 * heads, 0)),
                pl.BlockSpec((HEAD, group), lambda h, _: (h, 0)),
                pl.BlockSpec((1, 1, group), lambda h, _: (h, 0, 0)),
            ],
            out_specs=pl.BlockSpec((4, 3, HEAD, group // 4), lambda h, _: (0, 0, h, 0)),
            scratch_shapes=[
                pltpu.VMEM((MAXLEN + group, HEAD), BF16),
                pltpu.VMEM((MAXLEN + group, HEAD), BF16),
                pltpu.VMEM((HEAD, MAXLEN + group), BF16),
                pltpu.VMEM((HEAD, MAXLEN + group), F32),
                pltpu.VMEM((HEAD, MAXLEN + group), F32),
            ],
        ),
        out_shape=jax.ShapeDtypeStruct((4, 3, heads * HEAD, group // 4), BF16),
        compiler_params=pltpu.CompilerParams(vmem_limit_bytes=48 * 2**20),
        cost_estimate=cost_of(31),
        name="attend_back",
    )(scalars, qkv, qkv, qkv, grad_mixed, lse)


def inputs_back_kernel(scalars, grads, p0, p1, p2, p3, x_ref, gain_ref, hidden_ref, out_ref, sum_ref):
    total = 0.0
    for r, weight in enumerate((p0, p1, p2, p3)):
        total += lax.dot_general(
            grads[scalars[1] ^ r].T, weight[...], (((1,), (1,)), ((), ())),
            preferred_element_type=F32,
        )
    x = x_ref[...]
    scale = lax.rsqrt(jnp.mean(x * x, axis=1, keepdims=True) + EPSILON)
    through = total * gain_ref[...]
    inner = jnp.mean(through * x, axis=1, keepdims=True)
    out_ref[...] = hidden_ref[...] + scale * through - (scale * scale * scale * inner) * x
    sum_ref[...] = jnp.sum(total * x * scale, axis=0, keepdims=True)


def inputs_back(scalars, grads, weights, x, gain, grad_hidden):
    whole = pl.BlockSpec(memory_space=pltpu.VMEM)
    return pl.pallas_call(
        inputs_back_kernel,
        in_specs=[pl.BlockSpec(memory_space=pltpu.SMEM)] + [whole] * 8,
        out_specs=[whole] * 2,
        out_shape=[
            jax.ShapeDtypeStruct(x.shape, F32),
            jax.ShapeDtypeStruct((1, x.shape[1]), F32),
        ],
        compiler_params=pltpu.CompilerParams(vmem_limit_bytes=48 * 2**20),
        cost_estimate=cost_of(6),
        name="inputs_back",
    )(scalars, grads, *weights, x, gain, grad_hidden)


def expert_kernel(
    kinds, scalars, x_own, x_core, g_own, g_core, w_own, *refs
):
    w_far, refs = refs[:LOW], refs[LOW:]
    back_own, back_send, feed_own, feed_send, grads_own, *refs = refs
    grads_far, refs = refs[:LOW], refs[LOW:]
    x_all, g_all, x_t, g_t, weights, hidden, acc_feed, acc_back = refs
    slots, width = g_own.shape
    half = width // 2
    step = pl.program_id(0)
    near = pl.multiple_of(scalars[0] * half, half)
    far = pl.multiple_of((1 - scalars[0]) * half, half)
    contract_last = (((1,), (1,)), ((), ()))
    units = weights.shape[2]

    def weight_column(x_ref):
        extra = x_ref[:, width:].astype(F32)
        lanes = lax.broadcasted_iota(jnp.int32, extra.shape, 1)
        named = (lanes == scalars[1]) | (lanes == scalars[1] + kinds)
        return jnp.sum(jnp.where(named, extra, 0.0), axis=1, keepdims=True)

    @pl.when(step == 0)
    def _():
        for part, (x_ref, g_ref) in enumerate(((x_own, g_own), (x_core, g_core))):
            rows = pl.ds(part * slots, slots)
            x = x_ref[:, :width]
            grad = (g_ref[...].astype(F32) * weight_column(x_ref)).astype(BF16)
            x_all[rows, :] = x
            g_all[rows, :] = grad
            x_t[:, rows] = x.T
            g_t[:, rows] = grad.T
        acc_feed[...] = jnp.zeros_like(acc_feed)
        acc_back[...] = jnp.zeros_like(acc_back)

    for k in range(3):
        weights[k, pl.ds(near, half), :] = w_own[:, 0, k].reshape(half, units)
        for i in range(LOW):
            rows = half // LOW
            weights[k, pl.ds(pl.multiple_of(far + i * rows, rows), rows), :] = w_far[i][0, 0, k]

    for part in range(2):
        rows = pl.ds(part * slots, slots)
        x = x_all[rows, :]
        gate = jnp.dot(x, weights[0], preferred_element_type=F32)
        up = jnp.dot(x, weights[1], preferred_element_type=F32)
        grad_act = jnp.dot(g_all[rows, :], weights[2], preferred_element_type=F32)
        sig = jax.nn.sigmoid(gate)
        silu = gate * sig
        active = (silu * up).astype(BF16)
        grad_gate = (grad_act * up * (sig * (1.0 + gate * (1.0 - sig)))).astype(BF16)
        grad_up = (grad_act * silu).astype(BF16)
        hidden[0, rows, :] = grad_gate
        hidden[1, rows, :] = grad_up
        hidden[2, rows, :] = active
        acc_feed[rows, :] += lax.dot_general(
            active, weights[2], contract_last, preferred_element_type=F32
        )
        acc_back[rows, :] += lax.dot_general(
            grad_gate, weights[0], contract_last, preferred_element_type=F32
        ) + lax.dot_general(grad_up, weights[1], contract_last, preferred_element_type=F32)

    for k in range(3):
        left = (g_t if k == 2 else x_t)
        near_grad = jnp.dot(
            left[pl.ds(near, half), :], hidden[k], preferred_element_type=F32
        )
        far_grad = jnp.dot(left[pl.ds(far, half), :], hidden[k], preferred_element_type=F32)
        grads_own[:, 0, k] = near_grad.reshape(grads_own.shape[0], -1, units)
        for i in range(LOW):
            rows = half // LOW
            grads_far[i][0, 0, k] = far_grad[i * rows : (i + 1) * rows].astype(BF16)

    @pl.when(step == pl.num_programs(0) - 1)
    def _():
        for part, (x_ref, g_ref) in enumerate(((x_own, g_own), (x_core, g_core))):
            rows = pl.ds(part * slots, slots)
            feed = acc_feed[rows, :]
            inner = jnp.sum(feed * g_ref[...].astype(F32), axis=1, keepdims=True)
            feed = feed * weight_column(x_ref)
            lanes = lax.broadcasted_iota(jnp.int32, (slots, 128), 1)
            if part == 0:
                back_own[:, :width] = acc_back[rows, :]
                back_own[:, width:] = jnp.where(lanes == scalars[1], inner, 0.0)
                feed_own[...] = feed
            else:
                high = inner.astype(BF16).astype(F32)
                extra = jnp.where(lanes == scalars[1], high, 0.0)
                extra = jnp.where(lanes == scalars[1] + kinds, inner - high, extra)
                back_send[:, :width] = acc_back[rows, :].astype(BF16)
                back_send[:, width:] = extra.astype(BF16)
                feed_send[...] = feed.astype(BF16)


def expert_pass(kinds, scalars, x_own, x_core, g_own, g_core, w_own, w_far):
    slots, width = g_own.shape
    low, parities, _, shard_rows, shard_units = w_own.shape
    units = 256
    steps = shard_units // units

    def whole(shape):
        return pl.BlockSpec(
            shape, lambda i, _: (0,) * len(shape), pipeline_mode=pl.Buffered(1)
        )

    def weight_spec(count):
        return pl.BlockSpec(
            (count, 1, 3, shard_rows, units), lambda i, _: (0, i // steps, 0, 0, i % steps)
        )

    wide = width + 128
    return pl.pallas_call(
        functools.partial(expert_kernel, kinds),
        grid_spec=pltpu.PrefetchScalarGridSpec(
            num_scalar_prefetch=1,
            grid=(parities * steps,),
            in_specs=[
                whole((slots, wide)),
                whole((slots, wide)),
                whole((slots, width)),
                whole((slots, width)),
                weight_spec(low),
                *[weight_spec(1) for _ in range(low)],
            ],
            out_specs=[
                whole((slots, wide)),
                whole((slots, wide)),
                whole((slots, width)),
                whole((slots, width)),
                weight_spec(low),
                *[weight_spec(1) for _ in range(low)],
            ],
            scratch_shapes=[
                pltpu.VMEM((2 * slots, width), BF16),
                pltpu.VMEM((2 * slots, width), BF16),
                pltpu.VMEM((width, 2 * slots), BF16),
                pltpu.VMEM((width, 2 * slots), BF16),
                pltpu.VMEM((3, width, units), BF16),
                pltpu.VMEM((3, 2 * slots, units), BF16),
                pltpu.VMEM((2 * slots, width), F32),
                pltpu.VMEM((2 * slots, width), F32),
            ],
        ),
        out_shape=[
            jax.ShapeDtypeStruct((slots, wide), F32),
            jax.ShapeDtypeStruct((slots, wide), BF16),
            jax.ShapeDtypeStruct((slots, width), F32),
            jax.ShapeDtypeStruct((slots, width), BF16),
            jax.ShapeDtypeStruct(w_own.shape, F32),
            *[jax.ShapeDtypeStruct(item.shape, BF16) for item in w_far],
        ],
        compiler_params=pltpu.CompilerParams(vmem_limit_bytes=58 * 2**20),
        cost_estimate=cost_of(35),
        name="expert_pass",
    )(scalars, x_own, x_core, g_own, g_core, w_own, *w_far)


def pick_kernel(ids_ref, *refs):
    pieces, out_ref = refs[:4], refs[4]
    block = out_ref.shape[0]
    rows = pieces[0].shape[0]
    first = pl.program_id(0) * block
    total = jnp.zeros(out_ref.shape, F32)
    for r in range(4):
        slot = first + lax.broadcasted_iota(jnp.int32, (block, rows), 0)
        columns = pl.ds(r * rows, rows)
        held = (slot == ids_ref[0:1, columns]) | (slot == ids_ref[1:2, columns])
        held = jnp.where(held, 1.0, 0.0).astype(BF16)
        total = total + jnp.dot(held, pieces[r][...], preferred_element_type=F32)
    out_ref[...] = total.astype(BF16)


def pick(ids, pieces, slots):
    rows, width = pieces[0].shape
    block = 256 if slots % 256 == 0 else slots
    return pl.pallas_call(
        pick_kernel,
        grid=(slots // block,),
        in_specs=[
            pl.BlockSpec((8, 4 * rows), lambda i: (0, 0)),
            *[pl.BlockSpec((rows, width), lambda i: (0, 0)) for _ in range(4)],
        ],
        out_specs=pl.BlockSpec((block, width), lambda i: (i, 0)),
        out_shape=jax.ShapeDtypeStruct((slots, width), BF16),
        compiler_params=pltpu.CompilerParams(vmem_limit_bytes=32 * 2**20),
        cost_estimate=cost_of(5),
        name="pick",
    )(ids, *pieces)


def spread_kernel(ids_ref, slots_ref, near_ref, send_ref):
    rows = near_ref.shape[1]
    slots = slots_ref.shape[0]
    for k, out_ref in enumerate((near_ref, send_ref)):
        slot = lax.broadcasted_iota(jnp.int32, (rows, slots), 1)
        ids = ids_ref[pl.ds(k * rows, rows), :]
        held = (slot == ids[:, 0:1]) | (slot == ids[:, 1:2])
        held = jnp.where(held, 1.0, 0.0).astype(BF16)
        total = jnp.dot(held, slots_ref[...], preferred_element_type=F32)
        out_ref[0] = total.astype(out_ref.dtype)


def spread(ids, values, rows):
    slots, width = values.shape
    return pl.pallas_call(
        spread_kernel,
        grid=(2,),
        in_specs=[
            pl.BlockSpec((2 * rows, 8), lambda i: (i, 0)),
            pl.BlockSpec((slots, width), lambda i: (0, 0)),
        ],
        out_specs=[
            pl.BlockSpec((1, rows, width), lambda i: (i, 0, 0)),
            pl.BlockSpec((1, rows, width), lambda i: (i, 0, 0)),
        ],
        out_shape=[
            jax.ShapeDtypeStruct((2, rows, width), F32),
            jax.ShapeDtypeStruct((2, rows, width), BF16),
        ],
        compiler_params=pltpu.CompilerParams(vmem_limit_bytes=32 * 2**20),
        cost_estimate=cost_of(6),
        name="spread",
    )(ids, values)


def slots_kernel(experts, capacity, scalars, routes_col, order_col, routes_row, order_row,
                 row_ref, col_ref, places_ref):
    group = routes_row.shape[1]
    rows = group // 4
    share = capacity // 2
    span = 2 * group
    bound = scalars[BOUNDS + 2]

    def target_of(routes, axis):
        place = lax.broadcasted_iota(jnp.int32, routes.shape, axis)
        return jnp.where((routes < experts) & (place < bound), routes, experts)

    target = target_of(routes_row[...], 1)
    code = target * span + order_row[...]
    block = 256

    def count(i, carry):
        first = pl.multiple_of(i * block, block)
        routes = routes_col[pl.ds(first, block), :]
        place = first + lax.broadcasted_iota(jnp.int32, routes.shape, 0)
        held = jnp.where((routes < experts) & (place < bound), routes, experts)
        others = held * span + order_col[pl.ds(first, block), :]
        result = []
        for k in range(2):
            total = carry[k]
            for j in range(2):
                smaller = jnp.where(others[:, j : j + 1] < code[k : k + 1, :], 1.0, 0.0)
                total = total + jnp.sum(smaller, axis=0, keepdims=True)
            result.append(total)
        return tuple(result)

    zero = jnp.zeros((1, group), F32)
    counts = lax.fori_loop(0, group // block, count, (zero, zero))
    for k in range(2):
        mine_target = target[k : k + 1, :]
        base = jnp.zeros((1, group), F32)
        for e in range(1, experts):
            earlier = jnp.sum(jnp.where(target < e, 1.0, 0.0))
            base = jnp.where(mine_target == e, earlier, base)
        place = (counts[k] - base).astype(jnp.int32)
        first = scalars[3] * share
        held = (
            (mine_target < experts)
            & (place >= first)
            & (place < first + share)
            & (place < capacity)
            & (jnp.bitwise_and(mine_target, 1) == scalars[2])
        )
        slot = lax.shift_right_logical(mine_target, 1) * share + place - first
        places_ref[k : k + 1, :] = jnp.where(held, slot, -1)
    for r in range(4):
        start = pl.multiple_of((scalars[1] ^ r) * rows, rows)
        piece = places_ref[:, pl.ds(start, rows)]
        row_ref[:, pl.ds(r * rows, rows)] = piece
        col_ref[pl.ds(r * rows, rows), :] = piece.T


def slots_of(scalars, routes, drop_order, experts, capacity):
    group = routes.shape[0]
    whole = pl.BlockSpec(memory_space=pltpu.VMEM)
    return pl.pallas_call(
        functools.partial(slots_kernel, experts, capacity),
        in_specs=[pl.BlockSpec(memory_space=pltpu.SMEM)] + [whole] * 4,
        out_specs=[whole] * 2,
        out_shape=[
            jax.ShapeDtypeStruct((8, group), jnp.int32),
            jax.ShapeDtypeStruct((group, 8), jnp.int32),
        ],
        scratch_shapes=[pltpu.VMEM((8, group), jnp.int32)],
        compiler_params=pltpu.CompilerParams(vmem_limit_bytes=32 * 2**20),
        cost_estimate=cost_of(8),
        name="slots",
    )(scalars, routes, drop_order, routes.T, drop_order.T)


def middle_kernel(kinds, scalars, mixed, p0, p1, p2, p3, x_ref, gain_ref, router_w, prior_ref,
                  prior_w, hidden_ref, sent_ref, router_ref):
    hidden = x_ref[...]
    for r, weight in enumerate((p0, p1, p2, p3)):
        hidden += lax.dot_general(
            mixed[scalars[1] ^ r].T, weight[...], (((1,), (1,)), ((), ())),
            preferred_element_type=F32,
        )
    hidden_ref[...] = hidden
    scale = lax.rsqrt(jnp.mean(hidden * hidden, axis=1, keepdims=True) + EPSILON)
    rounded = (hidden * scale * gain_ref[...]).astype(BF16)
    width = hidden.shape[1]
    sent_ref[:, :width] = rounded
    logits = jnp.dot(
        rounded.astype(F32), router_w[...], precision=PRECISE, preferred_element_type=F32
    ) + jnp.dot(prior_ref[...], prior_w[...], precision=PRECISE, preferred_element_type=F32)
    lanes = lax.broadcasted_iota(jnp.int32, logits.shape, 1)
    logits = jnp.where(lanes < 2 * kinds, logits, NEGATIVE)
    weights = jnp.exp(logits - jnp.max(logits, axis=1, keepdims=True))
    total = jnp.sum(jnp.where(lanes < kinds, weights, 0.0), axis=1, keepdims=True)
    router = weights / total
    router_ref[...] = router
    high = router.astype(BF16).astype(F32)
    sent_ref[:, width:] = jnp.where(lanes < kinds, high, router - high).astype(BF16)


def middle(kinds, scalars, mixed, weights, x, gain, router_w, prior, prior_w):
    rows, width = x.shape
    lanes = router_w.shape[1]

    def whole(shape):
        return pl.BlockSpec(shape, lambda i, _: (0,) * len(shape))

    return pl.pallas_call(
        functools.partial(middle_kernel, kinds),
        grid_spec=pltpu.PrefetchScalarGridSpec(
            num_scalar_prefetch=1,
            grid=(1,),
            in_specs=[
                whole(mixed.shape),
                *[whole(item.shape) for item in weights],
                whole(x.shape),
                whole(gain.shape),
                whole(router_w.shape),
                pl.BlockSpec((rows, kinds), lambda i, scalars: (scalars[1], 0)),
                whole(prior_w.shape),
            ],
            out_specs=[whole((rows, width)), whole((rows, width + lanes)), whole((rows, lanes))],
        ),
        out_shape=[
            jax.ShapeDtypeStruct((rows, width), F32),
            jax.ShapeDtypeStruct((rows, width + lanes), BF16),
            jax.ShapeDtypeStruct((rows, lanes), F32),
        ],
        compiler_params=pltpu.CompilerParams(vmem_limit_bytes=48 * 2**20),
        cost_estimate=cost_of(6),
        name="middle",
    )(scalars, mixed, *weights, x, gain, router_w, prior, prior_w)


def router_back_kernel(kinds, experts, scalars, near_ref, far_ref, hidden_ref, router_ref,
                       routes_ref, cotangent_ref, prior_ref, gain_ref, small_ref, small_t_ref,
                       vector_ref, prior_w_ref,
                       grad_hidden_ref, grad_low_ref, partial_ref, grad_prior_ref, sums_ref):
    step = pl.program_id(0)
    rows, width = hidden_ref.shape
    place = scalars[1] * rows * pl.num_programs(0) + step * rows
    valid = place + lax.broadcasted_iota(jnp.int32, (rows, 1), 0) < scalars[BOUNDS + 2]
    valid = jnp.where(valid, 1.0, 0.0)
    back = near_ref[...] + far_ref[...].astype(F32)
    hidden = hidden_ref[...]
    grad_out = cotangent_ref[...] * valid
    scale = lax.rsqrt(jnp.mean(hidden * hidden, axis=1, keepdims=True) + EPSILON)
    unit = hidden * scale
    normed = unit * gain_ref[...]
    router = router_ref[...]
    lanes = lax.broadcasted_iota(jnp.int32, router.shape, 1)
    routes = routes_ref[...]

    def column(array, k):
        return jnp.sum(jnp.where(lanes == k, array, 0.0), axis=1, keepdims=True)

    def named(kind):
        return jnp.where((routes[:, 0:1] == kind) | (routes[:, 1:2] == kind), 1.0, 0.0)

    copy, first, second = (named(experts + k) for k in (1, 2, 3))
    weight_copy = column(router, experts + 1) * copy
    weight_first = column(router, experts + 2) * first
    weight_second = column(router, experts + 3) * second
    mixlog = jnp.dot(normed, small_ref[...], precision=PRECISE, preferred_element_type=F32)

    def softmax_two(k):
        one, two = column(mixlog, k), column(mixlog, k + 1)
        highest = jnp.maximum(one, two)
        one, two = jnp.exp(one - highest), jnp.exp(two - highest)
        return one / (one + two), two / (one + two)

    mix_one, mix_two = softmax_two(kinds), softmax_two(kinds + 2)
    vector_one, vector_two = vector_ref[0:1, :], vector_ref[1:2, :]
    along = jnp.sum(normed * grad_out, axis=1, keepdims=True)
    along_one = jnp.sum(vector_one * grad_out, axis=1, keepdims=True)
    along_two = jnp.sum(vector_two * grad_out, axis=1, keepdims=True)

    extra = back[:, width:]
    pairs = jnp.where(lanes < kinds, extra, 0.0) + jnp.where(
        lanes < kinds, pltpu.roll(extra, extra.shape[1] - kinds, 1), 0.0
    )
    grad_router = pairs + jnp.where(lanes == experts + 1, copy * along, 0.0)
    grad_router += jnp.where(
        lanes == experts + 2, first * (mix_one[0] * along + mix_one[1] * along_one), 0.0
    )
    grad_router += jnp.where(
        lanes == experts + 3, second * (mix_two[0] * along + mix_two[1] * along_two), 0.0
    )
    held = jnp.where(lanes < kinds, router, 0.0)
    grad_small = held * (grad_router - jnp.sum(held * grad_router, axis=1, keepdims=True))
    grad_prior_ref[...] = jnp.dot(
        grad_small, prior_w_ref[...], precision=PRECISE, preferred_element_type=F32
    )[:, :kinds]
    grad_logits = grad_small

    def mixed_back(weight, mix, other, k):
        one, two = weight * along, weight * other
        inner = mix[0] * one + mix[1] * two
        return jnp.where(lanes == k, mix[0] * (one - inner), 0.0) + jnp.where(
            lanes == k + 1, mix[1] * (two - inner), 0.0
        )

    grad_mixlog = mixed_back(weight_first, mix_one, along_one, kinds) + mixed_back(
        weight_second, mix_two, along_two, kinds + 2
    )
    grad_small = grad_logits + grad_mixlog
    share = weight_copy + weight_first * mix_one[0] + weight_second * mix_two[0]
    grad_normed = (
        back[:, :width]
        + share * grad_out
        + jnp.dot(grad_small, small_t_ref[...], precision=PRECISE, preferred_element_type=F32)
    )
    through = grad_normed * gain_ref[...]
    inner = jnp.mean(through * hidden, axis=1, keepdims=True)
    grad_hidden = grad_out + scale * through - (scale * scale * scale * inner) * hidden
    grad_hidden_ref[...] = grad_hidden
    grad_low_ref[...] = grad_hidden.astype(BF16)
    vector_first, vector_second = weight_first * mix_one[1], weight_second * mix_two[1]
    partial_ref[...] = valid * (
        hidden + share * normed + vector_first * vector_one + vector_second * vector_two
    )

    @pl.when(step == 0)
    def _():
        sums_ref[...] = jnp.zeros_like(sums_ref)

    def turned_dot(left, right):
        return jnp.dot(left.T, right, precision=PRECISE, preferred_element_type=F32)

    rounded = normed.astype(BF16).astype(F32)
    vectors = jnp.where(lanes == kinds + 5, vector_first, 0.0) + jnp.where(
        lanes == kinds + 6, vector_second, 0.0
    )
    total = (
        turned_dot(grad_logits, rounded)
        + turned_dot(grad_mixlog, normed)
        + turned_dot(vectors, grad_out)
    )
    sums_ref[: kinds + 8, :] += total[: kinds + 8, :]
    sums_ref[kinds + 4 : kinds + 5, :] += jnp.sum(grad_normed * unit, axis=0, keepdims=True)
    prior = turned_dot(prior_ref[...], grad_logits)
    sums_ref[pl.ds(kinds + 8, kinds), : lanes.shape[1]] += prior


def router_back(kinds, experts, scalars, near, far, hidden, router, routes, cotangent, prior,
                gain, small, small_t, vector, prior_w):
    rows, width = hidden.shape
    block = rows // 4
    lanes = router.shape[1]

    def whole(shape):
        return pl.BlockSpec(shape, lambda i, _: (0,) * len(shape))

    def part(columns):
        return pl.BlockSpec((block, columns), lambda i, _: (i, 0))

    def mine(columns):
        return pl.BlockSpec((block, columns), lambda i, scalars: (scalars[1] * 4 + i, 0))

    return pl.pallas_call(
        functools.partial(router_back_kernel, kinds, experts),
        grid_spec=pltpu.PrefetchScalarGridSpec(
            num_scalar_prefetch=1,
            grid=(4,),
            in_specs=[
                part(width + lanes),
                part(width + lanes),
                part(width),
                part(lanes),
                mine(2),
                part(width),
                mine(kinds),
                whole(gain.shape),
                whole(small.shape),
                whole(small_t.shape),
                whole(vector.shape),
                whole(prior_w.shape),
            ],
            out_specs=[
                part(width),
                part(width),
                part(width),
                part(kinds),
                whole((32, width)),
            ],
        ),
        out_shape=[
            jax.ShapeDtypeStruct((rows, width), F32),
            jax.ShapeDtypeStruct((rows, width), BF16),
            jax.ShapeDtypeStruct((rows, width), F32),
            jax.ShapeDtypeStruct((rows, kinds), F32),
            jax.ShapeDtypeStruct((32, width), F32),
        ],
        compiler_params=pltpu.CompilerParams(vmem_limit_bytes=48 * 2**20),
        cost_estimate=cost_of(8),
        name="router_back",
    )(scalars, near, far, hidden, router, routes, cotangent, prior, gain, small, small_t,
      vector, prior_w)


def two_parts(value):
    high = lax.reduce_precision(value, 8, 7)
    return jnp.concatenate([high, value - high], axis=-1).astype(BF16)


def after(value, *others):
    return lax.optimization_barrier((value, *others))[0]


def everywhere(value, axes, count):
    copies = jnp.broadcast_to(value[None], (count, *value.shape))
    return lax.all_to_all(copies, axes, 0, 0, tiled=True)


def flip(value, axis, size, bit):
    return lax.ppermute(value, axis, [(i, i ^ bit) for i in range(size)])


def gather_rows(value, many):
    if many != 2:
        full = lax.all_gather(value, ("hi", "lo"), axis=0, tiled=True)
        return list(full.reshape(SHARDS, -1, full.shape[1]))
    return [value] + [flip(value, ("hi", "lo"), SHARDS, bit) for bit in range(1, SHARDS)]


def scatter_rows(pieces, many):
    if many != 2:
        full = jnp.concatenate(pieces).astype(F32)
        return lax.psum_scatter(full, ("hi", "lo"), scatter_dimension=0, tiled=True)
    total = pieces[0].astype(F32)
    for bit in range(1, SHARDS):
        total = total + flip(pieces[bit], ("hi", "lo"), SHARDS, bit).astype(F32)
    return total


def per_device(
    many,
    inputs,
    cotangent,
    lengths,
    routes,
    drop_order,
    prior_logits,
    attn_gain,
    w_query,
    w_key,
    w_value,
    w_out,
    moe_gain,
    w_router,
    w_prior,
    w_const,
    const_vector,
    w_gate,
    w_up,
    w_down,
):
    tok_rows, width = inputs.shape
    group = tok_rows * 4
    kinds = w_router.shape[1]
    experts, shard_rows, shard_units = w_gate.shape
    capacity = 3 * group // 16
    share = capacity // 2
    slots = LOW * share
    local_width = w_query.shape[1]
    heads = local_width // HEAD
    tp_axes = ("y", "c")
    all_axes = ("hi", "lo", "y", "c")
    count = many * LOW * 4
    wide = width + 128
    high = lax.axis_index("hi")
    parity = lax.axis_index("y")
    core = lax.axis_index("c")
    place_in_group = parity * 2 + core
    mine = high * LOW + lax.axis_index("lo") if many == 2 else jnp.zeros_like(high)
    boundary = jnp.cumsum(lengths[0])
    scalars = jnp.concatenate(
        [jnp.stack([mine, place_in_group, parity, core]), boundary[:-1]]
    ).astype(jnp.int32)
    gain_one, gain_two = attn_gain.reshape(1, width), moe_gain.reshape(1, width)

    normed_one = rms_norm(inputs, attn_gain).astype(BF16)
    normed_pieces = gather_pieces(normed_one)
    attn_shard = jnp.concatenate([w_query, w_key, w_value, w_out.T], axis=1)
    attn_shards = gather_rows(attn_shard, many)
    expert_shards = jnp.stack([w_gate, w_up, w_down.transpose(0, 2, 1)], axis=1)
    expert_part = lax.all_to_all(expert_shards, ("lo", "y"), 0, 0, tiled=True)
    expert_part = expert_part.reshape(LOW, 2, 3, shard_rows, shard_units)
    if many == 2:
        expert_near = expert_part
        expert_far = [swap(expert_part[i : i + 1], "hi") for i in range(LOW)]
        high_place = high
    else:
        rows = lax.all_gather(expert_part, "hi", axis=0).transpose(2, 3, 0, 1, 4, 5)
        rows = rows.reshape(2, 3, 2, LOW, width // (2 * LOW), shard_units)
        rows = rows.transpose(2, 3, 0, 1, 4, 5)
        expert_near = rows[0]
        expert_far = [rows[1, i : i + 1] for i in range(LOW)]
        high_place = jnp.zeros_like(high)
    router_lanes = jnp.pad(jnp.concatenate([w_router, w_router], axis=1), ((0, 0), (0, 128 - 2 * kinds)))
    prior_lanes = jnp.pad(jnp.concatenate([w_prior, w_prior], axis=1), ((0, 0), (0, 128 - 2 * kinds)))
    const_flat = w_const.transpose(1, 0, 2).reshape(width, 4)
    small = jnp.pad(jnp.concatenate([w_router, const_flat], axis=1), ((0, 0), (0, 112 - kinds + 12)))
    small_t = small.T
    prior_back = jnp.pad(w_prior.T, ((0, 128 - kinds), (0, 128 - kinds)))

    valid_mine = place_in_group * tok_rows + jnp.arange(tok_rows)[:, None] < boundary[-2]
    valid_mine = valid_mine.astype(F32)
    grad_out_low = (cotangent * valid_mine).astype(BF16)
    grad_out_pieces = gather_pieces(after(grad_out_low, normed_pieces[3]))
    mixed, lse, qkv, qkv_full, out_full = attend(normed_pieces, attn_shards, scalars, heads)
    mixed, expert_far[0], grad_out_pieces = lax.optimization_barrier(
        (mixed, expert_far[0], grad_out_pieces)
    )

    mixed_mine = lax.all_to_all(mixed, tp_axes, 0, 0, tiled=True)
    out_pieces = gather_pieces(out_full)
    ids_rows, ids_cols = slots_of(
        after(scalars, mixed), routes, drop_order, experts, capacity
    )
    grad_out_slots = pick(ids_rows, grad_out_pieces, slots)
    mixed_mine, grad_out_slots, ids_cols, out_pieces = lax.optimization_barrier(
        (mixed_mine, grad_out_slots, ids_cols, out_pieces)
    )

    hidden, sent_two, router = middle(
        kinds, scalars, mixed_mine, out_pieces, inputs, gain_two, router_lanes, prior_logits, prior_lanes
    )
    sent_two, expert_far[1] = lax.optimization_barrier((sent_two, expert_far[1]))

    pieces_two = gather_pieces(sent_two)
    grad_taken = lax.all_to_all(
        grad_out_slots.reshape(LOW, share, width), "lo", 0, 0, tiled=True
    ).reshape(slots, width)
    pieces_two, grad_taken, expert_far[2] = lax.optimization_barrier(
        (pieces_two, grad_taken, expert_far[2])
    )

    grad_core = swap(grad_taken, "c")
    sent_slots = pick(ids_rows, pieces_two, slots)
    taken = lax.all_to_all(sent_slots.reshape(LOW, share, wide), "lo", 0, 0, tiled=True)
    taken = taken.reshape(slots, wide)
    qkv_pieces = gather_pieces(after(qkv_full, sent_slots))
    taken, qkv_pieces, expert_far[3] = lax.optimization_barrier(
        (taken, qkv_pieces, expert_far[3])
    )

    expert = lax.axis_index("lo") * 2 + parity
    back_own, back_send, feed_own, feed_send, grads_own, *grads_far = expert_pass(
        kinds, jnp.stack([high_place, expert]).astype(jnp.int32),
        taken, swap(taken, "c"), grad_taken, grad_core, expert_near, expert_far,
    )

    if many == 2:
        grads_far = [swap(item, "hi") for item in grads_far]
    back_core = swap(back_send, "c").astype(F32)
    inner = (
        back_own[:, width : width + kinds]
        + back_core[:, width : width + kinds]
        + back_core[:, width + kinds : width + 2 * kinds]
    )
    back_slots = jnp.concatenate(
        [
            (back_own[:, :width] + back_core[:, :width]).astype(BF16),
            jnp.pad(two_parts(inner), ((0, 0), (0, 128 - 2 * kinds))),
        ],
        axis=1,
    )
    feed_slots = (feed_own + swap(feed_send, "c").astype(F32)).astype(BF16)
    back_taken = lax.all_to_all(back_slots.reshape(LOW, share, wide), "lo", 0, 0, tiled=True)
    back_taken, feed_slots, grads_far[0] = lax.optimization_barrier(
        (back_taken.reshape(slots, wide), feed_slots, grads_far[0])
    )

    back_near, back_other = add_core(*spread(ids_cols, back_taken, tok_rows))
    back_far = swap(back_other, "y")
    feed_taken = lax.all_to_all(feed_slots.reshape(LOW, share, width), "lo", 0, 0, tiled=True)
    back_far, feed_taken, grads_far[1] = lax.optimization_barrier(
        (back_far, feed_taken.reshape(slots, width), grads_far[1])
    )

    grad_hidden, grad_low, partial, grad_prior, sums = router_back(
        kinds, experts, scalars, back_near, back_far, hidden, router, routes, cotangent,
        prior_logits, gain_two, small, small_t, const_vector, prior_back,
    )
    grad_attn_pieces = gather_pieces(grad_low)
    feed_near, feed_other = add_core(*spread(ids_cols, feed_taken, tok_rows))
    share_sums = lax.all_to_all(sums.reshape(count, 32 * width // count), all_axes, 0, 0, tiled=True)
    share_sums = jnp.sum(share_sums, axis=0)
    grad_attn_pieces, grads_far, feed_near, feed_other, share_sums = lax.optimization_barrier(
        (grad_attn_pieces, grads_far, feed_near, feed_other, share_sums)
    )

    feed_far = swap(feed_other, "y")
    grad_attn_all = natural(grad_attn_pieces, place_in_group)
    grad_mixed = lax.dot_general(
        out_full,
        grad_attn_all.reshape(group, width),
        (((0,), (1,)), ((), ())),
        preferred_element_type=F32,
    ).astype(BF16)
    far_grads = jnp.concatenate(grads_far).reshape(grads_own.shape)
    if many == 2:
        weight_part = (grads_own + far_grads.astype(F32)).astype(BF16)
    else:
        rows = jnp.stack([grads_own, far_grads.astype(F32)])
        rows = rows.transpose(2, 3, 0, 1, 4, 5).reshape(
            2, 3, many, LOW, shard_rows, shard_units
        )
        weight_part = (
            lax.psum_scatter(rows, "hi", scatter_dimension=2).transpose(2, 0, 1, 3, 4).astype(BF16)
        )
    weight_own = lax.all_to_all(
        weight_part.reshape(2 * LOW, 3, shard_rows, shard_units), ("lo", "y"), 0, 0, tiled=True
    )
    grad_qkv = attend_back(qkv, grad_mixed, scalars, lse, heads).reshape(
        4, 3 * local_width, tok_rows
    )
    grad_qkv, weight_own, feed_far = lax.optimization_barrier((grad_qkv, weight_own, feed_far))

    grad_qkv_mine = lax.all_to_all(grad_qkv, tp_axes, 0, 0, tiled=True)
    weight_own = weight_own.astype(F32)
    output = partial + valid_mine * (feed_near + feed_far.astype(F32))
    grad_attn_own = scatter_rows(
        attn_grads(grad_qkv, mixed, normed_pieces, grad_attn_pieces, scalars), many
    )
    grad_inputs, gain_part = inputs_back(
        scalars, grad_qkv_mine, qkv_pieces, inputs, gain_one, grad_hidden
    )
    last = everywhere(
        jnp.concatenate([gain_part.reshape(-1), share_sums]), all_axes, count
    )
    grad_gain = jnp.sum(last[:, :width], axis=0)
    total = last[:, width:].reshape(32, width)
    return (
        output,
        grad_inputs,
        grad_prior,
        grad_gain,
        grad_attn_own[:, :local_width],
        grad_attn_own[:, local_width : 2 * local_width],
        grad_attn_own[:, 2 * local_width : 3 * local_width],
        grad_attn_own[:, 3 * local_width :].T,
        total[kinds + 4],
        total[:kinds].T,
        total[kinds + 8 : 2 * kinds + 8, :kinds],
        total[kinds : kinds + 4].reshape(2, 2, width).transpose(0, 2, 1),
        total[kinds + 5 : kinds + 7],
        weight_own[:, 0],
        weight_own[:, 1],
        weight_own[:, 2].transpose(0, 2, 1),
    )


def solution(mesh):
    many = mesh.shape["fsdp"] // LOW
    fine = Mesh(mesh.devices.reshape(many, LOW, 2, 2), ("hi", "lo", "y", "c"))
    fsdp, tp = ("hi", "lo"), ("y", "c")
    every = fsdp + tp
    return jax.shard_map(
        functools.partial(per_device, many),
        mesh=fine,
        in_specs=(
            P(every, None),
            P(every, None),
            P(fsdp, None),
            P(fsdp, None),
            P(fsdp, None),
            P(fsdp, None),
            P(),
            P(fsdp, tp),
            P(fsdp, tp),
            P(fsdp, tp),
            P(tp, fsdp),
            P(),
            P(),
            P(),
            P(),
            P(),
            P(None, fsdp, tp),
            P(None, fsdp, tp),
            P(None, tp, fsdp),
        ),
        out_specs=(
            P(every, None),
            P(every, None),
            P(every, None),
            P(),
            P(fsdp, tp),
            P(fsdp, tp),
            P(fsdp, tp),
            P(tp, fsdp),
            P(),
            P(),
            P(),
            P(),
            P(),
            P(None, fsdp, tp),
            P(None, fsdp, tp),
            P(None, tp, fsdp),
        ),
        check_vma=False,
    )
```

time: 829 us -> 658 us (0.79)
  matrix products: 110 us -> 1.21 us
  Pallas kernels: 50.5 us -> 157 us
  local copies, waits for them, and re-layouts: 143 us -> 58.9 us
  starting transfers between devices: 56.2 us -> 127 us
  other arithmetic: 102 us -> 32.4 us
  blocking collectives: 53.1 us -> 0 us
  waiting for transfers between devices: 288 us -> 272 us
  between operations: 16 us -> 1.79 us
    dot_general x31 -> x1, matrix products: 110 us -> 1.21 us  [per_device(): lax.dot_general(out_full, grad_attn_all.reshape(group, width), (((0,), (1...]
    pallas_call x1 -> x11, Pallas kernels: 19.2 us -> 125 us  [the longest x1 34.5 us: expert_pass(): pl.pallas_call(functools.partial(expert_kernel, kinds), grid_spec=pltpu.P...]
    psum x1 -> x0, blocking collectives: 53.1 us -> none  [per_device(): lax.psum((grad_attn_gain, grad_moe_gain, grad_router, grad_prior_w, grad_...]
    all_to_all x5 -> x8, waiting for transfers between devices: 10.5 us -> 57.6 us  [the longest x1 49.7 us: per_device(): lax.all_to_all(sums.reshape(count, 32 * width // count), all_axes, 0, 0,...]
    all_gather x2 -> x0, waiting for transfers between devices: 45.4 us -> none  [the longest x1 45.3 us: per_device(): attn_full = lax.all_gather(attn_weights, ('hi', 'lo'), axis=0, tiled=True)]
    ppermute x0 -> x14, starting transfers between devices: none -> 36.7 us  [flip(): return lax.ppermute(value, axis, [(i, i ^ bit) for i in range(size)])]
    ppermute x20 -> x34, starting transfers between devices: 24.5 us -> 46.2 us  [swap(): return lax.ppermute(value, axis, [(0, 1), (1, 0)])]
    another operation x4 -> x0, local copies, waits for them, and re-layouts: 20.6 us -> none  [the longest x2 11 us: per_device(): expert_rows = jnp.stack([expert_part, swap(expert_part, 'hi')])]
  transfers between devices with their start and end apart: 29 -> 58, of which waited for: 10 -> 18; matrix products, arithmetic and copies ran while one was open for 31% -> 8% of each run, Pallas kernels for 6% -> 17%
where the time goes in v2:
time: 658 us; the launch traced here: 651 us
  waiting for transfers between devices  272 us (41%)
  Pallas kernels  157 us (24%)
  starting transfers between devices  127 us (19%)
  local copies, waits for them, and re-layouts  58.9 us (9%)
  other arithmetic  32.4 us (5%)
    ppermute x34, waiting for transfers between devices, swap(): return lax.ppermute(value, axis, [(0, 1), (1, 0)])  212 us
    all_to_all x1, waiting for transfers between devices, per_device(): lax.all_to_all(sums.reshape(count, 32 * width // count), all_axes, 0, 0,...  49.7 us
    ppermute x34, starting transfers between devices, swap(): return lax.ppermute(value, axis, [(0, 1), (1, 0)])  46.2 us
    ppermute x14, starting transfers between devices, flip(): return lax.ppermute(value, axis, [(i, i ^ bit) for i in range(size)])  36.7 us
    pallas_call x1, Pallas kernels, expert_pass(): pl.pallas_call(functools.partial(expert_kernel, kinds), grid_spec=pltpu.P...  34.5 us
    unnamed x184, local copies, waits for them, and re-layouts  34.2 us
    pallas_call x1, Pallas kernels, attend_back(): pl.pallas_call(functools.partial(attend_back_kernel, block, MAXLEN), grid...  31.8 us
    pallas_call x1, Pallas kernels, attend(): pl.pallas_call(functools.partial(attend_kernel, block, MAXLEN), grid_spec...  24.2 us
  transfers between devices with their start and end apart: 58, of which 18 were waited for; matrix products, arithmetic and copies ran while one was open for 8% of the time, Pallas kernels for 17%

profile of v2, /device:TPU:1, one launch (start us, length us, event | category | flops | bytes accessed | tf_op | source)
XLA Modules:
  0.0 650.8 jit_solution(10087442588478049397)
XLA Ops:
  0.6 3.4 pad_maximum_fusion.1
  4.0 5.4 all-to-all-start
  11.4 42.0 %collective-permute-done.1.refs_2_.refs_4_ = bf16[512,768]{1,0:T(8,128)(2,1)S(1)} collective-permute-done((bf16[512,768]{1,0:T(8,128)(2,1)S(1)}, bf16[512,768]{1,0:T(8,128)(2,1)S(1)}, u32[]{:S(2)}, u32[]{:S(2)}) %collective-permute-start.1) | collective-permute-done | bytes 786464 | tf_op jit(solution)/shard_map/ppermute | solution.py:28
  56.4 2.4 multiply_convert_fusion.refs_0_
  68.2 2.7 collective-permute-start.8
  70.9 12.2 %collective-permute-start.9 = (bf16[96,768]{1,0:T(8,128)(2,1)S(1)}, bf16[96,768]{1,0:T(8,128)(2,1)}, u32[]{:S(2)}, u32[]{:S(2)}) collective-permute-start(bf16[96,768]{1,0:T(8,128)(2,1)S(1)} %pad_maximum_fusion.3.refs_4_), channel_id=1, source_target_pairs={{0,28},{4,24},{8,20},{12,16},{16,12},{20,8},{24,4},{28,0},{1,29},{... | collective-permute-start | bytes 442376 | tf_op jit(solution)/shard_map/ppermute | solution.py:852
  83.0 3.1 slice_bitcast_fusion.3
  86.8 3.7 collective-permute-start.11
  93.0 24.2 %attend.1 = (bf16[4,192,512]{2,1,0:T(8,128)(2,1)S(1)}, f32[3,1,2048]{2,1,0:T(1,128)S(1)}, bf16[576,2048]{1,0:T(8,128)(2,1)}, bf16[768,576]{1,0:T(8,128)(2,1)}, bf16[768,192]{1,0:T(8,128)(2,1)S(1)}) custom-call(s32[7]{0:T(128)S(1)} %concatenate.28.scalars, bf16[512,768]{1,0:T(8,128)(2,1)S(1)} %multiply_convert_fusion.1.refs_0_.refs_2_, ...), custom_call_target="tpu_custom_call" | custom-call | flops 27599998976 | bytes 1048576 | tf_op jit(solution)/shard_map/attend/pallas_call | solution.py:132
  127.3 3.6 collective-permute-start.14
  130.9 15.9 %collective-permute-start.17 = (bf16[1,2,3,96,512]{4,3,2,1,0:T(8,128)(2,1)}, bf16[1,2,3,96,512]{4,3,2,1,0:T(8,128)(2,1)}, u32[]{:S(2)}, u32[]{:S(2)}) collective-permute-start(bf16[1,2,3,96,512]{4,3,2,1,0:T(8,128)(2,1)} %get-tuple-element.271), channel_id=1, source_target_pairs={{0,16},{16,0},{1,17},{17,1},{2,18},{18,2},{3,19},{19,3},{4,20},{20... | collective-permute-start | bytes 1769480 | tf_op jit(solution)/shard_map/ppermute | solution.py:28
  146.8 4.7 all-to-all-start.1
  152.9 10.0 %slots.1 = (s32[8,2048]{1,0:T(8,128)S(1)}, s32[2048,8]{1,0:T(8,128)S(1)}) custom-call(s32[7]{0:T(128)S(1)} %copy-done.31, s32[2048,2]{1,0:T(8,128)S(1)} %copy.86.routes_col.routes_ref, s32[2048,2]{1,0:T(8,128)S(1)} %copy.87.order_col, s32[2,2048]{1,0:T(2,128)S(1)} %bitcast.82, s32[2,2048]{1,0:T(2,128)S(1)} %bitcast.83), custom_call_target="tpu_custom_call" | custom-call | flops 9200000000 | bytes 1048576 | tf_op jit(solution)/shard_map/slots/pallas_call | solution.py:596
  163.9 5.8 pick.2
  169.8 6.9 %middle.1 = (f32[512,768]{1,0:T(8,128)}, bf16[512,896]{1,0:T(8,128)(2,1)S(1)}, f32[512,128]{1,0:T(8,128)S(1)}) custom-call(s32[7]{0:T(128)S(1)} %copy-done.32, bf16[4,192,512]{2,1,0:T(8,128)(2,1)} %all-to-all-done.1.mixed, bf16[768,192]{1,0:T(8,128)(2,1)S(1)} %get-tuple-element.117.p0, bf16[768,192]{1,0:T(8,128)(2,1)} %collective-permute-done.14.p1, ...), custom_call_target="tpu_custom_call" | custom-call | flops 6899999744 | bytes 1048576 | tf_op jit(solution)/shard_map/middle/pallas_call | solution.py:644
  178.2 4.3 all-to-all-start.2
  183.2 15.5 %collective-permute-done.19.refs_2_ = bf16[512,896]{1,0:T(8,128)(2,1)S(1)} collective-permute-done((bf16[512,896]{1,0:T(8,128)(2,1)S(1)}, bf16[512,896]{1,0:T(8,128)(2,1)S(1)}, u32[]{:S(2)}, u32[]{:S(2)}) %collective-permute-start.19) | collective-permute-done | bytes 917536 | tf_op jit(solution)/shard_map/ppermute | solution.py:28
  199.6 26.6 %collective-permute-done.21.refs_2_ = bf16[1,2,3,96,512]{4,3,2,1,0:T(8,128)(2,1)} collective-permute-done((bf16[1,2,3,96,512]{4,3,2,1,0:T(8,128)(2,1)}, bf16[1,2,3,96,512]{4,3,2,1,0:T(8,128)(2,1)}, u32[]{:S(2)}, u32[]{:S(2)}) %collective-permute-start.21) | collective-permute-done | bytes 589856 | tf_op jit(solution)/shard_map/ppermute | solution.py:28
  228.3 5.8 pick.3
  234.1 3.9 all-to-all-start.3
  241.4 18.9 %collective-permute-done.23 = bf16[768,576]{0,1:T(8,128)(2,1)S(1)} collective-permute-done((bf16[768,576]{0,1:T(8,128)(2,1)}, bf16[768,576]{0,1:T(8,128)(2,1)S(1)}, u32[]{:S(2)}, u32[]{:S(2)}) %collective-permute-start.23) | collective-permute-done | bytes 884768 | tf_op jit(solution)/shard_map/ppermute | solution.py:28
  261.7 28.3 %collective-permute-done.25.refs_3_ = bf16[1,2,3,96,512]{4,3,2,1,0:T(8,128)(2,1)S(1)} collective-permute-done((bf16[1,2,3,96,512]{4,3,2,1,0:T(8,128)(2,1)S(1)}, bf16[1,2,3,96,512]{4,3,2,1,0:T(8,128)(2,1)S(1)}, u32[]{:S(2)}, u32[]{:S(2)}) %collective-permute-start.25) | collective-permute-done | bytes 589856 | tf_op jit(solution)/shard_map/ppermute | solution.py:28
  293.4 4.1 collective-permute-done.27.g_core
  297.5 34.5 %expert_pass.1 = (f32[768,896]{1,0:T(8,128)}, bf16[768,896]{1,0:T(8,128)(2,1)}, f32[768,768]{1,0:T(8,128)}, bf16[768,768]{1,0:T(8,128)(2,1)}, f32[4,2,3,96,512]{...) custom-call(s32[2]{0:T(128)} %pad_add_fusion.scalars, ...), custom_call_target="tpu_custom_call" | custom-call | flops 40249999360 | bytes 1048576 | tf_op jit(solution)/shard_map/expert_pass/pallas_call | solution.py:422
  332.5 3.0 collective-permute-done.28
  337.6 4.0 all-to-all-start.4
  344.7 3.1 add_convert_fusion.1
  347.8 21.5 %collective-permute-done.30 = bf16[1,2,3,96,512]{4,3,2,1,0:T(8,128)(2,1)S(1)} collective-permute-done((bf16[1,2,3,96,512]{4,3,2,1,0:T(8,128)(2,1)}, bf16[1,2,3,96,512]{4,3,2,1,0:T(8,128)(2,1)S(1)}, u32[]{:S(2)}, u32[]{:S(2)}) %collective-permute-start.30) | collective-permute-done | bytes 589856 | tf_op jit(solution)/shard_map/ppermute | solution.py:28
  371.1 4.8 spread.2
  379.0 3.5 all-to-all-start.5
  392.6 23.7 %collective-permute-done.33 = bf16[1,2,3,96,512]{4,3,2,1,0:T(8,128)(2,1)S(1)} collective-permute-done((bf16[1,2,3,96,512]{4,3,2,1,0:T(8,128)(2,1)}, bf16[1,2,3,96,512]{4,3,2,1,0:T(8,128)(2,1)S(1)}, u32[]{:S(2)}, u32[]{:S(2)}) %collective-permute-start.33) | collective-permute-done | bytes 589856 | tf_op jit(solution)/shard_map/ppermute | solution.py:28
  420.9 3.9 spread.3
  426.0 16.1 %router_back.1 = (f32[512,768]{1,0:T(8,128)}, bf16[512,768]{1,0:T(8,128)(2,1)}, f32[512,768]{1,0:T(8,128)}, f32[512,12]{1,0:T(8,128)S(1)}, f32[32,768]{1,0:T(8,128)S(1)}) custom-call(s32[7]{0:T(128)S(1)} %copy-done.32, f32[512,896]{1,0:T(8,128)} %get-tuple-element.257.near_ref, bf16[512,896]{1,0:T(8,128)(2,1)S(1)} %copy-done.34, ...), custom_call_target="tpu_custom_call" | custom-call | flops 9200000000 | bytes 1048576 | tf_op jit(solution)/shard_map/router_back/pallas_call | solution.py:796
  443.2 19.1 %collective-permute-done.35.refs_8_ = bf16[512,768]{1,0:T(8,128)(2,1)} collective-permute-done((bf16[512,768]{1,0:T(8,128)(2,1)}, bf16[512,768]{1,0:T(8,128)(2,1)}, u32[]{:S(2)}, u32[]{:S(2)}) %collective-permute-start.35) | collective-permute-done | bytes 786464 | tf_op jit(solution)/shard_map/ppermute | solution.py:28
  466.2 4.0 all-to-all-start.6
  470.2 49.7 %all-to-all-done.6 = f32[32,1,768]{2,1,0:T(1,128)} async-done(((f32[32,1,768]{2,1,0:T(1,128)}), f32[32,1,768]{2,1,0:T(1,128)}, u32[]{:S(2)}, u32[]{:S(2)}) %all-to-all-start.6) | async-done | bytes 98336 | tf_op jit(solution)/shard_map/all_to_all | solution.py:1024
  526.0 2.8 add_convert_fusion
  528.8 3.8 all-to-all-start.7
  538.4 31.8 %attend_back.1 = bf16[4,3,192,512]{3,2,1,0:T(8,128)(2,1)} custom-call(s32[7]{0:T(128)S(1)} %copy-done.32, bf16[576,2048]{1,0:T(8,128)(2,1)S(1)} %copy-done.53, bf16[576,2048]{1,0:T(8,128)(2,1)S(1)} %copy-done.53, bf16[576,2048]{1,0:T(8,128)(2,1)S(1)} %copy-done.53, bf16[192,2048]{1,0:T(8,128)(2,1)S(1)} %convolution_convert_fusion.g_ref, ...), custom_call_target="tpu_custom_call" | custom-call | flops 35649998848 | bytes 1048576 | tf_op jit(solution)/shard_map/attend_back/pallas_call | solution.py:253
  570.1 6.7 %collective-permute-done.40 = bf16[512,768]{1,0:T(8,128)(2,1)} collective-permute-done((bf16[512,768]{1,0:T(8,128)(2,1)}, bf16[512,768]{1,0:T(8,128)(2,1)}, u32[]{:S(2)}, u32[]{:S(2)}) %collective-permute-start.40) | collective-permute-done | bytes 786464 | tf_op jit(solution)/shard_map/ppermute | solution.py:28
  578.2 5.6 all-to-all-start.8
  593.0 6.8 %attn_grads.1 = (bf16[96,768]{1,0:T(8,128)(2,1)S(1)}, bf16[96,768]{1,0:T(8,128)(2,1)}, bf16[96,768]{1,0:T(8,128)(2,1)}, bf16[96,768]{1,0:T(8,128)(2,1)}, bf16[96...) custom-call(s32[7]{0:T(128)S(1)} %copy-done.32, ...), custom_call_target="tpu_custom_call" | custom-call | flops 9200000000 | bytes 1048576 | tf_op jit(solution)/shard_map/attn_grads/pallas_call | solution.py:190
  607.3 2.5 slice_bitcast_fusion
  610.9 2.7 multiply_add_fusion
  613.5 7.7 %collective-permute-start.42 = (bf16[96,768]{1,0:T(8,128)(2,1)}, bf16[96,768]{1,0:T(8,128)(2,1)}, u32[]{:S(2)}, u32[]{:S(2)}) collective-permute-start(bf16[96,768]{1,0:T(8,128)(2,1)} %get-tuple-element.185), channel_id=1, source_target_pairs={{0,8},{4,12},{8,0},{12,4},{16,24},{20,28},{24,16},{28,20},{1,9},{5... | collective-permute-start | bytes 442376 | tf_op jit(solution)/shard_map/ppermute | solution.py:852
  625.5 6.2 inputs_back.1
  632.5 5.2 all-to-all-start.9
  640.8 6.2 all-to-all-done.9
  (323 shorter events, 116.9 us)
Async XLA Ops:
  4.0 79.0 %all-to-all-start = ((bf16[8,3,96,512]{3,2,1,0:T(8,128)(2,1)}), bf16[8,3,96,512]{3,2,1,0:T(8,128)(2,1)}, u32[]{:S(2)}, u32[]{:S(2)}) async-start(bf16[8,3,96,512]{3,2,1,0:T(8,128)(2,1)} %pad_maximum_fusion.1), calls=%async_computation | async-start | bytes 4718592 | tf_op jit(solution)/shard_map/all_to_all | solution.py:923
  9.9 43.5 %collective-permute-start.1 = (bf16[512,768]{1,0:T(8,128)(2,1)S(1)}, bf16[512,768]{1,0:T(8,128)(2,1)S(1)}, u32[]{:S(2)}, u32[]{:S(2)}) collective-permute-start(bf16[512,768]{1,0:T(8,128)(2,1)S(1)} %multiply_convert_fusion.1.refs_0_.refs_2_), channel_id=1, source_target_pairs={{0,2},{2,0},{1,3},{3,1},{4,6},{6,4},{5,7},{7,5},{8,10},{10,8},{9,1... | collective-permute-start | bytes 2359304 | tf_op jit(solution)/shard_map/ppermute | solution.py:28
  54.9 36.2 %collective-permute-start = (bf16[512,768]{1,0:T(8,128)(2,1)S(1)}, bf16[512,768]{1,0:T(8,128)(2,1)}, u32[]{:S(2)}, u32[]{:S(2)}) collective-permute-start(bf16[512,768]{1,0:T(8,128)(2,1)S(1)} %multiply_convert_fusion.1.refs_0_.refs_2_), channel_id=1, source_target_pairs={{0,1},{1,0},{2,3},{3,2},{4,5},{5,4},{6,7},{7,6},{8,9},{9,8},{10,11... | collective-permute-start | bytes 2359304 | tf_op jit(solution)/shard_map/ppermute | solution.py:28
  58.9 31.6 %collective-permute-start.12 = (bf16[512,768]{1,0:T(8,128)(2,1)}, bf16[512,768]{1,0:T(8,128)(2,1)}, u32[]{:S(2)}, u32[]{:S(2)}) collective-permute-start(bf16[512,768]{1,0:T(8,128)(2,1)} %multiply_convert_fusion.refs_0_), channel_id=1, source_target_pairs={{0,2},{2,0},{1,3},{3,1},{4,6},{6,4},{5,7},{7,5},{8,10},{10,8},{9,1... | collective-permute-start | bytes 2359304 | tf_op jit(solution)/shard_map/ppermute | solution.py:28
  66.2 19.9 %collective-permute-start.7 = (bf16[96,768]{1,0:T(8,128)(2,1)S(1)}, bf16[96,768]{1,0:T(8,128)(2,1)S(1)}, u32[]{:S(2)}, u32[]{:S(2)}) collective-permute-start(bf16[96,768]{1,0:T(8,128)(2,1)S(1)} %pad_maximum_fusion.3.refs_4_), channel_id=1, source_target_pairs={{0,20},{4,16},{8,28},{12,24},{16,4},{20,0},{24,12},{28,8},{1,21},{... | collective-permute-start | bytes 442376 | tf_op jit(solution)/shard_map/ppermute | solution.py:852
  68.2 22.3 %collective-permute-start.8 = (bf16[96,768]{1,0:T(8,128)(2,1)S(1)}, bf16[96,768]{1,0:T(8,128)(2,1)S(1)}, u32[]{:S(2)}, u32[]{:S(2)}) collective-permute-start(bf16[96,768]{1,0:T(8,128)(2,1)S(1)} %pad_maximum_fusion.3.refs_4_), channel_id=1, source_target_pairs={{0,24},{4,28},{8,16},{12,20},{16,8},{20,12},{24,0},{28,4},{1,25},{... | collective-permute-start | bytes 442376 | tf_op jit(solution)/shard_map/ppermute | solution.py:852
  70.9 20.2 %collective-permute-start.9 = (bf16[96,768]{1,0:T(8,128)(2,1)S(1)}, bf16[96,768]{1,0:T(8,128)(2,1)}, u32[]{:S(2)}, u32[]{:S(2)}) collective-permute-start(bf16[96,768]{1,0:T(8,128)(2,1)S(1)} %pad_maximum_fusion.3.refs_4_), channel_id=1, source_target_pairs={{0,28},{4,24},{8,20},{12,16},{16,12},{20,8},{24,4},{28,0},{1,29},{... | collective-permute-start | bytes 442376 | tf_op jit(solution)/shard_map/ppermute | solution.py:852
  86.8 44.1 %collective-permute-start.11 = (bf16[512,768]{1,0:T(8,128)(2,1)}, bf16[512,768]{1,0:T(8,128)(2,1)}, u32[]{:S(2)}, u32[]{:S(2)}) collective-permute-start(bf16[512,768]{1,0:T(8,128)(2,1)} %multiply_convert_fusion.refs_0_), channel_id=1, source_target_pairs={{0,1},{1,0},{2,3},{3,2},{4,5},{5,4},{6,7},{7,6},{8,9},{9,8},{10,11... | collective-permute-start | bytes 2359304 | tf_op jit(solution)/shard_map/ppermute | solution.py:28
  90.4 56.4 %collective-permute-start.13 = (bf16[512,768]{1,0:T(8,128)(2,1)}, bf16[512,768]{1,0:T(8,128)(2,1)}, u32[]{:S(2)}, u32[]{:S(2)}) collective-permute-start(bf16[512,768]{1,0:T(8,128)(2,1)} %collective-permute-done.12.refs_2_), channel_id=1, source_target_pairs={{0,1},{1,0},{2,3},{3,2},{4,5},{5,4},{6,7},{7,6},{8,9},{9,8},{10,11... | collective-permute-start | bytes 2359304 | tf_op jit(solution)/shard_map/ppermute | solution.py:28
  91.1 55.7 %collective-permute-start.10 = (bf16[1,2,3,96,512]{4,3,2,1,0:T(8,128)(2,1)}, bf16[1,2,3,96,512]{4,3,2,1,0:T(8,128)(2,1)}, u32[]{:S(2)}, u32[]{:S(2)}) collective-permute-start(bf16[1,2,3,96,512]{4,3,2,1,0:T(8,128)(2,1)} %get-tuple-element.272), channel_id=1, source_target_pairs={{0,16},{16,0},{1,17},{17,1},{2,18},{18,2},{3,19},{19,3},{4,20},{20... | collective-permute-start | bytes 1769480 | tf_op jit(solution)/shard_map/ppermute | solution.py:28
  118.7 12.2 %collective-permute-start.15 = (bf16[768,192]{1,0:T(8,128)(2,1)S(1)}, bf16[768,192]{1,0:T(8,128)(2,1)}, u32[]{:S(2)}, u32[]{:S(2)}) collective-permute-start(bf16[768,192]{1,0:T(8,128)(2,1)S(1)} %get-tuple-element.117.p0), channel_id=1, source_target_pairs={{0,2},{2,0},{1,3},{3,1},{4,6},{6,4},{5,7},{7,5},{8,10},{10,8},{9,1... | collective-permute-start | bytes 884744 | tf_op jit(solution)/shard_map/ppermute | solution.py:28
  127.3 42.4 %collective-permute-start.14 = (bf16[768,192]{1,0:T(8,128)(2,1)S(1)}, bf16[768,192]{1,0:T(8,128)(2,1)}, u32[]{:S(2)}, u32[]{:S(2)}) collective-permute-start(bf16[768,192]{1,0:T(8,128)(2,1)S(1)} %get-tuple-element.117.p0), channel_id=1, source_target_pairs={{0,1},{1,0},{2,3},{3,2},{4,5},{5,4},{6,7},{7,6},{8,9},{9,8},{10,11... | collective-permute-start | bytes 884744 | tf_op jit(solution)/shard_map/ppermute | solution.py:28
  130.9 38.8 %collective-permute-start.16 = (bf16[768,192]{1,0:T(8,128)(2,1)}, bf16[768,192]{1,0:T(8,128)(2,1)}, u32[]{:S(2)}, u32[]{:S(2)}) collective-permute-start(bf16[768,192]{1,0:T(8,128)(2,1)} %collective-permute-done.15.p2), channel_id=1, source_target_pairs={{0,1},{1,0},{2,3},{3,2},{4,5},{5,4},{6,7},{7,6},{8,9},{9,8},{10,11... | collective-permute-start | bytes 884744 | tf_op jit(solution)/shard_map/ppermute | solution.py:28
  130.9 45.9 %collective-permute-start.17 = (bf16[1,2,3,96,512]{4,3,2,1,0:T(8,128)(2,1)}, bf16[1,2,3,96,512]{4,3,2,1,0:T(8,128)(2,1)}, u32[]{:S(2)}, u32[]{:S(2)}) collective-permute-start(bf16[1,2,3,96,512]{4,3,2,1,0:T(8,128)(2,1)} %get-tuple-element.271), channel_id=1, source_target_pairs={{0,16},{16,0},{1,17},{17,1},{2,18},{18,2},{3,19},{19,3},{4,20},{20... | collective-permute-start | bytes 1769480 | tf_op jit(solution)/shard_map/ppermute | solution.py:28
  146.8 22.9 %all-to-all-start.1 = ((bf16[4,192,512]{2,1,0:T(8,128)(2,1)}), bf16[4,192,512]{2,1,0:T(8,128)(2,1)}, u32[]{:S(2)}, u32[]{:S(2)}) async-start(bf16[4,192,512]{2,1,0:T(8,128)(2,1)} %copy-done.14), calls=%async_computation.1 | async-start | bytes 1572864 | tf_op jit(solution)/shard_map/all_to_all | solution.py:952
  176.8 22.0 %collective-permute-start.19 = (bf16[512,896]{1,0:T(8,128)(2,1)S(1)}, bf16[512,896]{1,0:T(8,128)(2,1)S(1)}, u32[]{:S(2)}, u32[]{:S(2)}) collective-permute-start(bf16[512,896]{1,0:T(8,128)(2,1)S(1)} %get-tuple-element.124.refs_0_), channel_id=1, source_target_pairs={{0,2},{2,0},{1,3},{3,1},{4,6},{6,4},{5,7},{7,5},{8,10},{10,8},{9,1... | collective-permute-start | bytes 2752520 | tf_op jit(solution)/shard_map/ppermute | solution.py:28
  178.2 48.9 %all-to-all-start.2 = ((bf16[4,192,768]{2,1,0:T(8,128)(2,1)}), bf16[4,192,768]{2,1,0:T(8,128)(2,1)}, u32[]{:S(2)}, u32[]{:S(2)}) async-start(bf16[4,192,768]{2,1,0:T(8,128)(2,1)} %bitcast.18), calls=%async_computation.2 | async-start | bytes 2359296 | tf_op jit(solution)/shard_map/all_to_all | solution.py:968
  182.5 43.7 %collective-permute-start.18 = (bf16[512,896]{1,0:T(8,128)(2,1)S(1)}, bf16[512,896]{1,0:T(8,128)(2,1)S(1)}, u32[]{:S(2)}, u32[]{:S(2)}) collective-permute-start(bf16[512,896]{1,0:T(8,128)(2,1)S(1)} %get-tuple-element.124.refs_0_), channel_id=1, source_target_pairs={{0,1},{1,0},{2,3},{3,2},{4,5},{5,4},{6,7},{7,6},{8,9},{9,8},{10,11... | collective-permute-start | bytes 2752520 | tf_op jit(solution)/shard_map/ppermute | solution.py:28
  198.8 28.3 %collective-permute-start.20 = (bf16[512,896]{1,0:T(8,128)(2,1)S(1)}, bf16[512,896]{1,0:T(8,128)(2,1)}, u32[]{:S(2)}, u32[]{:S(2)}) collective-permute-start(bf16[512,896]{1,0:T(8,128)(2,1)S(1)} %collective-permute-done.19.refs_2_), channel_id=1, source_target_pairs={{0,1},{1,0},{2,3},{3,2},{4,5},{5,4},{6,7},{7,6},{8,9},{9,8},{10,11... | collective-permute-start | bytes 2752520 | tf_op jit(solution)/shard_map/ppermute | solution.py:28
  199.6 26.6 %collective-permute-start.21 = (bf16[1,2,3,96,512]{4,3,2,1,0:T(8,128)(2,1)}, bf16[1,2,3,96,512]{4,3,2,1,0:T(8,128)(2,1)}, u32[]{:S(2)}, u32[]{:S(2)}) collective-permute-start(bf16[1,2,3,96,512]{4,3,2,1,0:T(8,128)(2,1)} %get-tuple-element.270), channel_id=1, source_target_pairs={{0,16},{16,0},{1,17},{17,1},{2,18},{18,2},{3,19},{19,3},{4,20},{20... | collective-permute-start | bytes 1769480 | tf_op jit(solution)/shard_map/ppermute | solution.py:28
  234.1 57.7 %all-to-all-start.3 = ((bf16[4,192,896]{2,1,0:T(8,128)(2,1)}), bf16[4,192,896]{2,1,0:T(8,128)(2,1)S(1)}, u32[]{:S(2)}, u32[]{:S(2)}) async-start(bf16[4,192,896]{2,1,0:T(8,128)(2,1)} %bitcast.21), calls=%async_computation.3 | async-start | bytes 2752512 | tf_op jit(solution)/shard_map/all_to_all | solution.py:977
  239.3 21.0 %collective-permute-start.23 = (bf16[768,576]{0,1:T(8,128)(2,1)}, bf16[768,576]{0,1:T(8,128)(2,1)S(1)}, u32[]{:S(2)}, u32[]{:S(2)}) collective-permute-start(bf16[768,576]{0,1:T(8,128)(2,1)} %copy.90), channel_id=1, source_target_pairs={{0,2},{2,0},{1,3},{3,1},{4,6},{6,4},{5,7},{7,5},{8,10},{10,8},{9,1... | collective-permute-start | bytes 2654216 | tf_op jit(solution)/shard_map/ppermute | solution.py:28
  240.7 49.3 %collective-permute-start.22 = (bf16[768,576]{0,1:T(8,128)(2,1)}, bf16[768,576]{0,1:T(8,128)(2,1)S(1)}, u32[]{:S(2)}, u32[]{:S(2)}) collective-permute-start(bf16[768,576]{0,1:T(8,128)(2,1)} %copy.90), channel_id=1, source_target_pairs={{0,1},{1,0},{2,3},{3,2},{4,5},{5,4},{6,7},{7,6},{8,9},{9,8},{10,11... | collective-permute-start | bytes 2654216 | tf_op jit(solution)/shard_map/ppermute | solution.py:28
  260.3 31.5 %collective-permute-start.24 = (bf16[768,576]{0,1:T(8,128)(2,1)S(1)}, bf16[768,576]{0,1:T(8,128)(2,1)}, u32[]{:S(2)}, u32[]{:S(2)}) collective-permute-start(bf16[768,576]{0,1:T(8,128)(2,1)S(1)} %collective-permute-done.23), channel_id=1, source_target_pairs={{0,1},{1,0},{2,3},{3,2},{4,5},{5,4},{6,7},{7,6},{8,9},{9,8},{10,11... | collective-permute-start | bytes 2654216 | tf_op jit(solution)/shard_map/ppermute | solution.py:28
  261.6 28.4 %collective-permute-start.25 = (bf16[1,2,3,96,512]{4,3,2,1,0:T(8,128)(2,1)S(1)}, bf16[1,2,3,96,512]{4,3,2,1,0:T(8,128)(2,1)S(1)}, u32[]{:S(2)}, u32[]{:S(2)}) collective-permute-start(bf16[1,2,3,96,512]{4,3,2,1,0:T(8,128)(2,1)S(1)} %copy-done.64), channel_id=1, source_target_pairs={{0,16},{16,0},{1,17},{17,1},{2,18},{18,2},{3,19},{19,3},{4,20},{20... | collective-permute-start | bytes 1769480 | tf_op jit(solution)/shard_map/ppermute | solution.py:28
  337.6 33.5 %all-to-all-start.4 = ((bf16[4,192,896]{2,1,0:T(8,128)(2,1)}), bf16[4,192,896]{2,1,0:T(8,128)(2,1)S(1)}, u32[]{:S(2)}, u32[]{:S(2)}) async-start(bf16[4,192,896]{2,1,0:T(8,128)(2,1)} %bitcast.25), calls=%async_computation.4 | async-start | bytes 2752512 | tf_op jit(solution)/shard_map/all_to_all | solution.py:1006
  342.0 27.3 %collective-permute-start.30 = (bf16[1,2,3,96,512]{4,3,2,1,0:T(8,128)(2,1)}, bf16[1,2,3,96,512]{4,3,2,1,0:T(8,128)(2,1)S(1)}, u32[]{:S(2)}, u32[]{:S(2)}) collective-permute-start(bf16[1,2,3,96,512]{4,3,2,1,0:T(8,128)(2,1)} %get-tuple-element.140), channel_id=1, source_target_pairs={{0,16},{16,0},{1,17},{17,1},{2,18},{18,2},{3,19},{19,3},{4,20},{20... | collective-permute-start | bytes 1769480 | tf_op jit(solution)/shard_map/ppermute | solution.py:28
  379.0 37.3 %all-to-all-start.5 = ((bf16[4,192,768]{2,1,0:T(8,128)(2,1)}), bf16[4,192,768]{2,1,0:T(8,128)(2,1)S(1)}, u32[]{:S(2)}, u32[]{:S(2)}) async-start(bf16[4,192,768]{2,1,0:T(8,128)(2,1)} %bitcast.88), calls=%async_computation.5 | async-start | bytes 2359296 | tf_op jit(solution)/shard_map/all_to_all | solution.py:1013
  386.4 30.9 %collective-permute-start.32 = (bf16[512,896]{1,0:T(8,128)(2,1)}, bf16[512,896]{1,0:T(8,128)(2,1)S(1)}, u32[]{:S(2)}, u32[]{:S(2)}) collective-permute-start(bf16[512,896]{1,0:T(8,128)(2,1)} %get-tuple-element.256), channel_id=1, source_target_pairs={{0,2},{2,0},{1,3},{3,1},{4,6},{6,4},{5,7},{7,5},{8,10},{10,8},{9,1... | collective-permute-start | bytes 2752520 | tf_op jit(solution)/shard_map/ppermute | solution.py:28
  387.8 28.4 %collective-permute-start.33 = (bf16[1,2,3,96,512]{4,3,2,1,0:T(8,128)(2,1)}, bf16[1,2,3,96,512]{4,3,2,1,0:T(8,128)(2,1)S(1)}, u32[]{:S(2)}, u32[]{:S(2)}) collective-permute-start(bf16[1,2,3,96,512]{4,3,2,1,0:T(8,128)(2,1)} %get-tuple-element.145), channel_id=1, source_target_pairs={{0,16},{16,0},{1,17},{17,1},{2,18},{18,2},{3,19},{19,3},{4,20},{20... | collective-permute-start | bytes 1769480 | tf_op jit(solution)/shard_map/ppermute | solution.py:28
  424.9 96.0 %collective-permute-start.39 = (bf16[2,512,768]{2,1,0:T(8,128)(2,1)}, bf16[2,512,768]{2,1,0:T(8,128)(2,1)}, u32[]{:S(2)}, u32[]{:S(2)}) collective-permute-start(bf16[2,512,768]{2,1,0:T(8,128)(2,1)} %get-tuple-element.157), channel_id=1, source_target_pairs={{0,1},{1,0},{2,3},{3,2},{4,5},{5,4},{6,7},{7,6},{8,9},{9,8},{10,11... | collective-permute-start | bytes 4718600 | tf_op jit(solution)/shard_map/ppermute | solution.py:28
  442.8 19.5 %collective-permute-start.35 = (bf16[512,768]{1,0:T(8,128)(2,1)}, bf16[512,768]{1,0:T(8,128)(2,1)}, u32[]{:S(2)}, u32[]{:S(2)}) collective-permute-start(bf16[512,768]{1,0:T(8,128)(2,1)} %get-tuple-element.164.refs_6_), channel_id=1, source_target_pairs={{0,2},{2,0},{1,3},{3,1},{4,6},{6,4},{5,7},{7,5},{8,10},{10,8},{9,1... | collective-permute-start | bytes 2359304 | tf_op jit(solution)/shard_map/ppermute | solution.py:28
  442.9 81.4 %collective-permute-start.34 = (bf16[512,768]{1,0:T(8,128)(2,1)}, bf16[512,768]{1,0:T(8,128)(2,1)}, u32[]{:S(2)}, u32[]{:S(2)}) collective-permute-start(bf16[512,768]{1,0:T(8,128)(2,1)} %get-tuple-element.164.refs_6_), channel_id=1, source_target_pairs={{0,1},{1,0},{2,3},{3,2},{4,5},{5,4},{6,7},{7,6},{8,9},{9,8},{10,11... | collective-permute-start | bytes 2359304 | tf_op jit(solution)/shard_map/ppermute | solution.py:28
  462.3 62.0 %collective-permute-start.36 = (bf16[512,768]{1,0:T(8,128)(2,1)}, bf16[512,768]{1,0:T(8,128)(2,1)}, u32[]{:S(2)}, u32[]{:S(2)}) collective-permute-start(bf16[512,768]{1,0:T(8,128)(2,1)} %collective-permute-done.35.refs_8_), channel_id=1, source_target_pairs={{0,1},{1,0},{2,3},{3,2},{4,5},{5,4},{6,7},{7,6},{8,9},{9,8},{10,11... | collective-permute-start | bytes 2359304 | tf_op jit(solution)/shard_map/ppermute | solution.py:28
  463.1 61.2 %collective-permute-start.37 = (bf16[1,2,3,96,512]{4,3,2,1,0:T(8,128)(2,1)}, bf16[1,2,3,96,512]{4,3,2,1,0:T(8,128)(2,1)}, u32[]{:S(2)}, u32[]{:S(2)}) collective-permute-start(bf16[1,2,3,96,512]{4,3,2,1,0:T(8,128)(2,1)} %get-tuple-element.153), channel_id=1, source_target_pairs={{0,16},{16,0},{1,17},{17,1},{2,18},{18,2},{3,19},{19,3},{4,20},{20... | collective-permute-start | bytes 1769480 | tf_op jit(solution)/shard_map/ppermute | solution.py:28
  463.1 61.2 %collective-permute-start.38 = (bf16[1,2,3,96,512]{4,3,2,1,0:T(8,128)(2,1)}, bf16[1,2,3,96,512]{4,3,2,1,0:T(8,128)(2,1)}, u32[]{:S(2)}, u32[]{:S(2)}) collective-permute-start(bf16[1,2,3,96,512]{4,3,2,1,0:T(8,128)(2,1)} %get-tuple-element.154), channel_id=1, source_target_pairs={{0,16},{16,0},{1,17},{17,1},{2,18},{18,2},{3,19},{19,3},{4,20},{20... | collective-permute-start | bytes 1769480 | tf_op jit(solution)/shard_map/ppermute | solution.py:28
  466.2 53.7 %all-to-all-start.6 = ((f32[32,1,768]{2,1,0:T(1,128)}), f32[32,1,768]{2,1,0:T(1,128)}, u32[]{:S(2)}, u32[]{:S(2)}) async-start(f32[32,1,768]{2,1,0:T(1,128)} %copy.96), calls=%async_computation.6 | async-start | bytes 196608 | tf_op jit(solution)/shard_map/all_to_all | solution.py:1024
  528.8 48.0 %all-to-all-start.7 = ((bf16[8,3,96,512]{3,2,1,0:T(8,128)(2,1)}), bf16[8,3,96,512]{3,2,1,0:T(8,128)(2,1)S(1)}, u32[]{:S(2)}, u32[]{:S(2)}) async-start(bf16[8,3,96,512]{3,2,1,0:T(8,128)(2,1)} %bitcast.85), calls=%async_computation.7 | async-start | bytes 4718592 | tf_op jit(solution)/shard_map/all_to_all | solution.py:1049
  532.6 44.2 %collective-permute-start.40 = (bf16[512,768]{1,0:T(8,128)(2,1)}, bf16[512,768]{1,0:T(8,128)(2,1)}, u32[]{:S(2)}, u32[]{:S(2)}) collective-permute-start(bf16[512,768]{1,0:T(8,128)(2,1)} %get-tuple-element.171), channel_id=1, source_target_pairs={{0,2},{2,0},{1,3},{3,1},{4,6},{6,4},{5,7},{7,5},{8,10},{10,8},{9,1... | collective-permute-start | bytes 2359304 | tf_op jit(solution)/shard_map/ppermute | solution.py:28
  578.2 44.9 %all-to-all-start.8 = ((bf16[4,576,512]{2,1,0:T(8,128)(2,1)}), bf16[4,576,512]{2,1,0:T(8,128)(2,1)}, u32[]{:S(2)}, u32[]{:S(2)}) async-start(bf16[4,576,512]{2,1,0:T(8,128)(2,1)} %bitcast.42.refs_0_), calls=%async_computation.8 | async-start | bytes 4718592 | tf_op jit(solution)/shard_map/all_to_all | solution.py:1057
  599.8 13.8 %collective-permute-start.47 = (bf16[96,768]{1,0:T(8,128)(2,1)S(1)}, bf16[96,768]{1,0:T(8,128)(2,1)S(1)}, u32[]{:S(2)}, u32[]{:S(2)}) collective-permute-start(bf16[96,768]{1,0:T(8,128)(2,1)S(1)} %get-tuple-element.190), channel_id=1, source_target_pairs={{0,28},{4,24},{8,20},{12,16},{16,12},{20,8},{24,4},{28,0},{1,29},{... | collective-permute-start | bytes 442376 | tf_op jit(solution)/shard_map/ppermute | solution.py:852
  602.0 19.2 %collective-permute-start.46 = (bf16[96,768]{1,0:T(8,128)(2,1)S(1)}, bf16[96,768]{1,0:T(8,128)(2,1)S(1)}, u32[]{:S(2)}, u32[]{:S(2)}) collective-permute-start(bf16[96,768]{1,0:T(8,128)(2,1)S(1)} %get-tuple-element.189), channel_id=1, source_target_pairs={{0,24},{4,28},{8,16},{12,20},{16,8},{20,12},{24,0},{28,4},{1,25},{... | collective-permute-start | bytes 442376 | tf_op jit(solution)/shard_map/ppermute | solution.py:852
  603.9 33.8 %collective-permute-start.45 = (bf16[96,768]{1,0:T(8,128)(2,1)}, bf16[96,768]{1,0:T(8,128)(2,1)}, u32[]{:S(2)}, u32[]{:S(2)}) collective-permute-start(bf16[96,768]{1,0:T(8,128)(2,1)} %get-tuple-element.188), channel_id=1, source_target_pairs={{0,20},{4,16},{8,28},{12,24},{16,4},{20,0},{24,12},{28,8},{1,21},{... | collective-permute-start | bytes 442376 | tf_op jit(solution)/shard_map/ppermute | solution.py:852
  603.9 33.8 %collective-permute-start.44 = (bf16[96,768]{1,0:T(8,128)(2,1)}, bf16[96,768]{1,0:T(8,128)(2,1)}, u32[]{:S(2)}, u32[]{:S(2)}) collective-permute-start(bf16[96,768]{1,0:T(8,128)(2,1)} %get-tuple-element.187), channel_id=1, source_target_pairs={{0,16},{4,20},{8,24},{12,28},{16,0},{20,4},{24,8},{28,12},{1,17},{... | collective-permute-start | bytes 442376 | tf_op jit(solution)/shard_map/ppermute | solution.py:852
  606.3 31.5 %collective-permute-start.43 = (bf16[96,768]{1,0:T(8,128)(2,1)}, bf16[96,768]{1,0:T(8,128)(2,1)}, u32[]{:S(2)}, u32[]{:S(2)}) collective-permute-start(bf16[96,768]{1,0:T(8,128)(2,1)} %get-tuple-element.186), channel_id=1, source_target_pairs={{0,12},{4,8},{8,4},{12,0},{16,28},{20,24},{24,20},{28,16},{1,13},{... | collective-permute-start | bytes 442376 | tf_op jit(solution)/shard_map/ppermute | solution.py:852
  613.5 24.3 %collective-permute-start.42 = (bf16[96,768]{1,0:T(8,128)(2,1)}, bf16[96,768]{1,0:T(8,128)(2,1)}, u32[]{:S(2)}, u32[]{:S(2)}) collective-permute-start(bf16[96,768]{1,0:T(8,128)(2,1)} %get-tuple-element.185), channel_id=1, source_target_pairs={{0,8},{4,12},{8,0},{12,4},{16,24},{20,28},{24,16},{28,20},{1,9},{5... | collective-permute-start | bytes 442376 | tf_op jit(solution)/shard_map/ppermute | solution.py:852
  621.9 15.9 %collective-permute-start.41 = (bf16[96,768]{1,0:T(8,128)(2,1)}, bf16[96,768]{1,0:T(8,128)(2,1)}, u32[]{:S(2)}, u32[]{:S(2)}) collective-permute-start(bf16[96,768]{1,0:T(8,128)(2,1)} %get-tuple-element.184), channel_id=1, source_target_pairs={{0,4},{4,0},{8,12},{12,8},{16,20},{20,16},{24,28},{28,24},{1,5},{5... | collective-permute-start | bytes 442376 | tf_op jit(solution)/shard_map/ppermute | solution.py:852
  632.5 14.5 %all-to-all-start.9 = ((f32[32,1,1536]{2,1,0:T(1,128)}), f32[32,1,1536]{2,1,0:T(1,128)S(1)}, u32[]{:S(2)}, u32[]{:S(2)}) async-start(f32[32,1,1536]{2,1,0:T(1,128)} %broadcast_in_dim.5), calls=%async_computation.9 | async-start | bytes 393216 | tf_op jit(solution)/shard_map/all_to_all | solution.py:848
  (98 other events, 1094.4 us)

commit v3 on v2

--- a/solution.py
+++ b/solution.py
@@ -12,7 +12,8 @@
 MAXLEN = 768
 LOW = 4
 SHARDS = 8
-BOUNDS = 4
+LOW_PLACE = 4
+BOUNDS = 5
 EPSILON = 1e-06
 PRECISE = lax.Precision.HIGHEST
 NEGATIVE = -1e30
@@ -66,7 +67,7 @@
 
 def attend_kernel(block, pad, scalars, *refs):
     pieces, refs = refs[:4], refs[4:]
-    shards, refs = refs[:SHARDS], refs[SHARDS:]
+    shards, refs = refs[:LOW], refs[LOW:]
     out_ref, lse_ref, qkv_ref, weight_ref, last_ref, key_rows, value_pad, full = refs
     group = qkv_ref.shape[1]
     window = pad + block
@@ -76,10 +77,10 @@
 
     @pl.when(head == 0)
     def _():
-        rows = shards[0].shape[0]
+        rows = shards[0].shape[1]
         for r in range(SHARDS):
             place = pl.multiple_of((scalars[0] ^ r) * rows, rows)
-            full[pl.ds(place, rows), :] = shards[r][...]
+            full[pl.ds(place, rows), :] = shards[r % LOW][r // LOW]
         weight_ref[...] = full[:, : 3 * inner]
         last_ref[...] = full[:, 3 * inner :]
         turned = full[:, : 3 * inner].T
@@ -136,7 +137,7 @@
             grid=(heads,),
             in_specs=[
                 *[whole((rows, width)) for _ in range(4)],
-                *[whole(shards[0].shape) for _ in range(SHARDS)],
+                *[whole(shards[0].shape) for _ in range(LOW)],
             ],
             out_specs=[
                 pl.BlockSpec((4, HEAD, rows), lambda h, _: (0, h, 0)),
@@ -167,7 +168,7 @@
 def attn_grads_kernel(scalars, *refs):
     grad_qkv, mixed, refs = refs[0], refs[1], refs[2:]
     tokens, grads, refs = refs[:4], refs[4:8], refs[8:]
-    outs, (total,) = refs[:SHARDS], refs[SHARDS:]
+    outs, (total,) = refs[:2], refs[2:]
     inner3 = grad_qkv.shape[1]
     first, second = 0.0, 0.0
     for r in range(4):
@@ -176,10 +177,10 @@
         second += jnp.dot(mixed[j], grads[r][...], preferred_element_type=F32)
     total[:, :inner3] = first.T.astype(BF16)
     total[:, inner3:] = second.T.astype(BF16)
-    rows = outs[0].shape[0]
+    rows = outs[0].shape[1]
     for r in range(SHARDS):
         place = pl.multiple_of((scalars[0] ^ r) * rows, rows)
-        outs[r][...] = total[pl.ds(place, rows), :]
+        outs[r // LOW][r % LOW] = total[pl.ds(place, rows), :]
 
 
 def attn_grads(grad_qkv, mixed, tokens, grads, scalars):
@@ -190,8 +191,8 @@
     return pl.pallas_call(
         attn_grads_kernel,
         in_specs=[pl.BlockSpec(memory_space=pltpu.SMEM)] + [whole] * 10,
-        out_specs=[whole] * SHARDS,
-        out_shape=[jax.ShapeDtypeStruct((rows, columns), BF16)] * SHARDS,
+        out_specs=[whole] * 2,
+        out_shape=[jax.ShapeDtypeStruct((LOW, rows, columns), BF16)] * 2,
         scratch_shapes=[pltpu.VMEM((width, columns), BF16)],
         compiler_params=pltpu.CompilerParams(vmem_limit_bytes=48 * 2**20),
         cost_estimate=cost_of(8),
@@ -199,27 +200,40 @@
     )(scalars, grad_qkv, mixed, *tokens, *grads)
 
 
-def attend_back_kernel(
-    block, pad, scalars, q_ref, k_ref, v_ref, g_ref, lse_ref, out_ref,
-    key_rows, value_rows, key_pad, grad_key, grad_value,
-):
-    group = q_ref.shape[1]
+def attend_back_kernel(block, pad, scalars, qkv_ref, lse_ref, last_ref, *refs):
+    pieces, refs = refs[:4], refs[4:]
+    out_ref, grad_mixed, key_rows, value_rows, key_pad, grad_key, grad_value = refs
+    group = qkv_ref.shape[1]
+    inner_rows = qkv_ref.shape[0] // 3
     window = pad + block
     quarter = group // 4
     contract_last = (((1,), (1,)), ((), ()))
+    head = pl.program_id(0)
+
+    @pl.when(head == 0)
+    def _():
+        turned = last_ref[...].T
+        for r in range(4):
+            place = pl.multiple_of((scalars[1] ^ r) * quarter, quarter)
+            grad_mixed[:, pl.ds(place, quarter)] = lax.dot_general(
+                turned, pieces[r][...], contract_last, preferred_element_type=F32
+            ).astype(BF16)
+
+    first_row = pl.multiple_of(head * HEAD, HEAD)
+    keys = qkv_ref[pl.ds(inner_rows + first_row, HEAD), :]
     key_rows[pl.ds(0, pad), :] = jnp.zeros((pad, HEAD), BF16)
     value_rows[pl.ds(0, pad), :] = jnp.zeros((pad, HEAD), BF16)
     key_pad[:, pl.ds(0, pad)] = jnp.zeros((HEAD, pad), BF16)
-    key_rows[pl.ds(pad, group), :] = k_ref[...].T
-    value_rows[pl.ds(pad, group), :] = v_ref[...].T
-    key_pad[:, pl.ds(pad, group)] = k_ref[...]
+    key_rows[pl.ds(pad, group), :] = keys.T
+    value_rows[pl.ds(pad, group), :] = qkv_ref[pl.ds(2 * inner_rows + first_row, HEAD), :].T
+    key_pad[:, pl.ds(pad, group)] = keys
     grad_key[...] = jnp.zeros_like(grad_key)
     grad_value[...] = jnp.zeros_like(grad_value)
 
     def one(i, carry):
         first = pl.multiple_of(i * block, block)
-        query = q_ref[:, pl.ds(first, block)]
-        grad = g_ref[:, pl.ds(first, block)]
+        query = qkv_ref[pl.ds(first_row, HEAD), pl.ds(first, block)]
+        grad = grad_mixed[pl.ds(first_row, HEAD), pl.ds(first, block)]
         scores = jnp.dot(key_rows[pl.ds(first, window), :], query, preferred_element_type=F32)
         allowed = scores_mask(first - pad, first, window, block, scalars)
         exponent = jnp.where(allowed, scores * 0.125 - lse_ref[0, :, pl.ds(first, block)], NEGATIVE)
@@ -247,23 +261,29 @@
         out_ref[j, 2] = grad_value[:, pl.ds(pad + j * quarter, quarter)].astype(BF16)
 
 
-def attend_back(qkv, grad_mixed, scalars, lse, heads):
+def attend_back(scalars, qkv, lse, last, pieces, heads):
     group = qkv.shape[1]
     block = 256
+
+    def whole(shape):
+        return pl.BlockSpec(
+            shape, lambda i, _: (0,) * len(shape), pipeline_mode=pl.Buffered(1)
+        )
+
     return pl.pallas_call(
         functools.partial(attend_back_kernel, block, MAXLEN),
         grid_spec=pltpu.PrefetchScalarGridSpec(
             num_scalar_prefetch=1,
             grid=(heads,),
             in_specs=[
-                pl.BlockSpec((HEAD, group), lambda h, _: (h, 0)),
-                pl.BlockSpec((HEAD, group), lambda h, _: (h + heads, 0)),
-                pl.BlockSpec((HEAD, group), lambda h, _: (h + 2 * heads, 0)),
-                pl.BlockSpec((HEAD, group), lambda h, _: (h, 0)),
+                whole(qkv.shape),
                 pl.BlockSpec((1, 1, group), lambda h, _: (h, 0, 0)),
+                whole(last.shape),
+                *[whole(item.shape) for item in pieces],
             ],
             out_specs=pl.BlockSpec((4, 3, HEAD, group // 4), lambda h, _: (0, 0, h, 0)),
             scratch_shapes=[
+                pltpu.VMEM((heads * HEAD, group), BF16),
                 pltpu.VMEM((MAXLEN + group, HEAD), BF16),
                 pltpu.VMEM((MAXLEN + group, HEAD), BF16),
                 pltpu.VMEM((HEAD, MAXLEN + group), BF16),
@@ -273,9 +293,9 @@
         ),
         out_shape=jax.ShapeDtypeStruct((4, 3, heads * HEAD, group // 4), BF16),
         compiler_params=pltpu.CompilerParams(vmem_limit_bytes=48 * 2**20),
-        cost_estimate=cost_of(31),
+        cost_estimate=cost_of(34),
         name="attend_back",
-    )(scalars, qkv, qkv, qkv, grad_mixed, lse)
+    )(scalars, qkv, lse, last, *pieces)
 
 
 def inputs_back_kernel(scalars, grads, p0, p1, p2, p3, x_ref, gain_ref, hidden_ref, out_ref, sum_ref):
@@ -290,18 +310,34 @@
     through = total * gain_ref[...]
     inner = jnp.mean(through * x, axis=1, keepdims=True)
     out_ref[...] = hidden_ref[...] + scale * through - (scale * scale * scale * inner) * x
-    sum_ref[...] = jnp.sum(total * x * scale, axis=0, keepdims=True)
+    sum_ref[0] = jnp.sum(total * x * scale, axis=0, keepdims=True)
 
 
 def inputs_back(scalars, grads, weights, x, gain, grad_hidden):
-    whole = pl.BlockSpec(memory_space=pltpu.VMEM)
+    rows, width = x.shape
+    block = rows // 2
+
+    def whole(shape):
+        return pl.BlockSpec(shape, lambda i, _: (0,) * len(shape), pipeline_mode=pl.Buffered(1))
+
+    part = pl.BlockSpec((block, width), lambda i, _: (i, 0))
     return pl.pallas_call(
         inputs_back_kernel,
-        in_specs=[pl.BlockSpec(memory_space=pltpu.SMEM)] + [whole] * 8,
-        out_specs=[whole] * 2,
+        grid_spec=pltpu.PrefetchScalarGridSpec(
+            num_scalar_prefetch=1,
+            grid=(2,),
+            in_specs=[
+                pl.BlockSpec((4, grads.shape[1], block), lambda i, _: (0, 0, i)),
+                *[whole(item.shape) for item in weights],
+                part,
+                whole(gain.shape),
+                part,
+            ],
+            out_specs=[part, pl.BlockSpec((1, 1, width), lambda i, _: (i, 0, 0))],
+        ),
         out_shape=[
             jax.ShapeDtypeStruct(x.shape, F32),
-            jax.ShapeDtypeStruct((1, x.shape[1]), F32),
+            jax.ShapeDtypeStruct((2, 1, width), F32),
         ],
         compiler_params=pltpu.CompilerParams(vmem_limit_bytes=48 * 2**20),
         cost_estimate=cost_of(6),
@@ -310,44 +346,43 @@
 
 
 def expert_kernel(
-    kinds, scalars, x_own, x_core, g_own, g_core, w_own, *refs
+    kinds, scalars, w_gate, w_other, *refs
 ):
-    w_far, refs = refs[:LOW], refs[LOW:]
-    back_own, back_send, feed_own, feed_send, grads_own, *refs = refs
-    grads_far, refs = refs[:LOW], refs[LOW:]
-    x_all, g_all, x_t, g_t, weights, hidden, acc_feed, acc_back = refs
-    slots, width = g_own.shape
+    x_blocks, g_blocks, refs = refs[: 2 * LOW], refs[2 * LOW : 4 * LOW], refs[4 * LOW :]
+    back_own, back_send, feed_own, feed_send, grads_gate, grads_other, *refs = refs
+    x_all, g_all, x_t, g_t, weights, hidden, acc_feed, acc_back, scales, plain = refs
+    slots, width = feed_own.shape
+    block = slots // LOW
     half = width // 2
     step = pl.program_id(0)
-    near = pl.multiple_of(scalars[0] * half, half)
-    far = pl.multiple_of((1 - scalars[0]) * half, half)
     contract_last = (((1,), (1,)), ((), ()))
     units = weights.shape[2]
 
     def weight_column(x_ref):
         extra = x_ref[:, width:].astype(F32)
         lanes = lax.broadcasted_iota(jnp.int32, extra.shape, 1)
-        named = (lanes == scalars[1]) | (lanes == scalars[1] + kinds)
+        named = (lanes == scalars[0]) | (lanes == scalars[0] + kinds)
         return jnp.sum(jnp.where(named, extra, 0.0), axis=1, keepdims=True)
 
     @pl.when(step == 0)
     def _():
-        for part, (x_ref, g_ref) in enumerate(((x_own, g_own), (x_core, g_core))):
-            rows = pl.ds(part * slots, slots)
-            x = x_ref[:, :width]
-            grad = (g_ref[...].astype(F32) * weight_column(x_ref)).astype(BF16)
-            x_all[rows, :] = x
-            g_all[rows, :] = grad
-            x_t[:, rows] = x.T
-            g_t[:, rows] = grad.T
+        for i in range(2 * LOW):
+            rows = pl.ds(i * block, block)
+            scale = weight_column(x_blocks[i])
+            scales[rows, :] = jnp.broadcast_to(scale, (block, 128))
+            plain[rows, :] = g_blocks[i][...]
+            x_all[rows, :] = x_blocks[i][:, :width]
+            g_all[rows, :] = (g_blocks[i][...].astype(F32) * scale).astype(BF16)
+        x_t[...] = x_all[...].T
+        g_t[...] = g_all[...].T
         acc_feed[...] = jnp.zeros_like(acc_feed)
         acc_back[...] = jnp.zeros_like(acc_back)
 
-    for k in range(3):
-        weights[k, pl.ds(near, half), :] = w_own[:, 0, k].reshape(half, units)
-        for i in range(LOW):
-            rows = half // LOW
-            weights[k, pl.ds(pl.multiple_of(far + i * rows, rows), rows), :] = w_far[i][0, 0, k]
+    for i in range(2):
+        rows = pl.ds(i * half, half)
+        weights[0, rows, :] = w_gate[i, :, 0].reshape(half, units)
+        weights[1, rows, :] = w_other[i, :, 0, 0].reshape(half, units)
+        weights[2, rows, :] = w_other[i, :, 0, 1].reshape(half, units)
 
     for part in range(2):
         rows = pl.ds(part * slots, slots)
@@ -372,39 +407,39 @@
 
     for k in range(3):
         left = (g_t if k == 2 else x_t)
-        near_grad = jnp.dot(
-            left[pl.ds(near, half), :], hidden[k], preferred_element_type=F32
-        )
-        far_grad = jnp.dot(left[pl.ds(far, half), :], hidden[k], preferred_element_type=F32)
-        grads_own[:, 0, k] = near_grad.reshape(grads_own.shape[0], -1, units)
-        for i in range(LOW):
-            rows = half // LOW
-            grads_far[i][0, 0, k] = far_grad[i * rows : (i + 1) * rows].astype(BF16)
+        grad = jnp.dot(left[...], hidden[k], preferred_element_type=F32).astype(BF16)
+        for i in range(2):
+            part = grad[i * half : (i + 1) * half].reshape(LOW, -1, units)
+            if k == 0:
+                grads_gate[i, :, 0] = part
+            else:
+                grads_other[i, :, 0, k - 1] = part
 
     @pl.when(step == pl.num_programs(0) - 1)
     def _():
-        for part, (x_ref, g_ref) in enumerate(((x_own, g_own), (x_core, g_core))):
+        for part in range(2):
             rows = pl.ds(part * slots, slots)
             feed = acc_feed[rows, :]
-            inner = jnp.sum(feed * g_ref[...].astype(F32), axis=1, keepdims=True)
-            feed = feed * weight_column(x_ref)
+            inner = jnp.sum(feed * plain[rows, :].astype(F32), axis=1, keepdims=True)
+            feed = feed * scales[rows, 0:1]
             lanes = lax.broadcasted_iota(jnp.int32, (slots, 128), 1)
             if part == 0:
                 back_own[:, :width] = acc_back[rows, :]
-                back_own[:, width:] = jnp.where(lanes == scalars[1], inner, 0.0)
+                back_own[:, width:] = jnp.where(lanes == scalars[0], inner, 0.0)
                 feed_own[...] = feed
             else:
                 high = inner.astype(BF16).astype(F32)
-                extra = jnp.where(lanes == scalars[1], high, 0.0)
-                extra = jnp.where(lanes == scalars[1] + kinds, inner - high, extra)
+                extra = jnp.where(lanes == scalars[0], high, 0.0)
+                extra = jnp.where(lanes == scalars[0] + kinds, inner - high, extra)
                 back_send[:, :width] = acc_back[rows, :].astype(BF16)
                 back_send[:, width:] = extra.astype(BF16)
                 feed_send[...] = feed.astype(BF16)
 
 
-def expert_pass(kinds, scalars, x_own, x_core, g_own, g_core, w_own, w_far):
-    slots, width = g_own.shape
-    low, parities, _, shard_rows, shard_units = w_own.shape
+def expert_pass(kinds, expert, x_blocks, g_blocks, w_gate, w_other):
+    block, width = g_blocks[0].shape
+    slots = LOW * block
+    _, low, parities, _, shard_rows, shard_units = w_other.shape
     units = 256
     steps = shard_units // units
 
@@ -413,11 +448,14 @@
             shape, lambda i, _: (0,) * len(shape), pipeline_mode=pl.Buffered(1)
         )
 
-    def weight_spec(count):
-        return pl.BlockSpec(
-            (count, 1, 3, shard_rows, units), lambda i, _: (0, i // steps, 0, 0, i % steps)
-        )
-
+    weight_specs = [
+        pl.BlockSpec(
+            (2, low, 1, shard_rows, units), lambda i, _: (0, 0, i // steps, 0, i % steps)
+        ),
+        pl.BlockSpec(
+            (2, low, 1, 2, shard_rows, units), lambda i, _: (0, 0, i // steps, 0, 0, i % steps)
+        ),
+    ]
     wide = width + 128
     return pl.pallas_call(
         functools.partial(expert_kernel, kinds),
@@ -425,20 +463,16 @@
             num_scalar_prefetch=1,
             grid=(parities * steps,),
             in_specs=[
-                whole((slots, wide)),
-                whole((slots, wide)),
-                whole((slots, width)),
-                whole((slots, width)),
-                weight_spec(low),
-                *[weight_spec(1) for _ in range(low)],
+                *weight_specs,
+                *[whole((block, wide)) for _ in range(2 * LOW)],
+                *[whole((block, width)) for _ in range(2 * LOW)],
             ],
             out_specs=[
                 whole((slots, wide)),
                 whole((slots, wide)),
                 whole((slots, width)),
                 whole((slots, width)),
-                weight_spec(low),
-                *[weight_spec(1) for _ in range(low)],
+                *weight_specs,
             ],
             scratch_shapes=[
                 pltpu.VMEM((2 * slots, width), BF16),
@@ -449,6 +483,8 @@
                 pltpu.VMEM((3, 2 * slots, units), BF16),
                 pltpu.VMEM((2 * slots, width), F32),
                 pltpu.VMEM((2 * slots, width), F32),
+                pltpu.VMEM((2 * slots, 128), F32),
+                pltpu.VMEM((2 * slots, width), BF16),
             ],
         ),
         out_shape=[
@@ -456,51 +492,125 @@
             jax.ShapeDtypeStruct((slots, wide), BF16),
             jax.ShapeDtypeStruct((slots, width), F32),
             jax.ShapeDtypeStruct((slots, width), BF16),
-            jax.ShapeDtypeStruct(w_own.shape, F32),
-            *[jax.ShapeDtypeStruct(item.shape, BF16) for item in w_far],
+            jax.ShapeDtypeStruct(w_gate.shape, BF16),
+            jax.ShapeDtypeStruct(w_other.shape, BF16),
         ],
         compiler_params=pltpu.CompilerParams(vmem_limit_bytes=58 * 2**20),
         cost_estimate=cost_of(35),
         name="expert_pass",
-    )(scalars, x_own, x_core, g_own, g_core, w_own, *w_far)
+    )(expert.reshape(1), w_gate, w_other, *x_blocks, *g_blocks)
 
 
 def pick_kernel(ids_ref, *refs):
-    pieces, out_ref = refs[:4], refs[4]
-    block = out_ref.shape[0]
+    pieces, outs = refs[:4], refs[4:]
+    block = outs[0].shape[0]
     rows = pieces[0].shape[0]
-    first = pl.program_id(0) * block
-    total = jnp.zeros(out_ref.shape, F32)
-    for r in range(4):
-        slot = first + lax.broadcasted_iota(jnp.int32, (block, rows), 0)
-        columns = pl.ds(r * rows, rows)
-        held = (slot == ids_ref[0:1, columns]) | (slot == ids_ref[1:2, columns])
-        held = jnp.where(held, 1.0, 0.0).astype(BF16)
-        total = total + jnp.dot(held, pieces[r][...], preferred_element_type=F32)
-    out_ref[...] = total.astype(BF16)
+    for i, out_ref in enumerate(outs):
+        slot = i * block + lax.broadcasted_iota(jnp.int32, (block, rows), 0)
+        total = 0.0
+        for r in range(4):
+            columns = pl.ds(r * rows, rows)
+            held = (slot == ids_ref[0:1, columns]) | (slot == ids_ref[1:2, columns])
+            held = jnp.where(held, 1.0, 0.0).astype(BF16)
+            total += jnp.dot(held, pieces[r][...], preferred_element_type=F32)
+        out_ref[...] = total.astype(BF16)
 
 
 def pick(ids, pieces, slots):
     rows, width = pieces[0].shape
-    block = 256 if slots % 256 == 0 else slots
+    block = slots // LOW
+
+    def whole(shape):
+        return pl.BlockSpec(shape, lambda i: (0, 0))
+
     return pl.pallas_call(
         pick_kernel,
-        grid=(slots // block,),
-        in_specs=[
-            pl.BlockSpec((8, 4 * rows), lambda i: (0, 0)),
-            *[pl.BlockSpec((rows, width), lambda i: (0, 0)) for _ in range(4)],
-        ],
-        out_specs=pl.BlockSpec((block, width), lambda i: (i, 0)),
-        out_shape=jax.ShapeDtypeStruct((slots, width), BF16),
+        grid=(1,),
+        in_specs=[whole((8, 4 * rows)), *[whole((rows, width)) for _ in range(4)]],
+        out_specs=[whole((block, width)) for _ in range(LOW)],
+        out_shape=[jax.ShapeDtypeStruct((block, width), BF16) for _ in range(LOW)],
         compiler_params=pltpu.CompilerParams(vmem_limit_bytes=32 * 2**20),
         cost_estimate=cost_of(5),
         name="pick",
     )(ids, *pieces)
 
 
-def spread_kernel(ids_ref, slots_ref, near_ref, send_ref):
+def to_experts(blocks):
+    return [blocks[0]] + [flip(blocks[b], "lo", LOW, b) for b in range(1, LOW)]
+
+
+def back_sum_kernel(kinds, own_ref, core_ref, *outs):
+    width = own_ref.shape[1] - 128
+    block = outs[0].shape[0]
+    for i, out_ref in enumerate(outs):
+        rows = pl.ds(i * block, block)
+        out_ref[:, :width] = (
+            own_ref[rows, :width] + core_ref[rows, :width].astype(F32)
+        ).astype(BF16)
+        extra = own_ref[rows, width:] + core_ref[rows, width:].astype(F32)
+        lanes = lax.broadcasted_iota(jnp.int32, extra.shape, 1)
+        high = jnp.where(lanes < kinds, extra, 0.0).astype(BF16).astype(F32)
+        low = jnp.where(lanes < kinds, extra - high, 0.0)
+        low = pltpu.roll(low, kinds, 1) + jnp.where(lanes >= kinds, extra, 0.0)
+        out_ref[:, width:] = (high + low).astype(BF16)
+
+
+def back_sum(kinds, own, core):
+    slots, wide = own.shape
+    block = slots // LOW
+
+    def whole(shape):
+        return pl.BlockSpec(shape, lambda i: (0, 0))
+
+    return pl.pallas_call(
+        functools.partial(back_sum_kernel, kinds),
+        grid=(1,),
+        in_specs=[whole(own.shape), whole(core.shape)],
+        out_specs=[whole((block, wide)) for _ in range(LOW)],
+        out_shape=[jax.ShapeDtypeStruct((block, wide), BF16) for _ in range(LOW)],
+        compiler_params=pltpu.CompilerParams(vmem_limit_bytes=32 * 2**20),
+        cost_estimate=cost_of(3),
+        name="back_sum",
+    )(own, core)
+
+
+def feed_sum_kernel(own_ref, core_ref, *outs):
+    block = outs[0].shape[0]
+    for i, out_ref in enumerate(outs):
+        rows = pl.ds(i * block, block)
+        out_ref[...] = (own_ref[rows, :] + core_ref[rows, :].astype(F32)).astype(BF16)
+
+
+def feed_sum(own, core):
+    slots, width = own.shape
+    block = slots // LOW
+
+    def whole(shape):
+        return pl.BlockSpec(shape, lambda i: (0, 0))
+
+    return pl.pallas_call(
+        feed_sum_kernel,
+        grid=(1,),
+        in_specs=[whole(own.shape), whole(core.shape)],
+        out_specs=[whole((block, width)) for _ in range(LOW)],
+        out_shape=[jax.ShapeDtypeStruct((block, width), BF16) for _ in range(LOW)],
+        compiler_params=pltpu.CompilerParams(vmem_limit_bytes=32 * 2**20),
+        cost_estimate=cost_of(3),
+        name="feed_sum",
+    )(own, core)
+
+
+def spread_kernel(ids_ref, *refs):
+    blocks, (near_ref, send_ref, slots_ref) = refs[:LOW], refs[LOW:]
     rows = near_ref.shape[1]
     slots = slots_ref.shape[0]
+    block = slots // LOW
+
+    @pl.when(pl.program_id(0) == 0)
+    def _():
+        for i in range(LOW):
+            slots_ref[pl.ds(i * block, block), :] = blocks[i][...]
+
     for k, out_ref in enumerate((near_ref, send_ref)):
         slot = lax.broadcasted_iota(jnp.int32, (rows, slots), 1)
         ids = ids_ref[pl.ds(k * rows, rows), :]
@@ -511,13 +621,13 @@
 
 
 def spread(ids, values, rows):
-    slots, width = values.shape
+    block, width = values[0].shape
     return pl.pallas_call(
         spread_kernel,
         grid=(2,),
         in_specs=[
             pl.BlockSpec((2 * rows, 8), lambda i: (i, 0)),
-            pl.BlockSpec((slots, width), lambda i: (0, 0)),
+            *[pl.BlockSpec((block, width), lambda i: (0, 0)) for _ in range(LOW)],
         ],
         out_specs=[
             pl.BlockSpec((1, rows, width), lambda i: (i, 0, 0)),
@@ -527,10 +637,11 @@
             jax.ShapeDtypeStruct((2, rows, width), F32),
             jax.ShapeDtypeStruct((2, rows, width), BF16),
         ],
+        scratch_shapes=[pltpu.VMEM((LOW * block, width), BF16)],
         compiler_params=pltpu.CompilerParams(vmem_limit_bytes=32 * 2**20),
         cost_estimate=cost_of(6),
         name="spread",
-    )(ids, values)
+    )(ids, *values)
 
 
 def slots_kernel(experts, capacity, scalars, routes_col, order_col, routes_row, order_row,
@@ -581,7 +692,8 @@
             & (place < capacity)
             & (jnp.bitwise_and(mine_target, 1) == scalars[2])
         )
-        slot = lax.shift_right_logical(mine_target, 1) * share + place - first
+        block = jnp.bitwise_xor(lax.shift_right_logical(mine_target, 1), scalars[LOW_PLACE])
+        slot = block * share + place - first
         places_ref[k : k + 1, :] = jnp.where(held, slot, -1)
     for r in range(4):
         start = pl.multiple_of((scalars[1] ^ r) * rows, rows)
@@ -609,11 +721,15 @@
 
 
 def middle_kernel(kinds, scalars, mixed, p0, p1, p2, p3, x_ref, gain_ref, router_w, prior_ref,
-                  prior_w, hidden_ref, sent_ref, router_ref):
+                  prior_w, hidden_ref, sent_ref, router_ref, weight):
     hidden = x_ref[...]
-    for r, weight in enumerate((p0, p1, p2, p3)):
+    rows = p0.shape[2]
+    for r, shards in enumerate((p0, p1, p2, p3)):
+        for k in range(SHARDS):
+            place = pl.multiple_of((scalars[0] ^ k) * rows, rows)
+            weight[r, pl.ds(place, rows), :] = shards[k % LOW, k // LOW]
         hidden += lax.dot_general(
-            mixed[scalars[1] ^ r].T, weight[...], (((1,), (1,)), ((), ())),
+            mixed[scalars[1] ^ r].T, weight[r], (((1,), (1,)), ((), ())),
             preferred_element_type=F32,
         )
     hidden_ref[...] = hidden
@@ -656,6 +772,7 @@
                 whole(prior_w.shape),
             ],
             out_specs=[whole((rows, width)), whole((rows, width + lanes)), whole((rows, lanes))],
+            scratch_shapes=[pltpu.VMEM((4, width, mixed.shape[1]), BF16)],
         ),
         out_shape=[
             jax.ShapeDtypeStruct((rows, width), F32),
@@ -666,6 +783,27 @@
         cost_estimate=cost_of(6),
         name="middle",
     )(scalars, mixed, *weights, x, gain, router_w, prior, prior_w)
+
+
+def halves(value):
+    high = value.astype(BF16)
+    return high, (value - high.astype(F32)).astype(BF16)
+
+
+def split_dot(left, right):
+    (left_high, left_low), (right_high, right_low) = halves(left), halves(right)
+    return (
+        jnp.dot(left_high, right_high, preferred_element_type=F32)
+        + jnp.dot(left_low, right_high, preferred_element_type=F32)
+        + jnp.dot(left_high, right_low, preferred_element_type=F32)
+    )
+
+
+def turned_dot(left, right):
+    high, low = halves(left.T)
+    return jnp.dot(high, right, preferred_element_type=F32) + jnp.dot(
+        low, right, preferred_element_type=F32
+    )
 
 
 def router_back_kernel(kinds, experts, scalars, near_ref, far_ref, hidden_ref, router_ref,
@@ -697,7 +835,7 @@
     weight_copy = column(router, experts + 1) * copy
     weight_first = column(router, experts + 2) * first
     weight_second = column(router, experts + 3) * second
-    mixlog = jnp.dot(normed, small_ref[...], precision=PRECISE, preferred_element_type=F32)
+    mixlog = split_dot(normed, small_ref[...])
 
     def softmax_two(k):
         one, two = column(mixlog, k), column(mixlog, k + 1)
@@ -724,9 +862,7 @@
     )
     held = jnp.where(lanes < kinds, router, 0.0)
     grad_small = held * (grad_router - jnp.sum(held * grad_router, axis=1, keepdims=True))
-    grad_prior_ref[...] = jnp.dot(
-        grad_small, prior_w_ref[...], precision=PRECISE, preferred_element_type=F32
-    )[:, :kinds]
+    grad_prior_ref[...] = split_dot(grad_small, prior_w_ref[...])[:, :kinds]
     grad_logits = grad_small
 
     def mixed_back(weight, mix, other, k):
@@ -744,7 +880,7 @@
     grad_normed = (
         back[:, :width]
         + share * grad_out
-        + jnp.dot(grad_small, small_t_ref[...], precision=PRECISE, preferred_element_type=F32)
+        + split_dot(grad_small, small_t_ref[...])
     )
     through = grad_normed * gain_ref[...]
     inner = jnp.mean(through * hidden, axis=1, keepdims=True)
@@ -760,28 +896,21 @@
     def _():
         sums_ref[...] = jnp.zeros_like(sums_ref)
 
-    def turned_dot(left, right):
-        return jnp.dot(left.T, right, precision=PRECISE, preferred_element_type=F32)
-
-    rounded = normed.astype(BF16).astype(F32)
     vectors = jnp.where(lanes == kinds + 5, vector_first, 0.0) + jnp.where(
         lanes == kinds + 6, vector_second, 0.0
     )
-    total = (
-        turned_dot(grad_logits, rounded)
-        + turned_dot(grad_mixlog, normed)
-        + turned_dot(vectors, grad_out)
-    )
+    low = normed.astype(BF16)
+    total = turned_dot(grad_small, low) + turned_dot(vectors, grad_out.astype(BF16))
     sums_ref[: kinds + 8, :] += total[: kinds + 8, :]
     sums_ref[kinds + 4 : kinds + 5, :] += jnp.sum(grad_normed * unit, axis=0, keepdims=True)
-    prior = turned_dot(prior_ref[...], grad_logits)
+    prior = split_dot(prior_ref[...].T, grad_logits)
     sums_ref[pl.ds(kinds + 8, kinds), : lanes.shape[1]] += prior
 
 
 def router_back(kinds, experts, scalars, near, far, hidden, router, routes, cotangent, prior,
                 gain, small, small_t, vector, prior_w):
     rows, width = hidden.shape
-    block = rows // 4
+    block = rows // 2
     lanes = router.shape[1]
 
     def whole(shape):
@@ -791,13 +920,13 @@
         return pl.BlockSpec((block, columns), lambda i, _: (i, 0))
 
     def mine(columns):
-        return pl.BlockSpec((block, columns), lambda i, scalars: (scalars[1] * 4 + i, 0))
+        return pl.BlockSpec((block, columns), lambda i, scalars: (scalars[1] * 2 + i, 0))
 
     return pl.pallas_call(
         functools.partial(router_back_kernel, kinds, experts),
         grid_spec=pltpu.PrefetchScalarGridSpec(
             num_scalar_prefetch=1,
-            grid=(4,),
+            grid=(2,),
             in_specs=[
                 part(width + lanes),
                 part(width + lanes),
@@ -852,20 +981,46 @@
     return lax.ppermute(value, axis, [(i, i ^ bit) for i in range(size)])
 
 
-def gather_rows(value, many):
+def by_halves(value):
+    if value.shape[0] == 2:
+        return value
+    rows, units = value.shape[-2:]
+    middle_axes = tuple(range(2, value.ndim - 2))
+    turned = value.transpose(*middle_axes, 0, 1, value.ndim - 2, value.ndim - 1)
+    turned = turned.reshape(*turned.shape[:-4], 2, LOW, value.shape[0] * rows // 2, units)
+    axes = turned.ndim
+    return turned.transpose(axes - 4, axes - 3, *range(axes - 4), axes - 2, axes - 1)
+
+
+def scatter_high(value, many):
+    if many != 2:
+        rows, units = value.shape[-2:]
+        middle_axes = tuple(range(2, value.ndim - 2))
+        turned = value.transpose(*middle_axes, 0, 1, value.ndim - 2, value.ndim - 1)
+        turned = turned.reshape(*turned.shape[:-4], many, LOW, 2 * rows // many, units)
+        axes = turned.ndim
+        value = turned.transpose(axes - 4, axes - 3, *range(axes - 4), axes - 2, axes - 1)
+    return lax.psum_scatter(value, "hi", scatter_dimension=0)
+
+
+def gather_rows(value, later, many):
     if many != 2:
         full = lax.all_gather(value, ("hi", "lo"), axis=0, tiled=True)
-        return list(full.reshape(SHARDS, -1, full.shape[1]))
-    return [value] + [flip(value, ("hi", "lo"), SHARDS, bit) for bit in range(1, SHARDS)]
-
-
-def scatter_rows(pieces, many):
+        full = full.reshape(2, LOW, -1, full.shape[1])
+        return [full[:, i] for i in range(LOW)], later
+    far, later = lax.optimization_barrier((swap(value, "hi"), later))
+    both = jnp.stack([value, far])
+    return [both] + [flip(both, "lo", LOW, bit) for bit in range(1, LOW)], later
+
+
+def scatter_rows(near, far, many):
     if many != 2:
-        full = jnp.concatenate(pieces).astype(F32)
+        full = jnp.stack([near, far]).astype(F32).reshape(-1, near.shape[2])
         return lax.psum_scatter(full, ("hi", "lo"), scatter_dimension=0, tiled=True)
-    total = pieces[0].astype(F32)
-    for bit in range(1, SHARDS):
-        total = total + flip(pieces[bit], ("hi", "lo"), SHARDS, bit).astype(F32)
+    both = near.astype(F32) + swap(far, "hi").astype(F32)
+    total = both[0]
+    for bit in range(1, LOW):
+        total = total + flip(both[bit].astype(BF16), "lo", LOW, bit).astype(F32)
     return total
 
 
@@ -911,160 +1066,131 @@
     mine = high * LOW + lax.axis_index("lo") if many == 2 else jnp.zeros_like(high)
     boundary = jnp.cumsum(lengths[0])
     scalars = jnp.concatenate(
-        [jnp.stack([mine, place_in_group, parity, core]), boundary[:-1]]
+        [jnp.stack([mine, place_in_group, parity, core, lax.axis_index("lo")]), boundary[:-1]]
     ).astype(jnp.int32)
     gain_one, gain_two = attn_gain.reshape(1, width), moe_gain.reshape(1, width)
 
     normed_one = rms_norm(inputs, attn_gain).astype(BF16)
-    normed_pieces = gather_pieces(normed_one)
+    normed_other = swap(normed_one, "y")
     attn_shard = jnp.concatenate([w_query, w_key, w_value, w_out.T], axis=1)
-    attn_shards = gather_rows(attn_shard, many)
-    expert_shards = jnp.stack([w_gate, w_up, w_down.transpose(0, 2, 1)], axis=1)
-    expert_part = lax.all_to_all(expert_shards, ("lo", "y"), 0, 0, tiled=True)
-    expert_part = expert_part.reshape(LOW, 2, 3, shard_rows, shard_units)
+    attn_shards, w_gate = gather_rows(attn_shard, w_gate, many)
+    other_shards = jnp.stack([w_up, w_down.transpose(0, 2, 1)], axis=1)
+    other_part = lax.all_to_all(other_shards, ("lo", "y"), 0, 0, tiled=True)
+    other_part = other_part.reshape(LOW, 2, 2, shard_rows, shard_units)
     if many == 2:
-        expert_near = expert_part
-        expert_far = [swap(expert_part[i : i + 1], "hi") for i in range(LOW)]
-        high_place = high
+        gate_far = swap(w_gate, "hi")
+        gate_both = jnp.where(
+            high == 0, jnp.stack([w_gate, gate_far], axis=1), jnp.stack([gate_far, w_gate], axis=1)
+        )
     else:
-        rows = lax.all_gather(expert_part, "hi", axis=0).transpose(2, 3, 0, 1, 4, 5)
-        rows = rows.reshape(2, 3, 2, LOW, width // (2 * LOW), shard_units)
-        rows = rows.transpose(2, 3, 0, 1, 4, 5)
-        expert_near = rows[0]
-        expert_far = [rows[1, i : i + 1] for i in range(LOW)]
-        high_place = jnp.zeros_like(high)
+        gate_both = lax.all_gather(w_gate, "hi", axis=1)
+    gate_part = lax.all_to_all(gate_both, ("lo", "y"), 0, 0, tiled=True)
+    gate_part = gate_part.reshape(LOW, 2, many, shard_rows, shard_units).transpose(2, 0, 1, 3, 4)
+    ids_rows, ids_cols = slots_of(
+        after(scalars, attn_shards[0]), routes, drop_order, experts, capacity
+    )
+    normed_other, attn_shards, other_part, ids_rows = lax.optimization_barrier(
+        (normed_other, attn_shards, other_part, ids_rows)
+    )
+    w_other = by_halves(lax.all_gather(other_part, "hi"))
+    out_mine = jnp.stack([item[:, :, 3 * local_width :] for item in attn_shards])
+    out_other = swap(out_mine, "y")
+    normed_pieces = [normed_one, swap(normed_one, "c"), normed_other, swap(normed_other, "c")]
     router_lanes = jnp.pad(jnp.concatenate([w_router, w_router], axis=1), ((0, 0), (0, 128 - 2 * kinds)))
     prior_lanes = jnp.pad(jnp.concatenate([w_prior, w_prior], axis=1), ((0, 0), (0, 128 - 2 * kinds)))
     const_flat = w_const.transpose(1, 0, 2).reshape(width, 4)
     small = jnp.pad(jnp.concatenate([w_router, const_flat], axis=1), ((0, 0), (0, 112 - kinds + 12)))
     small_t = small.T
     prior_back = jnp.pad(w_prior.T, ((0, 128 - kinds), (0, 128 - kinds)))
+    attn_shards, router_lanes, prior_lanes, small, small_t, prior_back = lax.optimization_barrier(
+        (attn_shards, router_lanes, prior_lanes, small, small_t, prior_back)
+    )
 
     valid_mine = place_in_group * tok_rows + jnp.arange(tok_rows)[:, None] < boundary[-2]
     valid_mine = valid_mine.astype(F32)
     grad_out_low = (cotangent * valid_mine).astype(BF16)
-    grad_out_pieces = gather_pieces(after(grad_out_low, normed_pieces[3]))
+    grad_out_other = swap(after(grad_out_low, normed_pieces[3]), "y")
     mixed, lse, qkv, qkv_full, out_full = attend(normed_pieces, attn_shards, scalars, heads)
-    mixed, expert_far[0], grad_out_pieces = lax.optimization_barrier(
-        (mixed, expert_far[0], grad_out_pieces)
-    )
+    mixed, grad_out_other, gate_part, out_other = lax.optimization_barrier(
+        (mixed, grad_out_other, gate_part, out_other)
+    )
+    out_pieces = [out_mine, swap(after(out_mine, mixed), "c"), out_other, swap(out_other, "c")]
 
     mixed_mine = lax.all_to_all(mixed, tp_axes, 0, 0, tiled=True)
-    out_pieces = gather_pieces(out_full)
-    ids_rows, ids_cols = slots_of(
-        after(scalars, mixed), routes, drop_order, experts, capacity
-    )
+    grad_out_pieces = [
+        grad_out_low, swap(after(grad_out_low, mixed), "c"), grad_out_other, swap(grad_out_other, "c"),
+    ]
     grad_out_slots = pick(ids_rows, grad_out_pieces, slots)
-    mixed_mine, grad_out_slots, ids_cols, out_pieces = lax.optimization_barrier(
-        (mixed_mine, grad_out_slots, ids_cols, out_pieces)
-    )
+    mixed_mine, grad_out_slots = lax.optimization_barrier((mixed_mine, grad_out_slots))
 
     hidden, sent_two, router = middle(
         kinds, scalars, mixed_mine, out_pieces, inputs, gain_two, router_lanes, prior_logits, prior_lanes
     )
-    sent_two, expert_far[1] = lax.optimization_barrier((sent_two, expert_far[1]))
 
     pieces_two = gather_pieces(sent_two)
-    grad_taken = lax.all_to_all(
-        grad_out_slots.reshape(LOW, share, width), "lo", 0, 0, tiled=True
-    ).reshape(slots, width)
-    pieces_two, grad_taken, expert_far[2] = lax.optimization_barrier(
-        (pieces_two, grad_taken, expert_far[2])
-    )
-
-    grad_core = swap(grad_taken, "c")
+    grad_taken = to_experts(grad_out_slots)
+    pieces_two, grad_taken = lax.optimization_barrier((pieces_two, grad_taken))
+
+    grad_taken += [swap(item, "c") for item in grad_taken]
     sent_slots = pick(ids_rows, pieces_two, slots)
-    taken = lax.all_to_all(sent_slots.reshape(LOW, share, wide), "lo", 0, 0, tiled=True)
-    taken = taken.reshape(slots, wide)
-    qkv_pieces = gather_pieces(after(qkv_full, sent_slots))
-    taken, qkv_pieces, expert_far[3] = lax.optimization_barrier(
-        (taken, qkv_pieces, expert_far[3])
-    )
+    taken = to_experts(sent_slots)
+    taken += [swap(item, "c") for item in taken]
+    qkv_pieces = gather_pieces(after(qkv_full, sent_slots[0]))
+    taken, qkv_pieces = lax.optimization_barrier((taken, qkv_pieces))
 
     expert = lax.axis_index("lo") * 2 + parity
-    back_own, back_send, feed_own, feed_send, grads_own, *grads_far = expert_pass(
-        kinds, jnp.stack([high_place, expert]).astype(jnp.int32),
-        taken, swap(taken, "c"), grad_taken, grad_core, expert_near, expert_far,
-    )
-
-    if many == 2:
-        grads_far = [swap(item, "hi") for item in grads_far]
-    back_core = swap(back_send, "c").astype(F32)
-    inner = (
-        back_own[:, width : width + kinds]
-        + back_core[:, width : width + kinds]
-        + back_core[:, width + kinds : width + 2 * kinds]
-    )
-    back_slots = jnp.concatenate(
-        [
-            (back_own[:, :width] + back_core[:, :width]).astype(BF16),
-            jnp.pad(two_parts(inner), ((0, 0), (0, 128 - 2 * kinds))),
-        ],
-        axis=1,
-    )
-    feed_slots = (feed_own + swap(feed_send, "c").astype(F32)).astype(BF16)
-    back_taken = lax.all_to_all(back_slots.reshape(LOW, share, wide), "lo", 0, 0, tiled=True)
-    back_taken, feed_slots, grads_far[0] = lax.optimization_barrier(
-        (back_taken.reshape(slots, wide), feed_slots, grads_far[0])
-    )
+    back_own, back_send, feed_own, feed_send, grads_gate, grads_other = expert_pass(
+        kinds, expert.astype(jnp.int32), taken, grad_taken, by_halves(gate_part), w_other
+    )
+
+    other_sum = scatter_high(grads_other, many)
+    gate_sum = scatter_high(grads_gate, many)
+    back_taken = to_experts(back_sum(kinds, back_own, swap(back_send, "c")))
+    feed_core = swap(feed_send, "c")
+    back_taken, feed_core = lax.optimization_barrier((back_taken, feed_core))
 
     back_near, back_other = add_core(*spread(ids_cols, back_taken, tok_rows))
     back_far = swap(back_other, "y")
-    feed_taken = lax.all_to_all(feed_slots.reshape(LOW, share, width), "lo", 0, 0, tiled=True)
-    back_far, feed_taken, grads_far[1] = lax.optimization_barrier(
-        (back_far, feed_taken.reshape(slots, width), grads_far[1])
-    )
+    feed_taken = to_experts(feed_sum(feed_own, after(feed_core, back_other)))
+    back_far, feed_taken = lax.optimization_barrier((back_far, feed_taken))
 
     grad_hidden, grad_low, partial, grad_prior, sums = router_back(
         kinds, experts, scalars, back_near, back_far, hidden, router, routes, cotangent,
         prior_logits, gain_two, small, small_t, const_vector, prior_back,
     )
     grad_attn_pieces = gather_pieces(grad_low)
-    feed_near, feed_other = add_core(*spread(ids_cols, feed_taken, tok_rows))
+    feed_near, feed_other = add_core(
+        *spread(ids_cols, [after(item, grad_attn_pieces[2]) for item in feed_taken], tok_rows)
+    )
+    sums = after(sums, grad_attn_pieces[2])
     share_sums = lax.all_to_all(sums.reshape(count, 32 * width // count), all_axes, 0, 0, tiled=True)
     share_sums = jnp.sum(share_sums, axis=0)
-    grad_attn_pieces, grads_far, feed_near, feed_other, share_sums = lax.optimization_barrier(
-        (grad_attn_pieces, grads_far, feed_near, feed_other, share_sums)
-    )
 
     feed_far = swap(feed_other, "y")
-    grad_attn_all = natural(grad_attn_pieces, place_in_group)
-    grad_mixed = lax.dot_general(
-        out_full,
-        grad_attn_all.reshape(group, width),
-        (((0,), (1,)), ((), ())),
-        preferred_element_type=F32,
-    ).astype(BF16)
-    far_grads = jnp.concatenate(grads_far).reshape(grads_own.shape)
-    if many == 2:
-        weight_part = (grads_own + far_grads.astype(F32)).astype(BF16)
-    else:
-        rows = jnp.stack([grads_own, far_grads.astype(F32)])
-        rows = rows.transpose(2, 3, 0, 1, 4, 5).reshape(
-            2, 3, many, LOW, shard_rows, shard_units
-        )
-        weight_part = (
-            lax.psum_scatter(rows, "hi", scatter_dimension=2).transpose(2, 0, 1, 3, 4).astype(BF16)
-        )
-    weight_own = lax.all_to_all(
-        weight_part.reshape(2 * LOW, 3, shard_rows, shard_units), ("lo", "y"), 0, 0, tiled=True
-    )
-    grad_qkv = attend_back(qkv, grad_mixed, scalars, lse, heads).reshape(
+    other_own = lax.all_to_all(
+        other_sum.reshape(2 * LOW, 2, shard_rows, shard_units), ("lo", "y"), 0, 0, tiled=True
+    )
+    grad_qkv = attend_back(scalars, qkv, lse, out_full, grad_attn_pieces, heads).reshape(
         4, 3 * local_width, tok_rows
     )
-    grad_qkv, weight_own, feed_far = lax.optimization_barrier((grad_qkv, weight_own, feed_far))
+    grad_qkv, other_own, feed_far, share_sums, gate_sum = lax.optimization_barrier(
+        (grad_qkv, other_own, feed_far, share_sums, gate_sum)
+    )
 
     grad_qkv_mine = lax.all_to_all(grad_qkv, tp_axes, 0, 0, tiled=True)
-    weight_own = weight_own.astype(F32)
+    gate_own = lax.all_to_all(
+        after(gate_sum, grad_qkv_mine).reshape(2 * LOW, shard_rows, shard_units),
+        ("lo", "y"), 0, 0, tiled=True,
+    )
     output = partial + valid_mine * (feed_near + feed_far.astype(F32))
     grad_attn_own = scatter_rows(
-        attn_grads(grad_qkv, mixed, normed_pieces, grad_attn_pieces, scalars), many
+        *attn_grads(grad_qkv, mixed, normed_pieces, grad_attn_pieces, scalars), many
     )
     grad_inputs, gain_part = inputs_back(
         scalars, grad_qkv_mine, qkv_pieces, inputs, gain_one, grad_hidden
     )
     last = everywhere(
-        jnp.concatenate([gain_part.reshape(-1), share_sums]), all_axes, count
+        jnp.concatenate([jnp.sum(gain_part, axis=0).reshape(-1), share_sums]), all_axes, count
     )
     grad_gain = jnp.sum(last[:, :width], axis=0)
     total = last[:, width:].reshape(32, width)
@@ -1082,9 +1208,9 @@
         total[kinds + 8 : 2 * kinds + 8, :kinds],
         total[kinds : kinds + 4].reshape(2, 2, width).transpose(0, 2, 1),
         total[kinds + 5 : kinds + 7],
-        weight_own[:, 0],
-        weight_own[:, 1],
-        weight_own[:, 2].transpose(0, 2, 1),
+        gate_own.astype(F32),
+        other_own[:, 0].astype(F32),
+        other_own[:, 1].transpose(0, 2, 1).astype(F32),
     )
 
 

time: 658 us -> 567 us (0.86)
  waiting for transfers between devices: 272 us -> 212 us
  starting transfers between devices: 127 us -> 94.3 us
  between operations: 1.79 us -> 15 us
  local copies, waits for them, and re-layouts: 58.9 us -> 47.1 us
    ppermute x34 -> x35, waiting for transfers between devices: 212 us -> 85.2 us  [swap(): return lax.ppermute(value, axis, [(0, 1), (1, 0)])]
    ppermute x14 -> x18, waiting for transfers between devices: 3.04 us -> 103 us  [flip(): return lax.ppermute(value, axis, [(i, i ^ bit) for i in range(size)])]
    all_to_all x1, waiting for transfers between devices: 49.7 us -> 6.94 us  [per_device(): lax.all_to_all(sums.reshape(count, 32 * width // count), all_axes, 0, 0,...]
    ppermute x14 -> x18, starting transfers between devices: 36.7 us -> 20.2 us  [flip(): return lax.ppermute(value, axis, [(i, i ^ bit) for i in range(size)])]
    all_to_all x1, waiting for transfers between devices: 0.01 us -> 11.9 us  [per_device(): grad_qkv_mine = lax.all_to_all(grad_qkv, tp_axes, 0, 0, tiled=True)]
    ppermute x34 -> x35, starting transfers between devices: 46.2 us -> 37.9 us  [swap(): return lax.ppermute(value, axis, [(0, 1), (1, 0)])]
    all_to_all x6 -> x4, starting transfers between devices: 25 us -> 17.8 us  [the longest x1 5.43 us: per_device(): other_part = lax.all_to_all(other_shards, ('lo', 'y'), 0, 0, tiled=True)]
    pallas_call x1, Pallas kernels: 16.1 us -> 9.2 us  [router_back(): pl.pallas_call(functools.partial(router_back_kernel, kinds, experts), gri...]
  transfers between devices with their start and end apart: 58 -> 64, of which waited for: 18 -> 32; matrix products, arithmetic and copies ran while one was open for 8% -> 9% of each run, Pallas kernels for 17% -> 20%
where the time goes in v3:
time: 567 us; the launch traced here: 559 us
  waiting for transfers between devices  212 us (37%)
  Pallas kernels  159 us (28%)
  starting transfers between devices  94.3 us (17%)
  local copies, waits for them, and re-layouts  47.1 us (8%)
  other arithmetic  31.6 us (6%)
  between operations  15 us (3%)
    ppermute x18, waiting for transfers between devices, flip(): return lax.ppermute(value, axis, [(i, i ^ bit) for i in range(size)])  103 us
    ppermute x35, waiting for transfers between devices, swap(): return lax.ppermute(value, axis, [(0, 1), (1, 0)])  85.2 us
    ppermute x35, starting transfers between devices, swap(): return lax.ppermute(value, axis, [(0, 1), (1, 0)])  37.9 us
    pallas_call x1, Pallas kernels, expert_pass(): pl.pallas_call(functools.partial(expert_kernel, kinds), grid_spec=pltpu.P...  36 us
    pallas_call x1, Pallas kernels, attend_back(): pl.pallas_call(functools.partial(attend_back_kernel, block, MAXLEN), grid...  35.5 us
    unnamed x166, local copies, waits for them, and re-layouts  28.5 us
    pallas_call x1, Pallas kernels, attend(): pl.pallas_call(functools.partial(attend_kernel, block, MAXLEN), grid_spec...  24.8 us
    ppermute x18, starting transfers between devices, flip(): return lax.ppermute(value, axis, [(i, i ^ bit) for i in range(size)])  20.2 us
  transfers between devices with their start and end apart: 64, of which 32 were waited for; matrix products, arithmetic and copies ran while one was open for 9% of the time, Pallas kernels for 20%

profile of v3, /device:TPU:1, one launch (start us, length us, event | category | flops | bytes accessed | tf_op | source)
XLA Modules:
  0.0 558.8 jit_solution(17868994990259327954)
XLA Ops:
  9.9 5.4 all-to-all-start
  26.8 8.8 %collective-permute-done = bf16[96,768]{1,0:T(8,128)(2,1)S(1)} collective-permute-done((bf16[96,768]{1,0:T(8,128)(2,1)}, bf16[96,768]{1,0:T(8,128)(2,1)S(1)}, u32[]{:S(2)}, u32[]{:S(2)}) %collective-permute-start) | collective-permute-done | bytes 147488 | tf_op jit(solution)/shard_map/ppermute | solution.py:29
  38.6 4.1 collective-permute-start.4
  43.0 10.0 %slots.1 = (s32[8,2048]{1,0:T(8,128)S(1)}, s32[2048,8]{1,0:T(8,128)S(1)}) custom-call(s32[8]{0:T(128)S(1)} %concatenate.18.scalars, s32[2048,2]{1,0:T(8,128)S(1)} %copy.50.routes_col.routes_ref, s32[2048,2]{1,0:T(8,128)S(1)} %copy.51.order_col, s32[2,2048]{1,0:T(2,128)S(1)} %bitcast.91, s32[2,2048]{1,0:T(2,128)S(1)} %bitcast.92), custom_call_target="tpu_custom_call" | custom-call | flops 9200000000 | bytes 1048576 | tf_op jit(solution)/shard_map/slots/pallas_call | solution.py:708
  56.9 6.6 %collective-permute-done.5.refs_7_ = bf16[2,96,768]{2,1,0:T(8,128)(2,1)S(1)} collective-permute-done((bf16[2,96,768]{2,1,0:T(8,128)(2,1)S(1)}, bf16[2,96,768]{2,1,0:T(8,128)(2,1)S(1)}, u32[]{:S(2)}, u32[]{:S(2)}) %collective-permute-start.5) | collective-permute-done | bytes 294944 | tf_op jit(solution)/shard_map/ppermute | solution.py:981
  67.8 9.6 %collective-permute-done.8 = bf16[8,96,512]{2,1,0:T(8,128)(2,1)} collective-permute-done((bf16[8,96,512]{2,1,0:T(8,128)(2,1)}, bf16[8,96,512]{2,1,0:T(8,128)(2,1)}, u32[]{:S(2)}, u32[]{:S(2)}) %collective-permute-start.8) | collective-permute-done | bytes 786464 | tf_op jit(solution)/shard_map/ppermute | solution.py:29
  77.5 3.3 maximum_select_fusion
  80.8 4.4 all-to-all-start.1
  88.2 24.8 %attend.1 = (bf16[4,192,512]{2,1,0:T(8,128)(2,1)}, f32[3,1,2048]{2,1,0:T(1,128)S(1)}, bf16[576,2048]{1,0:T(8,128)(2,1)}, bf16[768,576]{1,0:T(8,128)(2,1)}, bf16[768,192]{1,0:T(8,128)(2,1)S(1)}) custom-call(s32[8]{0:T(128)S(1)} %concatenate.18.scalars, bf16[512,768]{1,0:T(8,128)(2,1)S(1)} %multiply_convert_fusion.1.refs_0_.refs_2_, ...), custom_call_target="tpu_custom_call" | custom-call | flops 27599998976 | bytes 1048576 | tf_op jit(solution)/shard_map/attend/pallas_call | solution.py:133
  116.4 12.8 %collective-permute-done.7.refs_2_ = bf16[512,768]{1,0:T(8,128)(2,1)} collective-permute-done((bf16[512,768]{1,0:T(8,128)(2,1)}, bf16[512,768]{1,0:T(8,128)(2,1)}, u32[]{:S(2)}, u32[]{:S(2)}) %collective-permute-start.7) | collective-permute-done | bytes 786464 | tf_op jit(solution)/shard_map/ppermute | solution.py:29
  130.7 4.0 all-to-all-start.2
  137.0 4.8 pick.2
  146.4 7.7 %middle.1 = (f32[512,768]{1,0:T(8,128)}, bf16[512,896]{1,0:T(8,128)(2,1)}, f32[512,128]{1,0:T(8,128)S(1)}) custom-call(s32[8]{0:T(128)S(1)} %concatenate.18.scalars, bf16[4,192,512]{2,1,0:T(8,128)(2,1)S(1)} %all-to-all-done.2.mixed, bf16[4,2,96,192]{3,2,1,0:T(8,128)(2,1)S(1)} %copy-done.15, bf16[4,2,96,192]{3,2,1,0:T(8,128)(2,1)} %collective-permute-done.12.p1, ...), custom_call_target="tpu_custom_call" | custom-call | flops 6899999744 | bytes 1048576 | tf_op jit(solution)/shard_map/middle/pallas_call | solution.py:760
  156.1 20.0 %collective-permute-done.15.refs_2_ = bf16[512,896]{1,0:T(8,128)(2,1)} collective-permute-done((bf16[512,896]{1,0:T(8,128)(2,1)}, bf16[512,896]{1,0:T(8,128)(2,1)}, u32[]{:S(2)}, u32[]{:S(2)}) %collective-permute-start.15) | collective-permute-done | bytes 917536 | tf_op jit(solution)/shard_map/ppermute | solution.py:29
  180.7 6.2 %collective-permute-done.17.refs_9_ = bf16[192,768]{1,0:T(8,128)(2,1)S(1)} collective-permute-done((bf16[192,768]{1,0:T(8,128)(2,1)}, bf16[192,768]{1,0:T(8,128)(2,1)S(1)}, u32[]{:S(2)}, u32[]{:S(2)}) %collective-permute-start.17) | collective-permute-done | bytes 294944 | tf_op jit(solution)/shard_map/ppermute | solution.py:981
  188.3 12.6 %collective-permute-done.19.refs_11_ = bf16[192,768]{1,0:T(8,128)(2,1)S(1)} collective-permute-done((bf16[192,768]{1,0:T(8,128)(2,1)}, bf16[192,768]{1,0:T(8,128)(2,1)S(1)}, u32[]{:S(2)}, u32[]{:S(2)}) %collective-permute-start.19) | collective-permute-done | bytes 294944 | tf_op jit(solution)/shard_map/ppermute | solution.py:981
  201.7 5.5 pick.3
  214.1 3.6 collective-permute-start.21
  218.8 3.4 collective-permute-start.23
  222.2 8.3 %collective-permute-done.28 = bf16[768,576]{0,1:T(8,128)(2,1)S(1)} collective-permute-done((bf16[768,576]{0,1:T(8,128)(2,1)}, bf16[768,576]{0,1:T(8,128)(2,1)S(1)}, u32[]{:S(2)}, u32[]{:S(2)}) %collective-permute-start.28) | collective-permute-done | bytes 884768 | tf_op jit(solution)/shard_map/ppermute | solution.py:29
  230.5 3.3 collective-permute-start.29
  234.5 25.6 %collective-permute-done.22.refs_3_ = bf16[192,896]{1,0:T(8,128)(2,1)S(1)} collective-permute-done((bf16[192,896]{1,0:T(8,128)(2,1)}, bf16[192,896]{1,0:T(8,128)(2,1)S(1)}, u32[]{:S(2)}, u32[]{:S(2)}) %collective-permute-start.22) | collective-permute-done | bytes 344096 | tf_op jit(solution)/shard_map/ppermute | solution.py:981
  265.2 36.0 %expert_pass.1 = (f32[768,896]{1,0:T(8,128)}, bf16[768,896]{1,0:T(8,128)(2,1)}, f32[768,768]{1,0:T(8,128)}, bf16[768,768]{1,0:T(8,128)(2,1)}, bf16[2,4,2,96,512]...) custom-call(s32[1]{0:T(128)} %bitcast.12.scalars, bf16[2,4,2,96,512]{4,3,2,1,0:T(8,128)(2,1)} %bitcast.93, ...), custom_call_target="tpu_custom_call" | custom-call | flops 40249999360 | bytes 1048576 | tf_op jit(solution)/shard_map/expert_pass/pallas_call | solution.py:460
  301.8 2.8 collective-permute-done.34.core_ref
  309.6 6.6 %collective-permute-done.35.refs_1_ = bf16[192,896]{1,0:T(8,128)(2,1)S(1)} collective-permute-done((bf16[192,896]{1,0:T(8,128)(2,1)S(1)}, bf16[192,896]{1,0:T(8,128)(2,1)S(1)}, u32[]{:S(2)}, u32[]{:S(2)}) %collective-permute-start.35) | collective-permute-done | bytes 344096 | tf_op jit(solution)/shard_map/ppermute | solution.py:981
  316.8 7.7 %collective-permute-done.37.refs_3_ = bf16[192,896]{1,0:T(8,128)(2,1)S(1)} collective-permute-done((bf16[192,896]{1,0:T(8,128)(2,1)S(1)}, bf16[192,896]{1,0:T(8,128)(2,1)S(1)}, u32[]{:S(2)}, u32[]{:S(2)}) %collective-permute-start.37) | collective-permute-done | bytes 344096 | tf_op jit(solution)/shard_map/ppermute | solution.py:981
  324.5 5.1 spread.2
  333.0 3.7 collective-permute-done.39
  348.6 4.4 collective-permute-done.41.refs_1_
  353.0 6.8 %collective-permute-done.42.refs_2_ = bf16[192,768]{1,0:T(8,128)(2,1)} collective-permute-done((bf16[192,768]{1,0:T(8,128)(2,1)}, bf16[192,768]{1,0:T(8,128)(2,1)}, u32[]{:S(2)}, u32[]{:S(2)}) %collective-permute-start.42) | collective-permute-done | bytes 294944 | tf_op jit(solution)/shard_map/ppermute | solution.py:981
  359.8 11.5 %collective-permute-done.43.refs_3_ = bf16[192,768]{1,0:T(8,128)(2,1)} collective-permute-done((bf16[192,768]{1,0:T(8,128)(2,1)}, bf16[192,768]{1,0:T(8,128)(2,1)}, u32[]{:S(2)}, u32[]{:S(2)}) %collective-permute-start.43) | collective-permute-done | bytes 294944 | tf_op jit(solution)/shard_map/ppermute | solution.py:981
  372.3 9.2 %router_back.1 = (f32[512,768]{1,0:T(8,128)}, bf16[512,768]{1,0:T(8,128)(2,1)}, f32[512,768]{1,0:T(8,128)}, f32[512,12]{1,0:T(8,128)S(1)}, f32[32,768]{1,0:T(8,128)S(1)}) custom-call(s32[8]{0:T(128)S(1)} %concatenate.18.scalars, f32[512,896]{1,0:T(8,128)} %get-tuple-element.287.near_ref, bf16[512,896]{1,0:T(8,128)(2,1)} %collective-permute-done.40.far_ref, ...), custom_call_target="tpu_custom_call" | custom-call | flops 9200000000 | bytes 1048576 | tf_op jit(solution)/shard_map/router_back/pallas_call | solution.py:925
  382.7 16.7 %collective-permute-done.44.refs_2_.refs_8_ = bf16[512,768]{1,0:T(8,128)(2,1)} collective-permute-done((bf16[512,768]{1,0:T(8,128)(2,1)}, bf16[512,768]{1,0:T(8,128)(2,1)}, u32[]{:S(2)}, u32[]{:S(2)}) %collective-permute-start.44) | collective-permute-done | bytes 786464 | tf_op jit(solution)/shard_map/ppermute | solution.py:29
  400.4 5.1 spread.3
  409.1 4.7 all-to-all-start.4
  414.6 6.9 %all-to-all-done.4 = f32[32,1,768]{2,1,0:T(1,128)S(1)} async-done(((f32[32,1,768]{2,1,0:T(1,128)}), f32[32,1,768]{2,1,0:T(1,128)S(1)}, u32[]{:S(2)}, u32[]{:S(2)}) %all-to-all-start.4) | async-done | bytes 98336 | tf_op jit(solution)/shard_map/all_to_all | solution.py:1166
  422.3 4.4 all-to-all-start.3
  431.6 35.5 %attend_back.1 = bf16[4,3,192,512]{3,2,1,0:T(8,128)(2,1)} custom-call(s32[8]{0:T(128)S(1)} %concatenate.18.scalars, bf16[576,2048]{1,0:T(8,128)(2,1)} %get-tuple-element.231.qkv_ref, f32[3,1,2048]{2,1,0:T(1,128)S(1)} %get-tuple-element.232.lse_ref, bf16[768,192]{1,0:T(8,128)(2,1)S(1)} %copy-done.50, bf16[512,768]{1,0:T(8,128)(2,1)} %get-tuple-element.221.refs_0_.refs_6_, ...), custom_call_target="tpu_custom_call" | custom-call | flops 39099998208 | bytes 1048576 | tf_op jit(solution)/shard_map/attend_back/pallas_call | solution.py:273
  468.1 5.7 %all-to-all-start.5 = ((bf16[4,576,512]{2,1,0:T(8,128)(2,1)}), bf16[4,576,512]{2,1,0:T(8,128)(2,1)}, u32[]{:S(2)}, u32[]{:S(2)}) async-start(bf16[4,576,512]{2,1,0:T(8,128)(2,1)} %bitcast.33.refs_0_), calls=%async_computation.7 | async-start | bytes 4718592 | tf_op jit(solution)/shard_map/all_to_all | solution.py:1180
  480.8 7.5 %attn_grads.1 = (bf16[4,96,768]{2,1,0:T(8,128)(2,1)S(1)}, bf16[4,96,768]{2,1,0:T(8,128)(2,1)}) custom-call(s32[8]{0:T(128)S(1)} %concatenate.18.scalars, bf16[4,576,512]{2,1,0:T(8,128)(2,1)} %bitcast.33.refs_0_, bf16[4,192,512]{2,1,0:T(8,128)(2,1)} %get-tuple-element.154.refs_1_, bf16[512,768]{1,0:T(8,128)(2,1)S(1)} %copy-done.10, ...), custom_call_target="tpu_custom_call" | custom-call | flops 9200000000 | bytes 1048576 | tf_op jit(solution)/shard_map/attn_grads/pallas_call | solution.py:191
  489.6 11.9 %all-to-all-done.5.grads = bf16[4,576,512]{2,1,0:T(8,128)(2,1)} async-done(((bf16[4,576,512]{2,1,0:T(8,128)(2,1)}), bf16[4,576,512]{2,1,0:T(8,128)(2,1)}, u32[]{:S(2)}, u32[]{:S(2)}) %all-to-all-start.5) | async-done | bytes 2359328 | tf_op jit(solution)/shard_map/all_to_all | solution.py:1180
  503.9 6.1 %inputs_back.1 = (f32[512,768]{1,0:T(8,128)}, f32[2,1,768]{2,1,0:T(1,128)S(1)}) custom-call(s32[8]{0:T(128)S(1)} %concatenate.18.scalars, bf16[4,576,512]{2,1,0:T(8,128)(2,1)} %all-to-all-done.5.grads, bf16[768,576]{1,0:T(8,128)(2,1)S(1)} %copy-done.6, bf16[768,576]{1,0:T(8,128)(2,1)S(1)} %copy.62.p1, bf16[768,576]{1,0:T(8,128)(2,1)S(1)} %copy-done.7, ...), custom_call_target="tpu_custom_call" | custom-call | flops 6899999744 | bytes 1048576 | tf_op jit(solution)/shard_map/inputs_back/pallas_call | solution.py:324
  511.5 3.5 all-to-all-start.6
  515.0 4.1 fusion.6
  520.3 3.9 all-to-all-done.6
  524.2 3.5 all-to-all-start.7
  530.5 3.5 convert_bitcast_fusion
  534.0 9.6 %collective-permute-done.52 = bf16[96,768]{1,0:T(8,128)(2,1)S(1)} collective-permute-done((bf16[96,768]{1,0:T(8,128)(2,1)S(1)}, bf16[96,768]{1,0:T(8,128)(2,1)S(1)}, u32[]{:S(2)}, u32[]{:S(2)}) %collective-permute-start.52) | collective-permute-done | bytes 147488 | tf_op jit(solution)/shard_map/ppermute | solution.py:981
  (318 shorter events, 122.4 us)
Async XLA Ops:
  9.9 54.3 %all-to-all-start = ((bf16[8,2,96,512]{3,2,1,0:T(8,128)(2,1)}), bf16[8,2,96,512]{3,2,1,0:T(8,128)(2,1)}, u32[]{:S(2)}, u32[]{:S(2)}) async-start(bf16[8,2,96,512]{3,2,1,0:T(8,128)(2,1)} %pad_maximum_fusion), calls=%async_computation | async-start | bytes 3145728 | tf_op jit(solution)/shard_map/all_to_all | solution.py:1078
  16.2 19.4 %collective-permute-start = (bf16[96,768]{1,0:T(8,128)(2,1)}, bf16[96,768]{1,0:T(8,128)(2,1)S(1)}, u32[]{:S(2)}, u32[]{:S(2)}) collective-permute-start(bf16[96,768]{1,0:T(8,128)(2,1)} %pad_maximum_fusion.3), channel_id=1, source_target_pairs={{0,16},{16,0},{1,17},{17,1},{2,18},{18,2},{3,19},{19,3},{4,20},{20... | collective-permute-start | bytes 442376 | tf_op jit(solution)/shard_map/ppermute | solution.py:29
  19.0 45.2 %collective-permute-start.2 = (bf16[512,768]{1,0:T(8,128)(2,1)S(1)}, bf16[512,768]{1,0:T(8,128)(2,1)}, u32[]{:S(2)}, u32[]{:S(2)}) collective-permute-start(bf16[512,768]{1,0:T(8,128)(2,1)S(1)} %multiply_convert_fusion.1.refs_0_.refs_2_), channel_id=1, source_target_pairs={{0,2},{2,0},{1,3},{3,1},{4,6},{6,4},{5,7},{7,5},{8,10},{10,8},{9,1... | collective-permute-start | bytes 2359304 | tf_op jit(solution)/shard_map/ppermute | solution.py:29
  37.2 16.7 %collective-permute-start.3 = (bf16[2,96,768]{2,1,0:T(8,128)(2,1)S(1)}, bf16[2,96,768]{2,1,0:T(8,128)(2,1)S(1)}, u32[]{:S(2)}, u32[]{:S(2)}) collective-permute-start(bf16[2,96,768]{2,1,0:T(8,128)(2,1)S(1)} %pad_maximum_fusion.2.refs_4_), channel_id=1, source_target_pairs={{0,4},{4,0},{8,12},{12,8},{1,5},{5,1},{9,13},{13,9},{2,6},{6,2},{1... | collective-permute-start | bytes 884744 | tf_op jit(solution)/shard_map/ppermute | solution.py:981
  38.6 18.3 %collective-permute-start.4 = (bf16[2,96,768]{2,1,0:T(8,128)(2,1)S(1)}, bf16[2,96,768]{2,1,0:T(8,128)(2,1)S(1)}, u32[]{:S(2)}, u32[]{:S(2)}) collective-permute-start(bf16[2,96,768]{2,1,0:T(8,128)(2,1)S(1)} %pad_maximum_fusion.2.refs_4_), channel_id=1, source_target_pairs={{0,8},{4,12},{8,0},{12,4},{1,9},{5,13},{9,1},{13,5},{2,10},{6,14},... | collective-permute-start | bytes 884744 | tf_op jit(solution)/shard_map/ppermute | solution.py:981
  42.6 20.8 %collective-permute-start.5 = (bf16[2,96,768]{2,1,0:T(8,128)(2,1)S(1)}, bf16[2,96,768]{2,1,0:T(8,128)(2,1)S(1)}, u32[]{:S(2)}, u32[]{:S(2)}) collective-permute-start(bf16[2,96,768]{2,1,0:T(8,128)(2,1)S(1)} %pad_maximum_fusion.2.refs_4_), channel_id=1, source_target_pairs={{0,12},{4,8},{8,4},{12,0},{1,13},{5,9},{9,5},{13,1},{2,14},{6,10},... | collective-permute-start | bytes 884744 | tf_op jit(solution)/shard_map/ppermute | solution.py:981
  42.6 34.9 %collective-permute-start.8 = (bf16[8,96,512]{2,1,0:T(8,128)(2,1)}, bf16[8,96,512]{2,1,0:T(8,128)(2,1)}, u32[]{:S(2)}, u32[]{:S(2)}) collective-permute-start(bf16[8,96,512]{2,1,0:T(8,128)(2,1)} %param.35), channel_id=1, source_target_pairs={{0,16},{16,0},{1,17},{17,1},{2,18},{18,2},{3,19},{19,3},{4,20},{20... | collective-permute-start | bytes 2359304 | tf_op jit(solution)/shard_map/ppermute | solution.py:29
  53.9 34.2 %collective-permute-start.1 = (bf16[512,768]{1,0:T(8,128)(2,1)S(1)}, bf16[512,768]{1,0:T(8,128)(2,1)}, u32[]{:S(2)}, u32[]{:S(2)}) collective-permute-start(bf16[512,768]{1,0:T(8,128)(2,1)S(1)} %multiply_convert_fusion.1.refs_0_.refs_2_), channel_id=1, source_target_pairs={{0,1},{1,0},{2,3},{3,2},{4,5},{5,4},{6,7},{7,6},{8,9},{9,8},{10,11... | collective-permute-start | bytes 2359304 | tf_op jit(solution)/shard_map/ppermute | solution.py:29
  64.2 23.8 %collective-permute-start.6 = (bf16[512,768]{1,0:T(8,128)(2,1)}, bf16[512,768]{1,0:T(8,128)(2,1)}, u32[]{:S(2)}, u32[]{:S(2)}) collective-permute-start(bf16[512,768]{1,0:T(8,128)(2,1)} %collective-permute-done.2.refs_2_.refs_4_), channel_id=1, source_target_pairs={{0,1},{1,0},{2,3},{3,2},{4,5},{5,4},{6,7},{7,6},{8,9},{9,8},{10,11... | collective-permute-start | bytes 2359304 | tf_op jit(solution)/shard_map/ppermute | solution.py:29
  80.8 32.9 %all-to-all-start.1 = ((bf16[8,2,96,512]{3,2,1,0:T(8,128)(2,1)}), bf16[8,2,96,512]{3,2,1,0:T(8,128)(2,1)}, u32[]{:S(2)}, u32[]{:S(2)}) async-start(bf16[8,2,96,512]{3,2,1,0:T(8,128)(2,1)} %maximum_select_fusion), calls=%async_computation.1 | async-start | bytes 3145728 | tf_op jit(solution)/shard_map/all_to_all | solution.py:1087
  86.6 29.8 %collective-permute-start.9 = (bf16[4,2,96,192]{3,2,1,0:T(8,128)(2,1)S(1)}, bf16[4,2,96,192]{3,2,1,0:T(8,128)(2,1)}, u32[]{:S(2)}, u32[]{:S(2)}) collective-permute-start(bf16[4,2,96,192]{3,2,1,0:T(8,128)(2,1)S(1)} %pad_maximum_fusion.1.p0), channel_id=1, source_target_pairs={{0,2},{2,0},{1,3},{3,1},{4,6},{6,4},{5,7},{7,5},{8,10},{10,8},{9,1... | collective-permute-start | bytes 884744 | tf_op jit(solution)/shard_map/ppermute | solution.py:29
  88.0 41.2 %collective-permute-start.7 = (bf16[512,768]{1,0:T(8,128)(2,1)}, bf16[512,768]{1,0:T(8,128)(2,1)}, u32[]{:S(2)}, u32[]{:S(2)}) collective-permute-start(bf16[512,768]{1,0:T(8,128)(2,1)} %multiply_convert_fusion.refs_0_), channel_id=1, source_target_pairs={{0,2},{2,0},{1,3},{3,1},{4,6},{6,4},{5,7},{7,5},{8,10},{10,8},{9,1... | collective-permute-start | bytes 2359304 | tf_op jit(solution)/shard_map/ppermute | solution.py:29
  130.7 14.8 %all-to-all-start.2 = ((bf16[4,192,512]{2,1,0:T(8,128)(2,1)}), bf16[4,192,512]{2,1,0:T(8,128)(2,1)S(1)}, u32[]{:S(2)}, u32[]{:S(2)}) async-start(bf16[4,192,512]{2,1,0:T(8,128)(2,1)} %get-tuple-element.154.refs_1_), calls=%async_computation.2 | async-start | bytes 1572864 | tf_op jit(solution)/shard_map/all_to_all | solution.py:1119
  134.6 129.0 %all-gather.3.cloned.1.call-start = ((), (), s32[]{:S(2)}) async-start(), calls=%async_computation.12 | async-start | bytes 4718592 | tf_op jit(solution)/shard_map/all_gather | solution.py:1095
  136.4 9.0 %collective-permute-start.12 = (bf16[4,2,96,192]{3,2,1,0:T(8,128)(2,1)S(1)}, bf16[4,2,96,192]{3,2,1,0:T(8,128)(2,1)}, u32[]{:S(2)}, u32[]{:S(2)}) collective-permute-start(bf16[4,2,96,192]{3,2,1,0:T(8,128)(2,1)S(1)} %copy-done.15), channel_id=1, source_target_pairs={{0,1},{1,0},{2,3},{3,2},{4,5},{5,4},{6,7},{7,6},{8,9},{9,8},{10,11... | collective-permute-start | bytes 884744 | tf_op jit(solution)/shard_map/ppermute | solution.py:29
  154.8 21.3 %collective-permute-start.15 = (bf16[512,896]{1,0:T(8,128)(2,1)}, bf16[512,896]{1,0:T(8,128)(2,1)}, u32[]{:S(2)}, u32[]{:S(2)}) collective-permute-start(bf16[512,896]{1,0:T(8,128)(2,1)} %get-tuple-element.171.refs_0_), channel_id=1, source_target_pairs={{0,2},{2,0},{1,3},{3,1},{4,6},{6,4},{5,7},{7,5},{8,10},{10,8},{9,1... | collective-permute-start | bytes 2752520 | tf_op jit(solution)/shard_map/ppermute | solution.py:29
  155.4 45.6 %collective-permute-start.14 = (bf16[512,896]{1,0:T(8,128)(2,1)}, bf16[512,896]{1,0:T(8,128)(2,1)}, u32[]{:S(2)}, u32[]{:S(2)}) collective-permute-start(bf16[512,896]{1,0:T(8,128)(2,1)} %get-tuple-element.171.refs_0_), channel_id=1, source_target_pairs={{0,1},{1,0},{2,3},{3,2},{4,5},{5,4},{6,7},{7,6},{8,9},{9,8},{10,11... | collective-permute-start | bytes 2752520 | tf_op jit(solution)/shard_map/ppermute | solution.py:29
  176.1 25.6 %collective-permute-start.16 = (bf16[512,896]{1,0:T(8,128)(2,1)}, bf16[512,896]{1,0:T(8,128)(2,1)}, u32[]{:S(2)}, u32[]{:S(2)}) collective-permute-start(bf16[512,896]{1,0:T(8,128)(2,1)} %collective-permute-done.15.refs_2_), channel_id=1, source_target_pairs={{0,1},{1,0},{2,3},{3,2},{4,5},{5,4},{6,7},{7,6},{8,9},{9,8},{10,11... | collective-permute-start | bytes 2752520 | tf_op jit(solution)/shard_map/ppermute | solution.py:29
  177.9 244.3 %reduce-scatter.3.cloned.1.call-start = ((), (), s32[]{:S(2)}) async-start(), calls=%async_computation.10 | async-start | bytes 4718592 | tf_op jit(solution)/shard_map/reduce_scatter | solution.py:1003
  179.2 9.1 %collective-permute-start.18 = (bf16[192,768]{1,0:T(8,128)(2,1)}, bf16[192,768]{1,0:T(8,128)(2,1)S(1)}, u32[]{:S(2)}, u32[]{:S(2)}) collective-permute-start(bf16[192,768]{1,0:T(8,128)(2,1)} %copy-done.35), channel_id=1, source_target_pairs={{0,8},{4,12},{8,0},{12,4},{1,9},{5,13},{9,1},{13,5},{2,10},{6,14},... | collective-permute-start | bytes 884744 | tf_op jit(solution)/shard_map/ppermute | solution.py:981
  180.4 20.6 %collective-permute-start.19 = (bf16[192,768]{1,0:T(8,128)(2,1)}, bf16[192,768]{1,0:T(8,128)(2,1)S(1)}, u32[]{:S(2)}, u32[]{:S(2)}) collective-permute-start(bf16[192,768]{1,0:T(8,128)(2,1)} %copy-done.34), channel_id=1, source_target_pairs={{0,12},{4,8},{8,4},{12,0},{1,13},{5,9},{9,5},{13,1},{2,14},{6,10},... | collective-permute-start | bytes 884744 | tf_op jit(solution)/shard_map/ppermute | solution.py:981
  211.5 18.9 %collective-permute-start.28 = (bf16[768,576]{0,1:T(8,128)(2,1)}, bf16[768,576]{0,1:T(8,128)(2,1)S(1)}, u32[]{:S(2)}, u32[]{:S(2)}) collective-permute-start(bf16[768,576]{0,1:T(8,128)(2,1)} %copy.56), channel_id=1, source_target_pairs={{0,2},{2,0},{1,3},{3,1},{4,6},{6,4},{5,7},{7,5},{8,10},{10,8},{9,1... | collective-permute-start | bytes 2654216 | tf_op jit(solution)/shard_map/ppermute | solution.py:29
  212.0 50.9 %collective-permute-start.27 = (bf16[768,576]{0,1:T(8,128)(2,1)}, bf16[768,576]{0,1:T(8,128)(2,1)}, u32[]{:S(2)}, u32[]{:S(2)}) collective-permute-start(bf16[768,576]{0,1:T(8,128)(2,1)} %copy.56), channel_id=1, source_target_pairs={{0,1},{1,0},{2,3},{3,2},{4,5},{5,4},{6,7},{7,6},{8,9},{9,8},{10,11... | collective-permute-start | bytes 2654216 | tf_op jit(solution)/shard_map/ppermute | solution.py:29
  214.1 19.7 %collective-permute-start.21 = (bf16[192,896]{1,0:T(8,128)(2,1)}, bf16[192,896]{1,0:T(8,128)(2,1)S(1)}, u32[]{:S(2)}, u32[]{:S(2)}) collective-permute-start(bf16[192,896]{1,0:T(8,128)(2,1)} %copy-done.31), channel_id=1, source_target_pairs={{0,8},{4,12},{8,0},{12,4},{1,9},{5,13},{9,1},{13,5},{2,10},{6,14},... | collective-permute-start | bytes 1032200 | tf_op jit(solution)/shard_map/ppermute | solution.py:981
  217.7 42.4 %collective-permute-start.22 = (bf16[192,896]{1,0:T(8,128)(2,1)}, bf16[192,896]{1,0:T(8,128)(2,1)S(1)}, u32[]{:S(2)}, u32[]{:S(2)}) collective-permute-start(bf16[192,896]{1,0:T(8,128)(2,1)} %copy-done.30), channel_id=1, source_target_pairs={{0,12},{4,8},{8,4},{12,0},{1,13},{5,9},{9,5},{13,1},{2,14},{6,10},... | collective-permute-start | bytes 1032200 | tf_op jit(solution)/shard_map/ppermute | solution.py:981
  218.8 41.9 %collective-permute-start.23 = (bf16[192,896]{1,0:T(8,128)(2,1)}, bf16[192,896]{1,0:T(8,128)(2,1)S(1)}, u32[]{:S(2)}, u32[]{:S(2)}) collective-permute-start(bf16[192,896]{1,0:T(8,128)(2,1)} %copy-done.29), channel_id=1, source_target_pairs={{0,1},{1,0},{2,3},{3,2},{4,5},{5,4},{6,7},{7,6},{8,9},{9,8},{10,11... | collective-permute-start | bytes 1032200 | tf_op jit(solution)/shard_map/ppermute | solution.py:29
  230.5 33.2 %collective-permute-start.29 = (bf16[768,576]{0,1:T(8,128)(2,1)S(1)}, bf16[768,576]{0,1:T(8,128)(2,1)}, u32[]{:S(2)}, u32[]{:S(2)}) collective-permute-start(bf16[768,576]{0,1:T(8,128)(2,1)S(1)} %collective-permute-done.28), channel_id=1, source_target_pairs={{0,1},{1,0},{2,3},{3,2},{4,5},{5,4},{6,7},{7,6},{8,9},{9,8},{10,11... | collective-permute-start | bytes 2654216 | tf_op jit(solution)/shard_map/ppermute | solution.py:29
  233.8 27.0 %collective-permute-start.24 = (bf16[192,896]{1,0:T(8,128)(2,1)S(1)}, bf16[192,896]{1,0:T(8,128)(2,1)S(1)}, u32[]{:S(2)}, u32[]{:S(2)}) collective-permute-start(bf16[192,896]{1,0:T(8,128)(2,1)S(1)} %collective-permute-done.20.refs_1_), channel_id=1, source_target_pairs={{0,1},{1,0},{2,3},{3,2},{4,5},{5,4},{6,7},{7,6},{8,9},{9,8},{10,11... | collective-permute-start | bytes 1032200 | tf_op jit(solution)/shard_map/ppermute | solution.py:29
  306.9 9.3 %collective-permute-start.35 = (bf16[192,896]{1,0:T(8,128)(2,1)S(1)}, bf16[192,896]{1,0:T(8,128)(2,1)S(1)}, u32[]{:S(2)}, u32[]{:S(2)}) collective-permute-start(bf16[192,896]{1,0:T(8,128)(2,1)S(1)} %get-tuple-element.196), channel_id=1, source_target_pairs={{0,4},{4,0},{8,12},{12,8},{1,5},{5,1},{9,13},{13,9},{2,6},{6,2},{1... | collective-permute-start | bytes 1032200 | tf_op jit(solution)/shard_map/ppermute | solution.py:981
  307.8 16.7 %collective-permute-start.37 = (bf16[192,896]{1,0:T(8,128)(2,1)S(1)}, bf16[192,896]{1,0:T(8,128)(2,1)S(1)}, u32[]{:S(2)}, u32[]{:S(2)}) collective-permute-start(bf16[192,896]{1,0:T(8,128)(2,1)S(1)} %get-tuple-element.198), channel_id=1, source_target_pairs={{0,12},{4,8},{8,4},{12,0},{1,13},{5,9},{9,5},{13,1},{2,14},{6,10},... | collective-permute-start | bytes 1032200 | tf_op jit(solution)/shard_map/ppermute | solution.py:981
  341.0 30.4 %collective-permute-start.40 = (bf16[512,896]{1,0:T(8,128)(2,1)}, bf16[512,896]{1,0:T(8,128)(2,1)}, u32[]{:S(2)}, u32[]{:S(2)}) collective-permute-start(bf16[512,896]{1,0:T(8,128)(2,1)} %get-tuple-element.286), channel_id=1, source_target_pairs={{0,2},{2,0},{1,3},{3,1},{4,6},{6,4},{5,7},{7,5},{8,10},{10,8},{9,1... | collective-permute-start | bytes 2752520 | tf_op jit(solution)/shard_map/ppermute | solution.py:29
  345.7 14.2 %collective-permute-start.42 = (bf16[192,768]{1,0:T(8,128)(2,1)}, bf16[192,768]{1,0:T(8,128)(2,1)}, u32[]{:S(2)}, u32[]{:S(2)}) collective-permute-start(bf16[192,768]{1,0:T(8,128)(2,1)} %get-tuple-element.211), channel_id=1, source_target_pairs={{0,8},{4,12},{8,0},{12,4},{1,9},{5,13},{9,1},{13,5},{2,10},{6,14},... | collective-permute-start | bytes 884744 | tf_op jit(solution)/shard_map/ppermute | solution.py:981
  345.7 25.7 %collective-permute-start.43 = (bf16[192,768]{1,0:T(8,128)(2,1)}, bf16[192,768]{1,0:T(8,128)(2,1)}, u32[]{:S(2)}, u32[]{:S(2)}) collective-permute-start(bf16[192,768]{1,0:T(8,128)(2,1)} %get-tuple-element.212), channel_id=1, source_target_pairs={{0,12},{4,8},{8,4},{12,0},{1,13},{5,9},{9,5},{13,1},{2,14},{6,10},... | collective-permute-start | bytes 884744 | tf_op jit(solution)/shard_map/ppermute | solution.py:981
  381.5 17.9 %collective-permute-start.44 = (bf16[512,768]{1,0:T(8,128)(2,1)}, bf16[512,768]{1,0:T(8,128)(2,1)}, u32[]{:S(2)}, u32[]{:S(2)}) collective-permute-start(bf16[512,768]{1,0:T(8,128)(2,1)} %get-tuple-element.221.refs_0_.refs_6_), channel_id=1, source_target_pairs={{0,2},{2,0},{1,3},{3,1},{4,6},{6,4},{5,7},{7,5},{8,10},{10,8},{9,1... | collective-permute-start | bytes 2359304 | tf_op jit(solution)/shard_map/ppermute | solution.py:29
  405.5 21.2 %collective-permute-start.45 = (bf16[2,512,768]{2,1,0:T(8,128)(2,1)}, bf16[2,512,768]{2,1,0:T(8,128)(2,1)}, u32[]{:S(2)}, u32[]{:S(2)}) collective-permute-start(bf16[2,512,768]{2,1,0:T(8,128)(2,1)} %get-tuple-element.230), channel_id=1, source_target_pairs={{0,1},{1,0},{2,3},{3,2},{4,5},{5,4},{6,7},{7,6},{8,9},{9,8},{10,11... | collective-permute-start | bytes 4718600 | tf_op jit(solution)/shard_map/ppermute | solution.py:29
  407.9 23.7 %collective-permute-start.46 = (bf16[512,768]{1,0:T(8,128)(2,1)}, bf16[512,768]{1,0:T(8,128)(2,1)}, u32[]{:S(2)}, u32[]{:S(2)}) collective-permute-start(bf16[512,768]{1,0:T(8,128)(2,1)} %get-tuple-element.221.refs_0_.refs_6_), channel_id=1, source_target_pairs={{0,1},{1,0},{2,3},{3,2},{4,5},{5,4},{6,7},{7,6},{8,9},{9,8},{10,11... | collective-permute-start | bytes 2359304 | tf_op jit(solution)/shard_map/ppermute | solution.py:29
  408.0 23.6 %collective-permute-start.47 = (bf16[512,768]{1,0:T(8,128)(2,1)}, bf16[512,768]{1,0:T(8,128)(2,1)}, u32[]{:S(2)}, u32[]{:S(2)}) collective-permute-start(bf16[512,768]{1,0:T(8,128)(2,1)} %collective-permute-done.44.refs_2_.refs_8_), channel_id=1, source_target_pairs={{0,1},{1,0},{2,3},{3,2},{4,5},{5,4},{6,7},{7,6},{8,9},{9,8},{10,11... | collective-permute-start | bytes 2359304 | tf_op jit(solution)/shard_map/ppermute | solution.py:29
  409.1 12.4 %all-to-all-start.4 = ((f32[32,1,768]{2,1,0:T(1,128)}), f32[32,1,768]{2,1,0:T(1,128)S(1)}, u32[]{:S(2)}, u32[]{:S(2)}) async-start(f32[32,1,768]{2,1,0:T(1,128)} %copy.61), calls=%async_computation.5 | async-start | bytes 196608 | tf_op jit(solution)/shard_map/all_to_all | solution.py:1166
  413.9 53.3 %reduce-scatter.5.cloned.1.call-start = ((), (), s32[]{:S(2)}) async-start(), calls=%async_computation.11 | async-start | bytes 2359296 | tf_op jit(solution)/shard_map/reduce_scatter | solution.py:1003
  422.3 44.9 %all-to-all-start.3 = ((bf16[8,2,96,512]{3,2,1,0:T(8,128)(2,1)}), bf16[8,2,96,512]{3,2,1,0:T(8,128)(2,1)}, u32[]{:S(2)}, u32[]{:S(2)}) async-start(bf16[8,2,96,512]{3,2,1,0:T(8,128)(2,1)} %bitcast.94), calls=%async_computation.4 | async-start | bytes 3145728 | tf_op jit(solution)/shard_map/all_to_all | solution.py:1170
  430.3 36.9 %collective-permute-start.48 = (bf16[512,768]{1,0:T(8,128)(2,1)}, bf16[512,768]{1,0:T(8,128)(2,1)S(1)}, u32[]{:S(2)}, u32[]{:S(2)}) collective-permute-start(bf16[512,768]{1,0:T(8,128)(2,1)} %fusion.8), channel_id=1, source_target_pairs={{0,2},{2,0},{1,3},{3,1},{4,6},{6,4},{5,7},{7,5},{8,10},{10,8},{9,1... | collective-permute-start | bytes 2359304 | tf_op jit(solution)/shard_map/ppermute | solution.py:29
  468.1 33.4 %all-to-all-start.5 = ((bf16[4,576,512]{2,1,0:T(8,128)(2,1)}), bf16[4,576,512]{2,1,0:T(8,128)(2,1)}, u32[]{:S(2)}, u32[]{:S(2)}) async-start(bf16[4,576,512]{2,1,0:T(8,128)(2,1)} %bitcast.33.refs_0_), calls=%async_computation.7 | async-start | bytes 4718592 | tf_op jit(solution)/shard_map/all_to_all | solution.py:1180
  489.1 29.9 %collective-permute-start.49 = (bf16[4,96,768]{2,1,0:T(8,128)(2,1)}, bf16[4,96,768]{2,1,0:T(8,128)(2,1)}, u32[]{:S(2)}, u32[]{:S(2)}) collective-permute-start(bf16[4,96,768]{2,1,0:T(8,128)(2,1)} %get-tuple-element.250), channel_id=1, source_target_pairs={{0,16},{16,0},{1,17},{17,1},{2,18},{18,2},{3,19},{19,3},{4,20},{20... | collective-permute-start | bytes 1769480 | tf_op jit(solution)/shard_map/ppermute | solution.py:29
  511.5 12.7 %all-to-all-start.6 = ((f32[32,1,1536]{2,1,0:T(1,128)}), f32[32,1,1536]{2,1,0:T(1,128)S(1)}, u32[]{:S(2)}, u32[]{:S(2)}) async-start(f32[32,1,1536]{2,1,0:T(1,128)} %broadcast_in_dim.5), calls=%async_computation.8 | async-start | bytes 393216 | tf_op jit(solution)/shard_map/all_to_all | solution.py:977
  524.2 26.2 %all-to-all-start.7 = ((bf16[8,96,512]{2,1,0:T(8,128)(2,1)}), bf16[8,96,512]{2,1,0:T(8,128)(2,1)S(1)}, u32[]{:S(2)}, u32[]{:S(2)}) async-start(bf16[8,96,512]{2,1,0:T(8,128)(2,1)} %bitcast.45), calls=%async_computation.9 | async-start | bytes 1572864 | tf_op jit(solution)/shard_map/all_to_all | solution.py:1181
  527.8 15.8 %collective-permute-start.52 = (bf16[96,768]{1,0:T(8,128)(2,1)S(1)}, bf16[96,768]{1,0:T(8,128)(2,1)S(1)}, u32[]{:S(2)}, u32[]{:S(2)}) collective-permute-start(bf16[96,768]{1,0:T(8,128)(2,1)S(1)} %get-tuple-element.293), channel_id=1, source_target_pairs={{0,12},{4,8},{8,4},{12,0},{1,13},{5,9},{9,5},{13,1},{2,14},{6,10},... | collective-permute-start | bytes 442376 | tf_op jit(solution)/shard_map/ppermute | solution.py:981
  530.2 15.0 %collective-permute-start.51 = (bf16[96,768]{1,0:T(8,128)(2,1)S(1)}, bf16[96,768]{1,0:T(8,128)(2,1)S(1)}, u32[]{:S(2)}, u32[]{:S(2)}) collective-permute-start(bf16[96,768]{1,0:T(8,128)(2,1)S(1)} %get-tuple-element.294), channel_id=1, source_target_pairs={{0,8},{4,12},{8,0},{12,4},{1,9},{5,13},{9,1},{13,5},{2,10},{6,14},... | collective-permute-start | bytes 442376 | tf_op jit(solution)/shard_map/ppermute | solution.py:981
  530.4 14.8 %collective-permute-start.50 = (bf16[96,768]{1,0:T(8,128)(2,1)S(1)}, bf16[96,768]{1,0:T(8,128)(2,1)S(1)}, u32[]{:S(2)}, u32[]{:S(2)}) collective-permute-start(bf16[96,768]{1,0:T(8,128)(2,1)S(1)} %get-tuple-element.292), channel_id=1, source_target_pairs={{0,4},{4,0},{8,12},{12,8},{1,5},{5,1},{9,13},{13,9},{2,6},{6,2},{1... | collective-permute-start | bytes 442376 | tf_op jit(solution)/shard_map/ppermute | solution.py:981
  (95 other events, 828.8 us)
Sparse Core Ops, SparseCore 0:
  178.0 77.5 all-gather.2
  333.1 76.0 reduce-scatter.2
  417.6 44.1 reduce-scatter.4

commit v4 on v3

--- a/solution.py
+++ b/solution.py
@@ -45,8 +45,8 @@
 
 
 def add_core(near, sent):
-    got = swap(sent, "c").astype(F32)
-    return near[0] + got[0], (near[1] + got[1]).astype(BF16)
+    got = swap(sent, "c")
+    return got, (near[1] + got[1].astype(F32)).astype(BF16)
 
 
 def cost_of(microseconds):
@@ -55,11 +55,24 @@
     )
 
 
-def scores_mask(first_key, first_query, window, block, scalars):
-    row = first_query + lax.broadcasted_iota(jnp.int32, (1, block), 1)
+def start_of(row, scalars):
     start_row = jnp.zeros_like(row)
     for k in range(BOUNDS, scalars.shape[0]):
         start_row = jnp.where(row >= scalars[k], scalars[k], start_row)
+    return start_row
+
+
+def for_window(first, block, pad, scalars, body):
+    needed = (first - start_of(first, scalars) + block - 1) // block
+    most = pad // block
+    for blocks in range(most):
+        pl.when(needed == blocks)(functools.partial(body, (blocks + 1) * block))
+    pl.when(needed >= most)(functools.partial(body, pad + block))
+
+
+def scores_mask(first_key, first_query, window, block, scalars):
+    row = first_query + lax.broadcasted_iota(jnp.int32, (1, block), 1)
+    start_row = start_of(row, scalars)
     key_places = first_key + lax.broadcasted_iota(jnp.int32, (window, block), 0)
     query_places = first_query + lax.broadcasted_iota(jnp.int32, (window, block), 1)
     return (key_places >= start_row) & (key_places <= query_places)
@@ -70,7 +83,6 @@
     shards, refs = refs[:LOW], refs[LOW:]
     out_ref, lse_ref, qkv_ref, weight_ref, last_ref, key_rows, value_pad, full = refs
     group = qkv_ref.shape[1]
-    window = pad + block
     quarter = group // 4
     inner = qkv_ref.shape[0] // 3
     head = pl.program_id(0)
@@ -81,9 +93,9 @@
         for r in range(SHARDS):
             place = pl.multiple_of((scalars[0] ^ r) * rows, rows)
             full[pl.ds(place, rows), :] = shards[r % LOW][r // LOW]
-        weight_ref[...] = full[:, : 3 * inner]
         last_ref[...] = full[:, 3 * inner :]
         turned = full[:, : 3 * inner].T
+        weight_ref[...] = turned
         for r in range(4):
             place = pl.multiple_of((scalars[1] ^ r) * quarter, quarter)
             qkv_ref[:, pl.ds(place, quarter)] = lax.dot_general(
@@ -98,22 +110,30 @@
 
     def one(i, carry):
         first = pl.multiple_of(i * block, block)
-        scores = jnp.dot(
-            key_rows[pl.ds(first, window), :],
-            qkv_ref[pl.ds(first_row, HEAD), pl.ds(first, block)],
-            preferred_element_type=F32,
-        )
-        allowed = scores_mask(first - pad, first, window, block, scalars)
-        scores = jnp.where(allowed, scores * 0.125, NEGATIVE)
-        highest = jnp.max(scores, axis=0, keepdims=True)
-        weights = jnp.exp(scores - highest)
-        total = jnp.sum(weights, axis=0, keepdims=True)
-        mixed = jnp.dot(
-            value_pad[:, pl.ds(first, window)], weights.astype(BF16), preferred_element_type=F32
-        )
-        mixed = (mixed / total).astype(BF16)
-        out_ref[first // quarter, :, pl.ds(pl.multiple_of(first % quarter, block), block)] = mixed
-        lse_ref[0, :, pl.ds(first, block)] = highest + jnp.log(total)
+
+        def body(window):
+            begin = pl.multiple_of(first + pad + block - window, block)
+            scores = jnp.dot(
+                key_rows[pl.ds(begin, window), :],
+                qkv_ref[pl.ds(first_row, HEAD), pl.ds(first, block)],
+                preferred_element_type=F32,
+            )
+            allowed = scores_mask(begin - pad, first, window, block, scalars)
+            scores = jnp.where(allowed, scores * 0.125, NEGATIVE)
+            highest = jnp.max(scores, axis=0, keepdims=True)
+            weights = jnp.exp(scores - highest)
+            total = jnp.sum(weights, axis=0, keepdims=True)
+            mixed = jnp.dot(
+                value_pad[:, pl.ds(begin, window)],
+                weights.astype(BF16),
+                preferred_element_type=F32,
+            )
+            mixed = (mixed / total).astype(BF16)
+            column = pl.multiple_of(first % quarter, block)
+            out_ref[first // quarter, :, pl.ds(column, block)] = mixed
+            lse_ref[0, :, pl.ds(first, block)] = highest + jnp.log(total)
+
+        for_window(first, block, pad, scalars, body)
         return carry
 
     lax.fori_loop(0, group // block, one, 0)
@@ -143,7 +163,7 @@
                 pl.BlockSpec((4, HEAD, rows), lambda h, _: (0, h, 0)),
                 pl.BlockSpec((1, 1, group), lambda h, _: (h, 0, 0)),
                 whole((3 * inner, group)),
-                whole((width, 3 * inner)),
+                whole((3 * inner, width)),
                 whole((width, inner)),
             ],
             scratch_shapes=[
@@ -156,7 +176,7 @@
             jax.ShapeDtypeStruct((4, inner, rows), BF16),
             jax.ShapeDtypeStruct((heads, 1, group), F32),
             jax.ShapeDtypeStruct((3 * inner, group), BF16),
-            jax.ShapeDtypeStruct((width, 3 * inner), BF16),
+            jax.ShapeDtypeStruct((3 * inner, width), BF16),
             jax.ShapeDtypeStruct((width, inner), BF16),
         ],
         compiler_params=pltpu.CompilerParams(vmem_limit_bytes=48 * 2**20),
@@ -205,7 +225,6 @@
     out_ref, grad_mixed, key_rows, value_rows, key_pad, grad_key, grad_value = refs
     group = qkv_ref.shape[1]
     inner_rows = qkv_ref.shape[0] // 3
-    window = pad + block
     quarter = group // 4
     contract_last = (((1,), (1,)), ((), ()))
     head = pl.program_id(0)
@@ -232,27 +251,33 @@
 
     def one(i, carry):
         first = pl.multiple_of(i * block, block)
-        query = qkv_ref[pl.ds(first_row, HEAD), pl.ds(first, block)]
-        grad = grad_mixed[pl.ds(first_row, HEAD), pl.ds(first, block)]
-        scores = jnp.dot(key_rows[pl.ds(first, window), :], query, preferred_element_type=F32)
-        allowed = scores_mask(first - pad, first, window, block, scalars)
-        exponent = jnp.where(allowed, scores * 0.125 - lse_ref[0, :, pl.ds(first, block)], NEGATIVE)
-        probs = jnp.exp(exponent)
-        grad_probs = jnp.dot(
-            value_rows[pl.ds(first, window), :], grad, preferred_element_type=F32
-        )
-        inner = jnp.sum(probs * grad_probs, axis=0, keepdims=True)
-        raw = (0.125 * (probs * (grad_probs - inner))).astype(BF16)
-        grad_query = jnp.dot(key_pad[:, pl.ds(first, window)], raw, preferred_element_type=F32)
-        out_ref[
-            first // quarter, 0, :, pl.ds(pl.multiple_of(first % quarter, block), block)
-        ] = grad_query.astype(BF16)
-        grad_value[:, pl.ds(first, window)] += lax.dot_general(
-            grad, probs.astype(BF16), contract_last, preferred_element_type=F32
-        )
-        grad_key[:, pl.ds(first, window)] += lax.dot_general(
-            query, raw, contract_last, preferred_element_type=F32
-        )
+
+        def body(window):
+            begin = pl.multiple_of(first + pad + block - window, block)
+            query = qkv_ref[pl.ds(first_row, HEAD), pl.ds(first, block)]
+            grad = grad_mixed[pl.ds(first_row, HEAD), pl.ds(first, block)]
+            scores = jnp.dot(key_rows[pl.ds(begin, window), :], query, preferred_element_type=F32)
+            allowed = scores_mask(begin - pad, first, window, block, scalars)
+            exponent = scores * 0.125 - lse_ref[0, :, pl.ds(first, block)]
+            probs = jnp.exp(jnp.where(allowed, exponent, NEGATIVE))
+            grad_probs = jnp.dot(
+                value_rows[pl.ds(begin, window), :], grad, preferred_element_type=F32
+            )
+            inner = jnp.sum(probs * grad_probs, axis=0, keepdims=True)
+            raw = (0.125 * (probs * (grad_probs - inner))).astype(BF16)
+            grad_query = jnp.dot(
+                key_pad[:, pl.ds(begin, window)], raw, preferred_element_type=F32
+            )
+            column = pl.multiple_of(first % quarter, block)
+            out_ref[first // quarter, 0, :, pl.ds(column, block)] = grad_query.astype(BF16)
+            grad_value[:, pl.ds(begin, window)] += lax.dot_general(
+                grad, probs.astype(BF16), contract_last, preferred_element_type=F32
+            )
+            grad_key[:, pl.ds(begin, window)] += lax.dot_general(
+                query, raw, contract_last, preferred_element_type=F32
+            )
+
+        for_window(first, block, pad, scalars, body)
         return carry
 
     lax.fori_loop(0, group // block, one, 0)
@@ -301,10 +326,7 @@
 def inputs_back_kernel(scalars, grads, p0, p1, p2, p3, x_ref, gain_ref, hidden_ref, out_ref, sum_ref):
     total = 0.0
     for r, weight in enumerate((p0, p1, p2, p3)):
-        total += lax.dot_general(
-            grads[scalars[1] ^ r].T, weight[...], (((1,), (1,)), ((), ())),
-            preferred_element_type=F32,
-        )
+        total += jnp.dot(grads[scalars[1] ^ r].T, weight[...], preferred_element_type=F32)
     x = x_ref[...]
     scale = lax.rsqrt(jnp.mean(x * x, axis=1, keepdims=True) + EPSILON)
     through = total * gain_ref[...]
@@ -346,8 +368,9 @@
 
 
 def expert_kernel(
-    kinds, scalars, w_gate, w_other, *refs
+    kinds, scalars, w_gate, w_near, *refs
 ):
+    far_pieces, refs = refs[:4], refs[4:]
     x_blocks, g_blocks, refs = refs[: 2 * LOW], refs[2 * LOW : 4 * LOW], refs[4 * LOW :]
     back_own, back_send, feed_own, feed_send, grads_gate, grads_other, *refs = refs
     x_all, g_all, x_t, g_t, weights, hidden, acc_feed, acc_back, scales, plain = refs
@@ -380,9 +403,17 @@
 
     for i in range(2):
         rows = pl.ds(i * half, half)
-        weights[0, rows, :] = w_gate[i, :, 0].reshape(half, units)
-        weights[1, rows, :] = w_other[i, :, 0, 0].reshape(half, units)
-        weights[2, rows, :] = w_other[i, :, 0, 1].reshape(half, units)
+        weights[0, rows, :] = w_gate[:, 0, i].reshape(half, units)
+    near = pl.multiple_of(scalars[1] * half, half)
+    for k in range(2):
+        weights[k + 1, pl.ds(near, half), :] = w_near[:, 0, k].reshape(half, units)
+        place = (1 - scalars[1]) * half
+        for piece in far_pieces[2 * k : 2 * k + 2]:
+            rows = piece.shape[0] * half // LOW
+            weights[k + 1, pl.ds(pl.multiple_of(place, half // LOW), rows), :] = piece[
+                :, 0
+            ].reshape(rows, units)
+            place += rows
 
     for part in range(2):
         rows = pl.ds(part * slots, slots)
@@ -436,10 +467,10 @@
                 feed_send[...] = feed.astype(BF16)
 
 
-def expert_pass(kinds, expert, x_blocks, g_blocks, w_gate, w_other):
+def expert_pass(kinds, scalars, x_blocks, g_blocks, w_gate, w_near, w_far):
     block, width = g_blocks[0].shape
     slots = LOW * block
-    _, low, parities, _, shard_rows, shard_units = w_other.shape
+    low, parities, _, shard_rows, shard_units = w_gate.shape
     units = 256
     steps = shard_units // units
 
@@ -448,14 +479,21 @@
             shape, lambda i, _: (0,) * len(shape), pipeline_mode=pl.Buffered(1)
         )
 
-    weight_specs = [
-        pl.BlockSpec(
-            (2, low, 1, shard_rows, units), lambda i, _: (0, 0, i // steps, 0, i % steps)
-        ),
-        pl.BlockSpec(
-            (2, low, 1, 2, shard_rows, units), lambda i, _: (0, 0, i // steps, 0, 0, i % steps)
-        ),
-    ]
+    both_spec = pl.BlockSpec(
+        (2, low, 1, shard_rows, units), lambda i, _: (0, 0, i // steps, 0, i % steps)
+    )
+    other_spec = pl.BlockSpec(
+        (2, low, 1, 2, shard_rows, units), lambda i, _: (0, 0, i // steps, 0, 0, i % steps)
+    )
+
+    gate_spec = pl.BlockSpec(
+        (low, 1, 2, shard_rows, units), lambda i, _: (0, i // steps, 0, 0, i % steps)
+    )
+    def up_spec(count):
+        return pl.BlockSpec(
+            (count, 1, shard_rows, units), lambda i, _: (0, i // steps, 0, i % steps)
+        )
+
     wide = width + 128
     return pl.pallas_call(
         functools.partial(expert_kernel, kinds),
@@ -463,7 +501,9 @@
             num_scalar_prefetch=1,
             grid=(parities * steps,),
             in_specs=[
-                *weight_specs,
+                gate_spec,
+                gate_spec,
+                *[up_spec(item.shape[0]) for item in w_far],
                 *[whole((block, wide)) for _ in range(2 * LOW)],
                 *[whole((block, width)) for _ in range(2 * LOW)],
             ],
@@ -472,7 +512,8 @@
                 whole((slots, wide)),
                 whole((slots, width)),
                 whole((slots, width)),
-                *weight_specs,
+                both_spec,
+                other_spec,
             ],
             scratch_shapes=[
                 pltpu.VMEM((2 * slots, width), BF16),
@@ -492,13 +533,13 @@
             jax.ShapeDtypeStruct((slots, wide), BF16),
             jax.ShapeDtypeStruct((slots, width), F32),
             jax.ShapeDtypeStruct((slots, width), BF16),
-            jax.ShapeDtypeStruct(w_gate.shape, BF16),
-            jax.ShapeDtypeStruct(w_other.shape, BF16),
+            jax.ShapeDtypeStruct((2, low, parities, shard_rows, shard_units), BF16),
+            jax.ShapeDtypeStruct((2, low, parities, 2, shard_rows, shard_units), BF16),
         ],
         compiler_params=pltpu.CompilerParams(vmem_limit_bytes=58 * 2**20),
         cost_estimate=cost_of(35),
         name="expert_pass",
-    )(expert.reshape(1), w_gate, w_other, *x_blocks, *g_blocks)
+    )(scalars, w_gate, w_near, *w_far, *x_blocks, *g_blocks)
 
 
 def pick_kernel(ids_ref, *refs):
@@ -737,9 +778,12 @@
     rounded = (hidden * scale * gain_ref[...]).astype(BF16)
     width = hidden.shape[1]
     sent_ref[:, :width] = rounded
-    logits = jnp.dot(
-        rounded.astype(F32), router_w[...], precision=PRECISE, preferred_element_type=F32
-    ) + jnp.dot(prior_ref[...], prior_w[...], precision=PRECISE, preferred_element_type=F32)
+    router_high, router_low = halves(router_w[...])
+    logits = (
+        jnp.dot(rounded, router_high, preferred_element_type=F32)
+        + jnp.dot(rounded, router_low, preferred_element_type=F32)
+        + split_dot(prior_ref[...], prior_w[...])
+    )
     lanes = lax.broadcasted_iota(jnp.int32, logits.shape, 1)
     logits = jnp.where(lanes < 2 * kinds, logits, NEGATIVE)
     weights = jnp.exp(logits - jnp.max(logits, axis=1, keepdims=True))
@@ -806,7 +850,7 @@
     )
 
 
-def router_back_kernel(kinds, experts, scalars, near_ref, far_ref, hidden_ref, router_ref,
+def router_back_kernel(kinds, experts, scalars, near_ref, got_ref, far_ref, hidden_ref, router_ref,
                        routes_ref, cotangent_ref, prior_ref, gain_ref, small_ref, small_t_ref,
                        vector_ref, prior_w_ref,
                        grad_hidden_ref, grad_low_ref, partial_ref, grad_prior_ref, sums_ref):
@@ -815,7 +859,7 @@
     place = scalars[1] * rows * pl.num_programs(0) + step * rows
     valid = place + lax.broadcasted_iota(jnp.int32, (rows, 1), 0) < scalars[BOUNDS + 2]
     valid = jnp.where(valid, 1.0, 0.0)
-    back = near_ref[...] + far_ref[...].astype(F32)
+    back = near_ref[0] + got_ref[0].astype(F32) + far_ref[...].astype(F32)
     hidden = hidden_ref[...]
     grad_out = cotangent_ref[...] * valid
     scale = lax.rsqrt(jnp.mean(hidden * hidden, axis=1, keepdims=True) + EPSILON)
@@ -907,7 +951,7 @@
     sums_ref[pl.ds(kinds + 8, kinds), : lanes.shape[1]] += prior
 
 
-def router_back(kinds, experts, scalars, near, far, hidden, router, routes, cotangent, prior,
+def router_back(kinds, experts, scalars, near, got, far, hidden, router, routes, cotangent, prior,
                 gain, small, small_t, vector, prior_w):
     rows, width = hidden.shape
     block = rows // 2
@@ -928,7 +972,8 @@
             num_scalar_prefetch=1,
             grid=(2,),
             in_specs=[
-                part(width + lanes),
+                pl.BlockSpec((1, block, width + lanes), lambda i, _: (0, i, 0)),
+                pl.BlockSpec((1, block, width + lanes), lambda i, _: (0, i, 0)),
                 part(width + lanes),
                 part(width),
                 part(lanes),
@@ -959,17 +1004,13 @@
         compiler_params=pltpu.CompilerParams(vmem_limit_bytes=48 * 2**20),
         cost_estimate=cost_of(8),
         name="router_back",
-    )(scalars, near, far, hidden, router, routes, cotangent, prior, gain, small, small_t,
+    )(scalars, near, got, far, hidden, router, routes, cotangent, prior, gain, small, small_t,
       vector, prior_w)
 
 
 def two_parts(value):
     high = lax.reduce_precision(value, 8, 7)
     return jnp.concatenate([high, value - high], axis=-1).astype(BF16)
-
-
-def after(value, *others):
-    return lax.optimization_barrier((value, *others))[0]
 
 
 def everywhere(value, axes, count):
@@ -1008,16 +1049,16 @@
         full = lax.all_gather(value, ("hi", "lo"), axis=0, tiled=True)
         full = full.reshape(2, LOW, -1, full.shape[1])
         return [full[:, i] for i in range(LOW)], later
-    far, later = lax.optimization_barrier((swap(value, "hi"), later))
+    far, *later = lax.optimization_barrier((swap(value, "hi"), *later))
     both = jnp.stack([value, far])
-    return [both] + [flip(both, "lo", LOW, bit) for bit in range(1, LOW)], later
+    return [both] + [flip(both, "lo", LOW, bit) for bit in range(1, LOW)], tuple(later)
 
 
 def scatter_rows(near, far, many):
     if many != 2:
         full = jnp.stack([near, far]).astype(F32).reshape(-1, near.shape[2])
         return lax.psum_scatter(full, ("hi", "lo"), scatter_dimension=0, tiled=True)
-    both = near.astype(F32) + swap(far, "hi").astype(F32)
+    both = near.astype(F32) + far.astype(F32)
     total = both[0]
     for bit in range(1, LOW):
         total = total + flip(both[bit].astype(BF16), "lo", LOW, bit).astype(F32)
@@ -1070,29 +1111,28 @@
     ).astype(jnp.int32)
     gain_one, gain_two = attn_gain.reshape(1, width), moe_gain.reshape(1, width)
 
+    valid_mine = place_in_group * tok_rows + jnp.arange(tok_rows)[:, None] < boundary[-2]
+    valid_mine = valid_mine.astype(F32)
+
     normed_one = rms_norm(inputs, attn_gain).astype(BF16)
     normed_other = swap(normed_one, "y")
     attn_shard = jnp.concatenate([w_query, w_key, w_value, w_out.T], axis=1)
-    attn_shards, w_gate = gather_rows(attn_shard, w_gate, many)
     other_shards = jnp.stack([w_up, w_down.transpose(0, 2, 1)], axis=1)
+    attn_shards, (w_gate, other_shards, _) = gather_rows(
+        attn_shard, (w_gate, other_shards, normed_one), many
+    )
+    gate_far = swap(w_gate, "hi") if many == 2 else w_gate
+    attn_shards[0], scalars = lax.optimization_barrier((attn_shards[0], scalars))
+    ids_rows, ids_cols = slots_of(scalars, routes, drop_order, experts, capacity)
+    grad_out_low = (cotangent * valid_mine).astype(BF16)
+    grad_out_other = swap(grad_out_low, "y")
+    (
+        normed_other, attn_shards, ids_rows, prior_logits, other_shards, grad_out_other
+    ) = lax.optimization_barrier(
+        (normed_other, attn_shards, ids_rows, prior_logits, other_shards, grad_out_other)
+    )
     other_part = lax.all_to_all(other_shards, ("lo", "y"), 0, 0, tiled=True)
     other_part = other_part.reshape(LOW, 2, 2, shard_rows, shard_units)
-    if many == 2:
-        gate_far = swap(w_gate, "hi")
-        gate_both = jnp.where(
-            high == 0, jnp.stack([w_gate, gate_far], axis=1), jnp.stack([gate_far, w_gate], axis=1)
-        )
-    else:
-        gate_both = lax.all_gather(w_gate, "hi", axis=1)
-    gate_part = lax.all_to_all(gate_both, ("lo", "y"), 0, 0, tiled=True)
-    gate_part = gate_part.reshape(LOW, 2, many, shard_rows, shard_units).transpose(2, 0, 1, 3, 4)
-    ids_rows, ids_cols = slots_of(
-        after(scalars, attn_shards[0]), routes, drop_order, experts, capacity
-    )
-    normed_other, attn_shards, other_part, ids_rows = lax.optimization_barrier(
-        (normed_other, attn_shards, other_part, ids_rows)
-    )
-    w_other = by_halves(lax.all_gather(other_part, "hi"))
     out_mine = jnp.stack([item[:, :, 3 * local_width :] for item in attn_shards])
     out_other = swap(out_mine, "y")
     normed_pieces = [normed_one, swap(normed_one, "c"), normed_other, swap(normed_other, "c")]
@@ -1106,41 +1146,63 @@
         (attn_shards, router_lanes, prior_lanes, small, small_t, prior_back)
     )
 
-    valid_mine = place_in_group * tok_rows + jnp.arange(tok_rows)[:, None] < boundary[-2]
-    valid_mine = valid_mine.astype(F32)
-    grad_out_low = (cotangent * valid_mine).astype(BF16)
-    grad_out_other = swap(after(grad_out_low, normed_pieces[3]), "y")
     mixed, lse, qkv, qkv_full, out_full = attend(normed_pieces, attn_shards, scalars, heads)
-    mixed, grad_out_other, gate_part, out_other = lax.optimization_barrier(
-        (mixed, grad_out_other, gate_part, out_other)
-    )
-    out_pieces = [out_mine, swap(after(out_mine, mixed), "c"), out_other, swap(out_other, "c")]
+    mixed, out_other, out_mine, gate_far = lax.optimization_barrier(
+        (mixed, out_other, out_mine, gate_far)
+    )
+    if many == 2:
+        w_near, high_place = other_part, high
+        w_far = [
+            swap(other_part[first:last, :, k], "hi")
+            for k, first, last in ((0, 0, 1), (0, 1, 4), (1, 0, 1), (1, 1, 4))
+        ]
+        gate_both = jnp.where(
+            high == 0, jnp.stack([w_gate, gate_far], axis=1), jnp.stack([gate_far, w_gate], axis=1)
+        )
+    else:
+        w_all = by_halves(lax.all_gather(other_part, "hi"))
+        w_near, high_place = w_all[0], jnp.zeros_like(high)
+        w_far = [
+            w_all[1, first:last, :, k]
+            for k, first, last in ((0, 0, 1), (0, 1, 4), (1, 0, 1), (1, 1, 4))
+        ]
+        gate_both = lax.all_gather(w_gate, "hi", axis=1)
+    out_pieces = [out_mine, swap(out_mine, "c"), out_other, swap(out_other, "c")]
 
     mixed_mine = lax.all_to_all(mixed, tp_axes, 0, 0, tiled=True)
     grad_out_pieces = [
-        grad_out_low, swap(after(grad_out_low, mixed), "c"), grad_out_other, swap(grad_out_other, "c"),
+        grad_out_low, swap(grad_out_low, "c"), grad_out_other, swap(grad_out_other, "c"),
     ]
     grad_out_slots = pick(ids_rows, grad_out_pieces, slots)
-    mixed_mine, grad_out_slots = lax.optimization_barrier((mixed_mine, grad_out_slots))
+    mixed_mine, grad_out_slots, w_far[0], gate_both = lax.optimization_barrier(
+        (mixed_mine, grad_out_slots, w_far[0], gate_both)
+    )
 
     hidden, sent_two, router = middle(
         kinds, scalars, mixed_mine, out_pieces, inputs, gain_two, router_lanes, prior_logits, prior_lanes
     )
 
-    pieces_two = gather_pieces(sent_two)
-    grad_taken = to_experts(grad_out_slots)
-    pieces_two, grad_taken = lax.optimization_barrier((pieces_two, grad_taken))
+    gate_part = lax.all_to_all(gate_both, ("lo", "y"), 0, 0, tiled=True)
+    gate_part = gate_part.reshape(LOW, 2, many, shard_rows, shard_units)
+    if many != 2:
+        gate_part = by_halves(gate_part.transpose(2, 0, 1, 3, 4)).transpose(1, 2, 0, 3, 4)
+    other_two, grad_taken, gate_part, w_far[1], w_far[2] = lax.optimization_barrier(
+        (swap(sent_two, "y"), to_experts(grad_out_slots), gate_part, w_far[1], w_far[2])
+    )
+    pieces_two = [sent_two, swap(sent_two, "c"), other_two, swap(other_two, "c")]
 
     grad_taken += [swap(item, "c") for item in grad_taken]
     sent_slots = pick(ids_rows, pieces_two, slots)
+    sent_slots, qkv_full = lax.optimization_barrier((sent_slots, qkv_full))
     taken = to_experts(sent_slots)
     taken += [swap(item, "c") for item in taken]
-    qkv_pieces = gather_pieces(after(qkv_full, sent_slots[0]))
-    taken, qkv_pieces = lax.optimization_barrier((taken, qkv_pieces))
+    qkv_pieces = gather_pieces(qkv_full)
+    taken, qkv_pieces, w_far[3] = lax.optimization_barrier((taken, qkv_pieces, w_far[3]))
 
     expert = lax.axis_index("lo") * 2 + parity
     back_own, back_send, feed_own, feed_send, grads_gate, grads_other = expert_pass(
-        kinds, expert.astype(jnp.int32), taken, grad_taken, by_halves(gate_part), w_other
+        kinds, jnp.stack([expert, high_place]).astype(jnp.int32), taken, grad_taken,
+        gate_part, w_near, w_far,
     )
 
     other_sum = scatter_high(grads_other, many)
@@ -1149,49 +1211,58 @@
     feed_core = swap(feed_send, "c")
     back_taken, feed_core = lax.optimization_barrier((back_taken, feed_core))
 
-    back_near, back_other = add_core(*spread(ids_cols, back_taken, tok_rows))
-    back_far = swap(back_other, "y")
-    feed_taken = to_experts(feed_sum(feed_own, after(feed_core, back_other)))
-    back_far, feed_taken = lax.optimization_barrier((back_far, feed_taken))
+    back_near, back_sent = spread(ids_cols, back_taken, tok_rows)
+    back_got, back_other = add_core(back_near, back_sent)
+    back_other, feed_core = lax.optimization_barrier((back_other, feed_core))
+    back_far, feed_blocks = lax.optimization_barrier(
+        (swap(back_other, "y"), feed_sum(feed_own, feed_core))
+    )
 
     grad_hidden, grad_low, partial, grad_prior, sums = router_back(
-        kinds, experts, scalars, back_near, back_far, hidden, router, routes, cotangent,
+        kinds, experts, scalars, back_near, back_got, back_far, hidden, router, routes, cotangent,
         prior_logits, gain_two, small, small_t, const_vector, prior_back,
     )
-    grad_attn_pieces = gather_pieces(grad_low)
-    feed_near, feed_other = add_core(
-        *spread(ids_cols, [after(item, grad_attn_pieces[2]) for item in feed_taken], tok_rows)
-    )
-    sums = after(sums, grad_attn_pieces[2])
-    share_sums = lax.all_to_all(sums.reshape(count, 32 * width // count), all_axes, 0, 0, tiled=True)
-    share_sums = jnp.sum(share_sums, axis=0)
-
-    feed_far = swap(feed_other, "y")
+    feed_taken = to_experts(feed_blocks)
+    low_other = swap(grad_low, "y")
+    grad_attn_pieces = [grad_low, swap(grad_low, "c"), low_other, swap(low_other, "c")]
     other_own = lax.all_to_all(
         other_sum.reshape(2 * LOW, 2, shard_rows, shard_units), ("lo", "y"), 0, 0, tiled=True
     )
     grad_qkv = attend_back(scalars, qkv, lse, out_full, grad_attn_pieces, heads).reshape(
         4, 3 * local_width, tok_rows
     )
-    grad_qkv, other_own, feed_far, share_sums, gate_sum = lax.optimization_barrier(
-        (grad_qkv, other_own, feed_far, share_sums, gate_sum)
-    )
+    grad_qkv, other_own, feed_taken = lax.optimization_barrier((grad_qkv, other_own, feed_taken))
 
     grad_qkv_mine = lax.all_to_all(grad_qkv, tp_axes, 0, 0, tiled=True)
+    attn_near, attn_far = attn_grads(grad_qkv, mixed, normed_pieces, grad_attn_pieces, scalars)
+    if many == 2:
+        attn_far = swap(attn_far, "hi")
+    feed_near, feed_sent = spread(ids_cols, feed_taken, tok_rows)
+    feed_got, feed_other = add_core(feed_near, feed_sent)
+    (
+        grad_qkv_mine, sums, gate_sum, attn_near, attn_far, feed_near, feed_got, feed_other
+    ) = lax.optimization_barrier(
+        (grad_qkv_mine, sums, gate_sum, attn_near, attn_far, feed_near, feed_got, feed_other)
+    )
+    feed_far = swap(feed_other, "y")
+    sums = sums.reshape(count, 32 * width // count)
+    share_sums = lax.all_to_all(sums, all_axes, 0, 0, tiled=True)
+    share_sums, gate_sum = lax.optimization_barrier((share_sums, gate_sum))
+    share_sums = jnp.sum(share_sums, axis=0)
     gate_own = lax.all_to_all(
-        after(gate_sum, grad_qkv_mine).reshape(2 * LOW, shard_rows, shard_units),
-        ("lo", "y"), 0, 0, tiled=True,
-    )
-    output = partial + valid_mine * (feed_near + feed_far.astype(F32))
-    grad_attn_own = scatter_rows(
-        *attn_grads(grad_qkv, mixed, normed_pieces, grad_attn_pieces, scalars), many
+        gate_sum.reshape(2 * LOW, shard_rows, shard_units), ("lo", "y"), 0, 0, tiled=True
     )
     grad_inputs, gain_part = inputs_back(
         scalars, grad_qkv_mine, qkv_pieces, inputs, gain_one, grad_hidden
     )
-    last = everywhere(
-        jnp.concatenate([jnp.sum(gain_part, axis=0).reshape(-1), share_sums]), all_axes, count
-    )
+    output = partial + valid_mine * (
+        feed_near[0] + feed_got[0].astype(F32) + feed_far.astype(F32)
+    )
+    grad_attn_own = scatter_rows(attn_near, attn_far, many)
+    last = jnp.concatenate([jnp.sum(gain_part, axis=0).reshape(-1), share_sums])
+    last, gate_own = lax.optimization_barrier((last, gate_own))
+    last = everywhere(last, all_axes, count)
+    last, grad_attn_own = lax.optimization_barrier((last, grad_attn_own))
     grad_gain = jnp.sum(last[:, :width], axis=0)
     total = last[:, width:].reshape(32, width)
     return (

time: 567 us -> 542 us (0.956)
  Pallas kernels: 159 us -> 142 us
  waiting for transfers between devices: 212 us -> 202 us
    ppermute x18, waiting for transfers between devices: 103 us -> 39.5 us  [flip(): return lax.ppermute(value, axis, [(i, i ^ bit) for i in range(size)])]
    ppermute x35 -> x39, waiting for transfers between devices: 85.2 us -> 137 us  [swap(): return lax.ppermute(value, axis, [(0, 1), (1, 0)])]
    all_to_all x1, waiting for transfers between devices: 0.01 us -> 15.4 us  [per_device(): lax.all_to_all(other_sum.reshape(2 * LOW, 2, shard_rows, shard_units), ('...]
    all_to_all x1, waiting for transfers between devices: 11.9 us -> 0.01 us  [per_device(): grad_qkv_mine = lax.all_to_all(grad_qkv, tp_axes, 0, 0, tiled=True)]
    pallas_call x1, Pallas kernels: 35.5 us -> 24.2 us  [attend_back(): pl.pallas_call(functools.partial(attend_back_kernel, block, MAXLEN), grid...]
    unnamed x166 -> x176, local copies, waits for them, and re-layouts: 28.5 us -> 30.7 us
    ppermute x35 -> x39, starting transfers between devices: 37.9 us -> 37.8 us  [swap(): return lax.ppermute(value, axis, [(0, 1), (1, 0)])]
  transfers between devices with their start and end apart: 64 -> 67, of which waited for: 32 -> 27; matrix products, arithmetic and copies ran while one was open for 9% -> 9% of each run, Pallas kernels for 20% -> 19%
where the time goes in v4:
time: 542 us; the launch traced here: 531 us
  waiting for transfers between devices  202 us (37%)
  Pallas kernels  142 us (26%)
  starting transfers between devices  91.5 us (17%)
  local copies, waits for them, and re-layouts  45.7 us (8%)
  other arithmetic  34.9 us (6%)
  between operations  15.1 us (3%)
    ppermute x39, waiting for transfers between devices, swap(): return lax.ppermute(value, axis, [(0, 1), (1, 0)])  137 us
    ppermute x18, waiting for transfers between devices, flip(): return lax.ppermute(value, axis, [(i, i ^ bit) for i in range(size)])  39.5 us
    ppermute x39, starting transfers between devices, swap(): return lax.ppermute(value, axis, [(0, 1), (1, 0)])  37.8 us
    pallas_call x1, Pallas kernels, expert_pass(): pl.pallas_call(functools.partial(expert_kernel, kinds), grid_spec=pltpu.P...  37.5 us
    unnamed x176, local copies, waits for them, and re-layouts  30.7 us
    pallas_call x1, Pallas kernels, attend_back(): pl.pallas_call(functools.partial(attend_back_kernel, block, MAXLEN), grid...  24.2 us
    pallas_call x1, Pallas kernels, attend(): pl.pallas_call(functools.partial(attend_kernel, block, MAXLEN), grid_spec...  19.9 us
    ppermute x18, starting transfers between devices, flip(): return lax.ppermute(value, axis, [(i, i ^ bit) for i in range(size)])  16.2 us
  transfers between devices with their start and end apart: 67, of which 27 were waited for; matrix products, arithmetic and copies ran while one was open for 9% of the time, Pallas kernels for 19%

profile of v4, /device:TPU:1, one launch (start us, length us, event | category | flops | bytes accessed | tf_op | source)
XLA Modules:
  0.0 531.4 jit_solution(3450637717029535527)
XLA Ops:
  9.8 3.1 collective-permute-start
  18.2 2.4 multiply_convert_fusion.refs_0_
  25.1 2.7 pad_maximum_fusion
  31.5 10.0 %slots.1 = (s32[8,2048]{1,0:T(8,128)S(1)}, s32[2048,8]{1,0:T(8,128)S(1)}) custom-call(s32[8]{0:T(128)S(1)} %concatenate.19.scalars, s32[2048,2]{1,0:T(8,128)S(1)} %copy.51.routes_col.routes_ref, s32[2048,2]{1,0:T(8,128)S(1)} %copy.52.order_col, s32[2,2048]{1,0:T(2,128)S(1)} %bitcast.99, s32[2,2048]{1,0:T(2,128)S(1)} %bitcast.100), custom_call_target="tpu_custom_call" | custom-call | flops 9200000000 | bytes 1048576 | tf_op jit(solution)/shard_map/slots/pallas_call | solution.py:749
  43.0 2.3 collective-permute-start.1
  46.1 3.9 collective-permute-done.6.refs_2_
  52.9 4.6 all-to-all-start.1
  61.1 19.9 %attend.1 = (bf16[4,192,512]{2,1,0:T(8,128)(2,1)}, f32[3,1,2048]{2,1,0:T(1,128)S(1)}, bf16[576,2048]{1,0:T(8,128)(2,1)}, bf16[576,768]{1,0:T(8,128)(2,1)}, bf16[768,192]{1,0:T(8,128)(2,1)S(1)}) custom-call(s32[8]{0:T(128)S(1)} %concatenate.19.scalars, bf16[512,768]{1,0:T(8,128)(2,1)S(1)} %multiply_convert_fusion.1.refs_0_.refs_2_, ...), custom_call_target="tpu_custom_call" | custom-call | flops 27599998976 | bytes 1048576 | tf_op jit(solution)/shard_map/attend/pallas_call | solution.py:153
  81.0 9.1 %collective-permute-done.9 = bf16[8,96,512]{2,1,0:T(8,128)(2,1)} collective-permute-done((bf16[8,96,512]{2,1,0:T(8,128)(2,1)}, bf16[8,96,512]{2,1,0:T(8,128)(2,1)}, u32[]{:S(2)}, u32[]{:S(2)}) %collective-permute-start.9) | collective-permute-done | bytes 786464 | tf_op jit(solution)/shard_map/ppermute | solution.py:29
  90.2 3.4 all-to-all-done.1
  93.6 4.7 all-to-all-start
  101.1 4.8 pick.2
  108.1 3.3 maximum_select_fusion
  113.3 4.7 all-to-all-start.2
  121.5 5.8 %middle.1 = (f32[512,768]{1,0:T(8,128)}, bf16[512,896]{1,0:T(8,128)(2,1)}, f32[512,128]{1,0:T(8,128)S(1)}) custom-call(s32[8]{0:T(128)S(1)} %concatenate.19.scalars, bf16[4,192,512]{2,1,0:T(8,128)(2,1)S(1)} %all-to-all-done.mixed, bf16[4,2,96,192]{3,2,1,0:T(8,128)(2,1)} %pad_maximum_fusion.1.p0, bf16[4,2,96,192]{3,2,1,0:T(8,128)(2,1)} %collective-permute-done.13.p1, ...), custom_call_target="tpu_custom_call" | custom-call | flops 6899999744 | bytes 1048576 | tf_op jit(solution)/shard_map/middle/pallas_call | solution.py:804
  134.7 31.5 %collective-permute-done.20.refs_2_ = bf16[1,2,96,512]{3,2,1,0:T(8,128)(2,1)S(1)} collective-permute-done((bf16[1,2,96,512]{3,2,1,0:T(8,128)(2,1)S(1)}, bf16[1,2,96,512]{3,2,1,0:T(8,128)(2,1)S(1)}, u32[]{:S(2)}, u32[]{:S(2)}) %collective-permute-start.20) | collective-permute-done | bytes 196640 | tf_op jit(solution)/shard_map/ppermute | solution.py:29
  167.8 6.4 %collective-permute-done.18.refs_15_ = bf16[192,768]{1,0:T(8,128)(2,1)} collective-permute-done((bf16[192,768]{1,0:T(8,128)(2,1)S(1)}, bf16[192,768]{1,0:T(8,128)(2,1)}, u32[]{:S(2)}, u32[]{:S(2)}) %collective-permute-start.18) | collective-permute-done | bytes 294944 | tf_op jit(solution)/shard_map/ppermute | solution.py:1022
  175.1 2.5 collective-permute-start.22
  179.7 4.9 pick.3
  189.1 24.4 %collective-permute-done.33.refs_3_ = bf16[3,2,96,512]{3,2,1,0:T(8,128)(2,1)S(1)} collective-permute-done((bf16[3,2,96,512]{3,2,1,0:T(8,128)(2,1)S(1)}, bf16[3,2,96,512]{3,2,1,0:T(8,128)(2,1)S(1)}, u32[]{:S(2)}, u32[]{:S(2)}) %collective-permute-start.33) | collective-permute-done | bytes 589856 | tf_op jit(solution)/shard_map/ppermute | solution.py:29
  214.6 8.9 %collective-permute-done.25.refs_7_ = bf16[192,896]{1,0:T(8,128)(2,1)S(1)} collective-permute-done((bf16[192,896]{1,0:T(8,128)(2,1)S(1)}, bf16[192,896]{1,0:T(8,128)(2,1)S(1)}, u32[]{:S(2)}, u32[]{:S(2)}) %collective-permute-start.25) | collective-permute-done | bytes 344096 | tf_op jit(solution)/shard_map/ppermute | solution.py:1022
  230.2 37.5 %expert_pass.1 = (f32[768,896]{1,0:T(8,128)}, bf16[768,896]{1,0:T(8,128)(2,1)}, f32[768,768]{1,0:T(8,128)}, bf16[768,768]{1,0:T(8,128)(2,1)}, bf16[2,4,2,96,512]...) custom-call(s32[2]{0:T(128)} %pad_add_fusion.scalars, bf16[4,2,2,96,512]{4,3,2,1,0:T(8,128)(2,1)} %bitcast.29.w_gate, ...), custom_call_target="tpu_custom_call" | custom-call | flops 40249999360 | bytes 1048576 | tf_op jit(solution)/shard_map/expert_pass/pallas_call | solution.py:498
  268.3 3.6 collective-permute-done.38.core_ref
  278.5 6.7 %collective-permute-done.39.refs_1_ = bf16[192,896]{1,0:T(8,128)(2,1)S(1)} collective-permute-done((bf16[192,896]{1,0:T(8,128)(2,1)}, bf16[192,896]{1,0:T(8,128)(2,1)S(1)}, u32[]{:S(2)}, u32[]{:S(2)}) %collective-permute-start.39) | collective-permute-done | bytes 344096 | tf_op jit(solution)/shard_map/ppermute | solution.py:1022
  285.4 14.0 %collective-permute-done.41.refs_3_ = bf16[192,896]{1,0:T(8,128)(2,1)S(1)} collective-permute-done((bf16[192,896]{1,0:T(8,128)(2,1)}, bf16[192,896]{1,0:T(8,128)(2,1)S(1)}, u32[]{:S(2)}, u32[]{:S(2)}) %collective-permute-start.41) | collective-permute-done | bytes 344096 | tf_op jit(solution)/shard_map/ppermute | solution.py:1022
  300.6 4.1 spread.2
  306.6 3.4 collective-permute-done.43.got_ref
  319.2 14.3 %collective-permute-done.44.far_ref = bf16[512,896]{1,0:T(8,128)(2,1)S(1)} collective-permute-done((bf16[512,896]{1,0:T(8,128)(2,1)}, bf16[512,896]{1,0:T(8,128)(2,1)S(1)}, u32[]{:S(2)}, u32[]{:S(2)}) %collective-permute-start.44) | collective-permute-done | bytes 917536 | tf_op jit(solution)/shard_map/ppermute | solution.py:29
  335.6 9.2 %router_back.1 = (f32[512,768]{1,0:T(8,128)}, bf16[512,768]{1,0:T(8,128)(2,1)}, f32[512,768]{1,0:T(8,128)}, f32[512,12]{1,0:T(8,128)S(1)}, f32[32,768]{1,0:T(8,128)S(1)}) custom-call(s32[8]{0:T(128)S(1)} %concatenate.19.scalars, f32[2,512,896]{2,1,0:T(8,128)} %copy-done.3, bf16[2,512,896]{2,1,0:T(8,128)(2,1)} %copy-done.58, bf16[512,896]{1,0:T(8,128)(2,1)S(1)} %copy-done.17, ...), custom_call_target="tpu_custom_call" | custom-call | flops 9200000000 | bytes 1048576 | tf_op jit(solution)/shard_map/router_back/pallas_call | solution.py:969
  347.4 15.7 %collective-permute-done.46.refs_2_.refs_8_ = bf16[512,768]{1,0:T(8,128)(2,1)S(1)} collective-permute-done((bf16[512,768]{1,0:T(8,128)(2,1)}, bf16[512,768]{1,0:T(8,128)(2,1)S(1)}, u32[]{:S(2)}, u32[]{:S(2)}) %collective-permute-start.46) | collective-permute-done | bytes 786464 | tf_op jit(solution)/shard_map/ppermute | solution.py:29
  368.0 4.3 all-to-all-start.3
  373.7 24.2 %attend_back.1 = bf16[4,3,192,512]{3,2,1,0:T(8,128)(2,1)S(1)} custom-call(s32[8]{0:T(128)S(1)} %concatenate.19.scalars, bf16[576,2048]{1,0:T(8,128)(2,1)} %get-tuple-element.247.qkv_ref, f32[3,1,2048]{2,1,0:T(1,128)S(1)} %get-tuple-element.248.lse_ref, bf16[768,192]{1,0:T(8,128)(2,1)S(1)} %copy-done.54, bf16[512,768]{1,0:T(8,128)(2,1)} %get-tuple-element.250.refs_0_.refs_6_, ...), custom_call_target="tpu_custom_call" | custom-call | flops 39099998208 | bytes 1048576 | tf_op jit(solution)/shard_map/attend_back/pallas_call | solution.py:298
  399.4 15.4 %all-to-all-done.3 = bf16[8,2,96,512]{3,2,1,0:T(8,128)(2,1)} async-done(((bf16[8,2,96,512]{3,2,1,0:T(8,128)(2,1)}), bf16[8,2,96,512]{3,2,1,0:T(8,128)(2,1)}, u32[]{:S(2)}, u32[]{:S(2)}) %all-to-all-start.3) | async-done | bytes 1572896 | tf_op jit(solution)/shard_map/all_to_all | solution.py:1228
  417.0 5.1 spread.3
  423.3 4.7 all-to-all-start.4
  429.1 7.3 %attn_grads.1 = (bf16[4,96,768]{2,1,0:T(8,128)(2,1)S(1)}, bf16[4,96,768]{2,1,0:T(8,128)(2,1)}) custom-call(s32[8]{0:T(128)S(1)} %concatenate.19.scalars, bf16[4,576,512]{2,1,0:T(8,128)(2,1)} %bitcast.97, bf16[4,192,512]{2,1,0:T(8,128)(2,1)} %get-tuple-element.170.refs_1_, bf16[512,768]{1,0:T(8,128)(2,1)S(1)} %copy-done.5, ...), custom_call_target="tpu_custom_call" | custom-call | flops 9200000000 | bytes 1048576 | tf_op jit(solution)/shard_map/attn_grads/pallas_call | solution.py:211
  440.7 25.3 %collective-permute-done.51 = bf16[4,96,768]{2,1,0:T(8,128)(2,1)} collective-permute-done((bf16[4,96,768]{2,1,0:T(8,128)(2,1)}, bf16[4,96,768]{2,1,0:T(8,128)(2,1)}, u32[]{:S(2)}, u32[]{:S(2)}) %collective-permute-start.51) | collective-permute-done | bytes 589856 | tf_op jit(solution)/shard_map/ppermute | solution.py:29
  466.8 3.7 all-to-all-start.5
  470.5 3.5 convert_bitcast_fusion
  475.4 2.8 all-to-all-done.5
  478.8 4.2 all-to-all-start.6
  483.1 2.5 fusion.9
  486.3 2.2 collective-permute-start.56
  490.1 6.5 %inputs_back.1 = (f32[512,768]{1,0:T(8,128)}, f32[2,1,768]{2,1,0:T(1,128)S(1)}) custom-call(s32[8]{0:T(128)S(1)} %concatenate.19.scalars, bf16[4,576,512]{2,1,0:T(8,128)(2,1)} %all-to-all-done.4.grads, bf16[576,768]{1,0:T(8,128)(2,1)S(1)} %copy-done.19, bf16[576,768]{1,0:T(8,128)(2,1)S(1)} %copy-done.23, bf16[576,768]{1,0:T(8,128)(2,1)S(1)} %copy-done.21, ...), custom_call_target="tpu_custom_call" | custom-call | flops 6899999744 | bytes 1048576 | tf_op jit(solution)/shard_map/inputs_back/pallas_call | solution.py:346
  502.8 6.2 %all-to-all-start.7 = ((f32[32,1,1536]{2,1,0:T(1,128)}), f32[32,1,1536]{2,1,0:T(1,128)}, u32[]{:S(2)}, u32[]{:S(2)}) async-start(f32[32,1,1536]{2,1,0:T(1,128)} %broadcast_in_dim.5), calls=%async_computation.9 | async-start | bytes 393216 | tf_op jit(solution)/shard_map/all_to_all | solution.py:1018
  509.0 3.3 fusion.1
  512.3 2.5 convert_element_type.113
  514.8 3.5 all-to-all-done.7
  (331 shorter events, 116.9 us)
Async XLA Ops:
  9.8 18.0 %collective-permute-start = (bf16[96,768]{1,0:T(8,128)(2,1)}, bf16[96,768]{1,0:T(8,128)(2,1)}, u32[]{:S(2)}, u32[]{:S(2)}) collective-permute-start(bf16[96,768]{1,0:T(8,128)(2,1)} %pad_maximum_fusion.3), channel_id=1, source_target_pairs={{0,16},{16,0},{1,17},{17,1},{2,18},{18,2},{3,19},{19,3},{4,20},{20... | collective-permute-start | bytes 442376 | tf_op jit(solution)/shard_map/ppermute | solution.py:29
  14.9 30.6 %collective-permute-start.2 = (bf16[512,768]{1,0:T(8,128)(2,1)S(1)}, bf16[512,768]{1,0:T(8,128)(2,1)}, u32[]{:S(2)}, u32[]{:S(2)}) collective-permute-start(bf16[512,768]{1,0:T(8,128)(2,1)S(1)} %multiply_convert_fusion.1.refs_0_.refs_2_), channel_id=1, source_target_pairs={{0,2},{2,0},{1,3},{3,1},{4,6},{6,4},{5,7},{7,5},{8,10},{10,8},{9,1... | collective-permute-start | bytes 2359304 | tf_op jit(solution)/shard_map/ppermute | solution.py:29
  20.6 29.4 %collective-permute-start.6 = (bf16[512,768]{1,0:T(8,128)(2,1)}, bf16[512,768]{1,0:T(8,128)(2,1)}, u32[]{:S(2)}, u32[]{:S(2)}) collective-permute-start(bf16[512,768]{1,0:T(8,128)(2,1)} %multiply_convert_fusion.refs_0_), channel_id=1, source_target_pairs={{0,2},{2,0},{1,3},{3,1},{4,6},{6,4},{5,7},{7,5},{8,10},{10,8},{9,1... | collective-permute-start | bytes 2359304 | tf_op jit(solution)/shard_map/ppermute | solution.py:29
  28.7 14.3 %collective-permute-start.3 = (bf16[2,96,768]{2,1,0:T(8,128)(2,1)S(1)}, bf16[2,96,768]{2,1,0:T(8,128)(2,1)S(1)}, u32[]{:S(2)}, u32[]{:S(2)}) collective-permute-start(bf16[2,96,768]{2,1,0:T(8,128)(2,1)S(1)} %pad_maximum_fusion.2.refs_4_), channel_id=1, source_target_pairs={{0,4},{4,0},{8,12},{12,8},{1,5},{5,1},{9,13},{13,9},{2,6},{6,2},{1... | collective-permute-start | bytes 884744 | tf_op jit(solution)/shard_map/ppermute | solution.py:1022
  30.0 15.3 %collective-permute-start.4 = (bf16[2,96,768]{2,1,0:T(8,128)(2,1)S(1)}, bf16[2,96,768]{2,1,0:T(8,128)(2,1)S(1)}, u32[]{:S(2)}, u32[]{:S(2)}) collective-permute-start(bf16[2,96,768]{2,1,0:T(8,128)(2,1)S(1)} %pad_maximum_fusion.2.refs_4_), channel_id=1, source_target_pairs={{0,8},{4,12},{8,0},{12,4},{1,9},{5,13},{9,1},{13,5},{2,10},{6,14},... | collective-permute-start | bytes 884744 | tf_op jit(solution)/shard_map/ppermute | solution.py:1022
  31.3 14.1 %collective-permute-start.5 = (bf16[2,96,768]{2,1,0:T(8,128)(2,1)S(1)}, bf16[2,96,768]{2,1,0:T(8,128)(2,1)S(1)}, u32[]{:S(2)}, u32[]{:S(2)}) collective-permute-start(bf16[2,96,768]{2,1,0:T(8,128)(2,1)S(1)} %pad_maximum_fusion.2.refs_4_), channel_id=1, source_target_pairs={{0,12},{4,8},{8,4},{12,0},{1,13},{5,9},{9,5},{13,1},{2,14},{6,10},... | collective-permute-start | bytes 884744 | tf_op jit(solution)/shard_map/ppermute | solution.py:1022
  43.0 17.1 %collective-permute-start.1 = (bf16[512,768]{1,0:T(8,128)(2,1)S(1)}, bf16[512,768]{1,0:T(8,128)(2,1)}, u32[]{:S(2)}, u32[]{:S(2)}) collective-permute-start(bf16[512,768]{1,0:T(8,128)(2,1)S(1)} %multiply_convert_fusion.1.refs_0_.refs_2_), channel_id=1, source_target_pairs={{0,1},{1,0},{2,3},{3,2},{4,5},{5,4},{6,7},{7,6},{8,9},{9,8},{10,11... | collective-permute-start | bytes 2359304 | tf_op jit(solution)/shard_map/ppermute | solution.py:29
  45.3 55.8 %collective-permute-start.10 = (bf16[512,768]{1,0:T(8,128)(2,1)}, bf16[512,768]{1,0:T(8,128)(2,1)}, u32[]{:S(2)}, u32[]{:S(2)}) collective-permute-start(bf16[512,768]{1,0:T(8,128)(2,1)} %multiply_convert_fusion.refs_0_), channel_id=1, source_target_pairs={{0,1},{1,0},{2,3},{3,2},{4,5},{5,4},{6,7},{7,6},{8,9},{9,8},{10,11... | collective-permute-start | bytes 2359304 | tf_op jit(solution)/shard_map/ppermute | solution.py:29
  50.0 11.2 %collective-permute-start.7 = (bf16[512,768]{1,0:T(8,128)(2,1)}, bf16[512,768]{1,0:T(8,128)(2,1)}, u32[]{:S(2)}, u32[]{:S(2)}) collective-permute-start(bf16[512,768]{1,0:T(8,128)(2,1)} %collective-permute-done.2.refs_2_.refs_4_), channel_id=1, source_target_pairs={{0,1},{1,0},{2,3},{3,2},{4,5},{5,4},{6,7},{7,6},{8,9},{9,8},{10,11... | collective-permute-start | bytes 2359304 | tf_op jit(solution)/shard_map/ppermute | solution.py:29
  52.9 37.3 %collective-permute-start.9 = (bf16[8,96,512]{2,1,0:T(8,128)(2,1)}, bf16[8,96,512]{2,1,0:T(8,128)(2,1)}, u32[]{:S(2)}, u32[]{:S(2)}) collective-permute-start(bf16[8,96,512]{2,1,0:T(8,128)(2,1)} %param.35), channel_id=1, source_target_pairs={{0,16},{16,0},{1,17},{17,1},{2,18},{18,2},{3,19},{19,3},{4,20},{20... | collective-permute-start | bytes 2359304 | tf_op jit(solution)/shard_map/ppermute | solution.py:29
  52.9 40.7 %all-to-all-start.1 = ((bf16[8,2,96,512]{3,2,1,0:T(8,128)(2,1)}), bf16[8,2,96,512]{3,2,1,0:T(8,128)(2,1)}, u32[]{:S(2)}, u32[]{:S(2)}) async-start(bf16[8,2,96,512]{3,2,1,0:T(8,128)(2,1)} %pad_maximum_fusion), calls=%async_computation.1 | async-start | bytes 3145728 | tf_op jit(solution)/shard_map/all_to_all | solution.py:1134
  58.7 31.5 %collective-permute-start.8 = (bf16[4,2,96,192]{3,2,1,0:T(8,128)(2,1)}, bf16[4,2,96,192]{3,2,1,0:T(8,128)(2,1)}, u32[]{:S(2)}, u32[]{:S(2)}) collective-permute-start(bf16[4,2,96,192]{3,2,1,0:T(8,128)(2,1)} %pad_maximum_fusion.1.p0), channel_id=1, source_target_pairs={{0,2},{2,0},{1,3},{3,1},{4,6},{6,4},{5,7},{7,5},{8,10},{10,8},{9,1... | collective-permute-start | bytes 884744 | tf_op jit(solution)/shard_map/ppermute | solution.py:29
  60.1 41.0 %collective-permute-start.11 = (bf16[512,768]{1,0:T(8,128)(2,1)}, bf16[512,768]{1,0:T(8,128)(2,1)}, u32[]{:S(2)}, u32[]{:S(2)}) collective-permute-start(bf16[512,768]{1,0:T(8,128)(2,1)} %collective-permute-done.6.refs_2_), channel_id=1, source_target_pairs={{0,1},{1,0},{2,3},{3,2},{4,5},{5,4},{6,7},{7,6},{8,9},{9,8},{10,11... | collective-permute-start | bytes 2359304 | tf_op jit(solution)/shard_map/ppermute | solution.py:29
  93.6 17.7 %all-to-all-start = ((bf16[4,192,512]{2,1,0:T(8,128)(2,1)}), bf16[4,192,512]{2,1,0:T(8,128)(2,1)S(1)}, u32[]{:S(2)}, u32[]{:S(2)}) async-start(bf16[4,192,512]{2,1,0:T(8,128)(2,1)} %get-tuple-element.170.refs_1_), calls=%async_computation | async-start | bytes 1572864 | tf_op jit(solution)/shard_map/all_to_all | solution.py:1172
  100.7 11.9 %collective-permute-start.12 = (bf16[1,2,96,512]{3,2,1,0:T(8,128)(2,1)S(1)}, bf16[1,2,96,512]{3,2,1,0:T(8,128)(2,1)S(1)}, u32[]{:S(2)}, u32[]{:S(2)}) collective-permute-start(bf16[1,2,96,512]{3,2,1,0:T(8,128)(2,1)S(1)} %get-tuple-element.327), channel_id=1, source_target_pairs={{0,16},{16,0},{1,17},{17,1},{2,18},{18,2},{3,19},{19,3},{4,20},{20... | collective-permute-start | bytes 589832 | tf_op jit(solution)/shard_map/ppermute | solution.py:29
  113.3 61.8 %all-to-all-start.2 = ((bf16[8,2,96,512]{3,2,1,0:T(8,128)(2,1)}), bf16[8,2,96,512]{3,2,1,0:T(8,128)(2,1)}, u32[]{:S(2)}, u32[]{:S(2)}) async-start(bf16[8,2,96,512]{3,2,1,0:T(8,128)(2,1)} %maximum_select_fusion), calls=%async_computation.2 | async-start | bytes 3145728 | tf_op jit(solution)/shard_map/all_to_all | solution.py:1185
  118.0 250.0 %reduce-scatter.3.cloned.1.call-start = ((), (), s32[]{:S(2)}) async-start(), calls=%async_computation.10 | async-start | bytes 4718592 | tf_op jit(solution)/shard_map/reduce_scatter | solution.py:1044
  127.3 47.7 %collective-permute-start.15 = (bf16[512,896]{1,0:T(8,128)(2,1)}, bf16[512,896]{1,0:T(8,128)(2,1)S(1)}, u32[]{:S(2)}, u32[]{:S(2)}) collective-permute-start(bf16[512,896]{1,0:T(8,128)(2,1)} %get-tuple-element.185.refs_0_), channel_id=1, source_target_pairs={{0,2},{2,0},{1,3},{3,1},{4,6},{6,4},{5,7},{7,5},{8,10},{10,8},{9,1... | collective-permute-start | bytes 2752520 | tf_op jit(solution)/shard_map/ppermute | solution.py:29
  130.0 44.3 %collective-permute-start.19 = (bf16[3,2,96,512]{3,2,1,0:T(8,128)(2,1)S(1)}, bf16[3,2,96,512]{3,2,1,0:T(8,128)(2,1)S(1)}, u32[]{:S(2)}, u32[]{:S(2)}) collective-permute-start(bf16[3,2,96,512]{3,2,1,0:T(8,128)(2,1)S(1)} %get-tuple-element.325), channel_id=1, source_target_pairs={{0,16},{16,0},{1,17},{17,1},{2,18},{18,2},{3,19},{19,3},{4,20},{20... | collective-permute-start | bytes 1769480 | tf_op jit(solution)/shard_map/ppermute | solution.py:29
  130.5 35.7 %collective-permute-start.20 = (bf16[1,2,96,512]{3,2,1,0:T(8,128)(2,1)S(1)}, bf16[1,2,96,512]{3,2,1,0:T(8,128)(2,1)S(1)}, u32[]{:S(2)}, u32[]{:S(2)}) collective-permute-start(bf16[1,2,96,512]{3,2,1,0:T(8,128)(2,1)S(1)} %copy-done.61), channel_id=1, source_target_pairs={{0,16},{16,0},{1,17},{17,1},{2,18},{18,2},{3,19},{19,3},{4,20},{20... | collective-permute-start | bytes 589832 | tf_op jit(solution)/shard_map/ppermute | solution.py:29
  132.4 33.9 %collective-permute-start.16 = (bf16[192,768]{1,0:T(8,128)(2,1)S(1)}, bf16[192,768]{1,0:T(8,128)(2,1)}, u32[]{:S(2)}, u32[]{:S(2)}) collective-permute-start(bf16[192,768]{1,0:T(8,128)(2,1)S(1)} %copy-done.37), channel_id=1, source_target_pairs={{0,4},{4,0},{8,12},{12,8},{1,5},{5,1},{9,13},{13,9},{2,6},{6,2},{1... | collective-permute-start | bytes 884744 | tf_op jit(solution)/shard_map/ppermute | solution.py:1022
  133.6 34.3 %collective-permute-start.17 = (bf16[192,768]{1,0:T(8,128)(2,1)S(1)}, bf16[192,768]{1,0:T(8,128)(2,1)}, u32[]{:S(2)}, u32[]{:S(2)}) collective-permute-start(bf16[192,768]{1,0:T(8,128)(2,1)S(1)} %copy-done.31), channel_id=1, source_target_pairs={{0,8},{4,12},{8,0},{12,4},{1,9},{5,13},{9,1},{13,5},{2,10},{6,14},... | collective-permute-start | bytes 884744 | tf_op jit(solution)/shard_map/ppermute | solution.py:1022
  166.3 11.3 %collective-permute-start.21 = (bf16[512,896]{1,0:T(8,128)(2,1)}, bf16[512,896]{1,0:T(8,128)(2,1)}, u32[]{:S(2)}, u32[]{:S(2)}) collective-permute-start(bf16[512,896]{1,0:T(8,128)(2,1)} %get-tuple-element.185.refs_0_), channel_id=1, source_target_pairs={{0,1},{1,0},{2,3},{3,2},{4,5},{5,4},{6,7},{7,6},{8,9},{9,8},{10,11... | collective-permute-start | bytes 2752520 | tf_op jit(solution)/shard_map/ppermute | solution.py:29
  184.6 29.4 %collective-permute-start.31 = (bf16[576,768]{1,0:T(8,128)(2,1)S(1)}, bf16[576,768]{1,0:T(8,128)(2,1)S(1)}, u32[]{:S(2)}, u32[]{:S(2)}) collective-permute-start(bf16[576,768]{1,0:T(8,128)(2,1)S(1)} %copy-done.18), channel_id=1, source_target_pairs={{0,2},{2,0},{1,3},{3,1},{4,6},{6,4},{5,7},{7,5},{8,10},{10,8},{9,1... | collective-permute-start | bytes 2654216 | tf_op jit(solution)/shard_map/ppermute | solution.py:29
  185.0 28.5 %collective-permute-start.33 = (bf16[3,2,96,512]{3,2,1,0:T(8,128)(2,1)S(1)}, bf16[3,2,96,512]{3,2,1,0:T(8,128)(2,1)S(1)}, u32[]{:S(2)}, u32[]{:S(2)}) collective-permute-start(bf16[3,2,96,512]{3,2,1,0:T(8,128)(2,1)S(1)} %copy-done.57), channel_id=1, source_target_pairs={{0,16},{16,0},{1,17},{17,1},{2,18},{18,2},{3,19},{19,3},{4,20},{20... | collective-permute-start | bytes 1769480 | tf_op jit(solution)/shard_map/ppermute | solution.py:29
  185.3 28.2 %collective-permute-start.23 = (bf16[192,896]{1,0:T(8,128)(2,1)S(1)}, bf16[192,896]{1,0:T(8,128)(2,1)S(1)}, u32[]{:S(2)}, u32[]{:S(2)}) collective-permute-start(bf16[192,896]{1,0:T(8,128)(2,1)S(1)} %get-tuple-element.202), channel_id=1, source_target_pairs={{0,4},{4,0},{8,12},{12,8},{1,5},{5,1},{9,13},{13,9},{2,6},{6,2},{1... | collective-permute-start | bytes 1032200 | tf_op jit(solution)/shard_map/ppermute | solution.py:1022
  186.2 40.9 %collective-permute-start.30 = (bf16[576,768]{1,0:T(8,128)(2,1)S(1)}, bf16[576,768]{1,0:T(8,128)(2,1)S(1)}, u32[]{:S(2)}, u32[]{:S(2)}) collective-permute-start(bf16[576,768]{1,0:T(8,128)(2,1)S(1)} %copy-done.18), channel_id=1, source_target_pairs={{0,1},{1,0},{2,3},{3,2},{4,5},{5,4},{6,7},{7,6},{8,9},{9,8},{10,11... | collective-permute-start | bytes 2654216 | tf_op jit(solution)/shard_map/ppermute | solution.py:29
  187.1 27.1 %collective-permute-start.24 = (bf16[192,896]{1,0:T(8,128)(2,1)S(1)}, bf16[192,896]{1,0:T(8,128)(2,1)S(1)}, u32[]{:S(2)}, u32[]{:S(2)}) collective-permute-start(bf16[192,896]{1,0:T(8,128)(2,1)S(1)} %get-tuple-element.203), channel_id=1, source_target_pairs={{0,8},{4,12},{8,0},{12,4},{1,9},{5,13},{9,1},{13,5},{2,10},{6,14},... | collective-permute-start | bytes 1032200 | tf_op jit(solution)/shard_map/ppermute | solution.py:1022
  213.5 11.4 %collective-permute-start.26 = (bf16[192,896]{1,0:T(8,128)(2,1)S(1)}, bf16[192,896]{1,0:T(8,128)(2,1)S(1)}, u32[]{:S(2)}, u32[]{:S(2)}) collective-permute-start(bf16[192,896]{1,0:T(8,128)(2,1)S(1)} %get-tuple-element.207.refs_4_), channel_id=1, source_target_pairs={{0,1},{1,0},{2,3},{3,2},{4,5},{5,4},{6,7},{7,6},{8,9},{9,8},{10,11... | collective-permute-start | bytes 1032200 | tf_op jit(solution)/shard_map/ppermute | solution.py:29
  214.1 15.2 %collective-permute-start.32 = (bf16[576,768]{1,0:T(8,128)(2,1)S(1)}, bf16[576,768]{1,0:T(8,128)(2,1)}, u32[]{:S(2)}, u32[]{:S(2)}) collective-permute-start(bf16[576,768]{1,0:T(8,128)(2,1)S(1)} %collective-permute-done.31.p2), channel_id=1, source_target_pairs={{0,1},{1,0},{2,3},{3,2},{4,5},{5,4},{6,7},{7,6},{8,9},{9,8},{10,11... | collective-permute-start | bytes 2654216 | tf_op jit(solution)/shard_map/ppermute | solution.py:29
  276.2 23.1 %collective-permute-start.41 = (bf16[192,896]{1,0:T(8,128)(2,1)}, bf16[192,896]{1,0:T(8,128)(2,1)S(1)}, u32[]{:S(2)}, u32[]{:S(2)}) collective-permute-start(bf16[192,896]{1,0:T(8,128)(2,1)} %get-tuple-element.224), channel_id=1, source_target_pairs={{0,12},{4,8},{8,4},{12,0},{1,13},{5,9},{9,5},{13,1},{2,14},{6,10},... | collective-permute-start | bytes 1032200 | tf_op jit(solution)/shard_map/ppermute | solution.py:1022
  278.4 162.3 %reduce-scatter.5.cloned.1.call-start = ((), (), s32[]{:S(2)}) async-start(), calls=%async_computation.11 | async-start | bytes 2359296 | tf_op jit(solution)/shard_map/reduce_scatter | solution.py:1044
  311.6 21.9 %collective-permute-start.44 = (bf16[512,896]{1,0:T(8,128)(2,1)}, bf16[512,896]{1,0:T(8,128)(2,1)S(1)}, u32[]{:S(2)}, u32[]{:S(2)}) collective-permute-start(bf16[512,896]{1,0:T(8,128)(2,1)} %fusion.2), channel_id=1, source_target_pairs={{0,2},{2,0},{1,3},{3,1},{4,6},{6,4},{5,7},{7,5},{8,10},{10,8},{9,1... | collective-permute-start | bytes 2752520 | tf_op jit(solution)/shard_map/ppermute | solution.py:29
  344.8 18.2 %collective-permute-start.46 = (bf16[512,768]{1,0:T(8,128)(2,1)}, bf16[512,768]{1,0:T(8,128)(2,1)S(1)}, u32[]{:S(2)}, u32[]{:S(2)}) collective-permute-start(bf16[512,768]{1,0:T(8,128)(2,1)} %get-tuple-element.250.refs_0_.refs_6_), channel_id=1, source_target_pairs={{0,2},{2,0},{1,3},{3,1},{4,6},{6,4},{5,7},{7,5},{8,10},{10,8},{9,1... | collective-permute-start | bytes 2359304 | tf_op jit(solution)/shard_map/ppermute | solution.py:29
  346.0 26.3 %collective-permute-start.45 = (bf16[512,768]{1,0:T(8,128)(2,1)}, bf16[512,768]{1,0:T(8,128)(2,1)S(1)}, u32[]{:S(2)}, u32[]{:S(2)}) collective-permute-start(bf16[512,768]{1,0:T(8,128)(2,1)} %get-tuple-element.250.refs_0_.refs_6_), channel_id=1, source_target_pairs={{0,1},{1,0},{2,3},{3,2},{4,5},{5,4},{6,7},{7,6},{8,9},{9,8},{10,11... | collective-permute-start | bytes 2359304 | tf_op jit(solution)/shard_map/ppermute | solution.py:29
  365.1 34.3 %collective-permute-start.48 = (bf16[192,768]{1,0:T(8,128)(2,1)}, bf16[192,768]{1,0:T(8,128)(2,1)}, u32[]{:S(2)}, u32[]{:S(2)}) collective-permute-start(bf16[192,768]{1,0:T(8,128)(2,1)} %copy-done.38), channel_id=1, source_target_pairs={{0,4},{4,0},{8,12},{12,8},{1,5},{5,1},{9,13},{13,9},{2,6},{6,2},{1... | collective-permute-start | bytes 884744 | tf_op jit(solution)/shard_map/ppermute | solution.py:1022
  366.4 33.0 %collective-permute-start.49 = (bf16[192,768]{1,0:T(8,128)(2,1)S(1)}, bf16[192,768]{1,0:T(8,128)(2,1)}, u32[]{:S(2)}, u32[]{:S(2)}) collective-permute-start(bf16[192,768]{1,0:T(8,128)(2,1)S(1)} %copy-done.35), channel_id=1, source_target_pairs={{0,8},{4,12},{8,0},{12,4},{1,9},{5,13},{9,1},{13,5},{2,10},{6,14},... | collective-permute-start | bytes 884744 | tf_op jit(solution)/shard_map/ppermute | solution.py:1022
  367.7 31.7 %collective-permute-start.50 = (bf16[192,768]{1,0:T(8,128)(2,1)S(1)}, bf16[192,768]{1,0:T(8,128)(2,1)}, u32[]{:S(2)}, u32[]{:S(2)}) collective-permute-start(bf16[192,768]{1,0:T(8,128)(2,1)S(1)} %copy-done.33), channel_id=1, source_target_pairs={{0,12},{4,8},{8,4},{12,0},{1,13},{5,9},{9,5},{13,1},{2,14},{6,10},... | collective-permute-start | bytes 884744 | tf_op jit(solution)/shard_map/ppermute | solution.py:1022
  368.0 46.8 %all-to-all-start.3 = ((bf16[8,2,96,512]{3,2,1,0:T(8,128)(2,1)}), bf16[8,2,96,512]{3,2,1,0:T(8,128)(2,1)}, u32[]{:S(2)}, u32[]{:S(2)}) async-start(bf16[8,2,96,512]{3,2,1,0:T(8,128)(2,1)} %bitcast.103), calls=%async_computation.4 | async-start | bytes 3145728 | tf_op jit(solution)/shard_map/all_to_all | solution.py:1228
  422.2 16.4 %collective-permute-start.52 = (bf16[2,512,768]{2,1,0:T(8,128)(2,1)}, bf16[2,512,768]{2,1,0:T(8,128)(2,1)}, u32[]{:S(2)}, u32[]{:S(2)}) collective-permute-start(bf16[2,512,768]{2,1,0:T(8,128)(2,1)} %get-tuple-element.266), channel_id=1, source_target_pairs={{0,1},{1,0},{2,3},{3,2},{4,5},{5,4},{6,7},{7,6},{8,9},{9,8},{10,11... | collective-permute-start | bytes 4718600 | tf_op jit(solution)/shard_map/ppermute | solution.py:29
  423.3 42.8 %all-to-all-start.4 = ((bf16[4,576,512]{2,1,0:T(8,128)(2,1)}), bf16[4,576,512]{2,1,0:T(8,128)(2,1)}, u32[]{:S(2)}, u32[]{:S(2)}) async-start(bf16[4,576,512]{2,1,0:T(8,128)(2,1)} %bitcast.96), calls=%async_computation.5 | async-start | bytes 4718592 | tf_op jit(solution)/shard_map/all_to_all | solution.py:1236
  437.2 28.8 %collective-permute-start.51 = (bf16[4,96,768]{2,1,0:T(8,128)(2,1)}, bf16[4,96,768]{2,1,0:T(8,128)(2,1)}, u32[]{:S(2)}, u32[]{:S(2)}) collective-permute-start(bf16[4,96,768]{2,1,0:T(8,128)(2,1)} %get-tuple-element.260), channel_id=1, source_target_pairs={{0,16},{16,0},{1,17},{17,1},{2,18},{18,2},{3,19},{19,3},{4,20},{20... | collective-permute-start | bytes 1769480 | tf_op jit(solution)/shard_map/ppermute | solution.py:29
  466.8 11.4 %all-to-all-start.5 = ((f32[32,1,768]{2,1,0:T(1,128)}), f32[32,1,768]{2,1,0:T(1,128)S(1)}, u32[]{:S(2)}, u32[]{:S(2)}) async-start(f32[32,1,768]{2,1,0:T(1,128)} %copy.61), calls=%async_computation.7 | async-start | bytes 196608 | tf_op jit(solution)/shard_map/all_to_all | solution.py:1249
  474.0 35.0 %collective-permute-start.53 = (bf16[512,768]{1,0:T(8,128)(2,1)}, bf16[512,768]{1,0:T(8,128)(2,1)}, u32[]{:S(2)}, u32[]{:S(2)}) collective-permute-start(bf16[512,768]{1,0:T(8,128)(2,1)} %fusion.3), channel_id=1, source_target_pairs={{0,2},{2,0},{1,3},{3,1},{4,6},{6,4},{5,7},{7,5},{8,10},{10,8},{9,1... | collective-permute-start | bytes 2359304 | tf_op jit(solution)/shard_map/ppermute | solution.py:29
  478.8 23.2 %all-to-all-start.6 = ((bf16[8,96,512]{2,1,0:T(8,128)(2,1)}), bf16[8,96,512]{2,1,0:T(8,128)(2,1)}, u32[]{:S(2)}, u32[]{:S(2)}) async-start(bf16[8,96,512]{2,1,0:T(8,128)(2,1)} %bitcast.104), calls=%async_computation.8 | async-start | bytes 1572864 | tf_op jit(solution)/shard_map/all_to_all | solution.py:1252
  486.3 11.3 %collective-permute-start.56 = (bf16[96,768]{1,0:T(8,128)(2,1)}, bf16[96,768]{1,0:T(8,128)(2,1)}, u32[]{:S(2)}, u32[]{:S(2)}) collective-permute-start(bf16[96,768]{1,0:T(8,128)(2,1)} %get-tuple-element.331), channel_id=1, source_target_pairs={{0,12},{4,8},{8,4},{12,0},{1,13},{5,9},{9,5},{13,1},{2,14},{6,10},... | collective-permute-start | bytes 442376 | tf_op jit(solution)/shard_map/ppermute | solution.py:1022
  488.6 11.3 %collective-permute-start.55 = (bf16[96,768]{1,0:T(8,128)(2,1)S(1)}, bf16[96,768]{1,0:T(8,128)(2,1)}, u32[]{:S(2)}, u32[]{:S(2)}) collective-permute-start(bf16[96,768]{1,0:T(8,128)(2,1)S(1)} %get-tuple-element.332), channel_id=1, source_target_pairs={{0,8},{4,12},{8,0},{12,4},{1,9},{5,13},{9,1},{13,5},{2,10},{6,14},... | collective-permute-start | bytes 442376 | tf_op jit(solution)/shard_map/ppermute | solution.py:1022
  502.8 15.5 %all-to-all-start.7 = ((f32[32,1,1536]{2,1,0:T(1,128)}), f32[32,1,1536]{2,1,0:T(1,128)}, u32[]{:S(2)}, u32[]{:S(2)}) async-start(f32[32,1,1536]{2,1,0:T(1,128)} %broadcast_in_dim.5), calls=%async_computation.9 | async-start | bytes 393216 | tf_op jit(solution)/shard_map/all_to_all | solution.py:1018
  (103 other events, 868.4 us)
Sparse Core Ops, SparseCore 0:
  278.5 77.4 reduce-scatter.2
  365.2 41.7 reduce-scatter.4
